TPU v7x, 256 devices: a whole 4x4x8 slice. The times are simulated.
256 devices in a mesh: cast: 8 (over x, core), span: 32 (over z, y).
Axes of the slice: x: 4, y: 4, z: 8, core: 2. Of those that a mesh axis runs over, the one named last changes fastest.
Arguments:
- phase: int32 [16, 128, 4096], P(None, 'cast', 'span'), may hold values from 0 to 2
- viscosity_table: float32 [3], replicated, may hold values from 0.25 to 4
- pressure_source: float32 [16, 128, 4096], P(None, 'cast', 'span'), may hold values from -6 to 6
Outputs:
- solution_field: float32 [16, 128, 4096], P(None, 'cast', 'span')
- residual: float32 [16, 128, 4096], P(None, 'cast', 'span')
All inputs are finite; a program needn't handle non-finite values.
Results may differ from a plain program's by a relative error of at most 0.0003.
Values sent between devices are 32-bit elements; how exact they have to be, the bound alone decides.
No kernel may reach another device: no remote copies, remote signals or barrier semaphores. Data moves between devices by JAX's collectives and lax.ppermute only.
A program may use at most 64 MiB of HBM per device.

v0:
```python
import jax
import jax.numpy as jnp
from jax import lax
from jax.experimental import pallas as pl
from jax.experimental.pallas import tpu as pltpu
from jax.sharding import PartitionSpec as P

HZ, BC, BS = 16, 16, 128
HALO = 16
ROWS = BC + 2 * HALO
LANES = 256
SWEEPS_COARSE = 8
WEIGHT = 0.8
F32 = jnp.float32
HIGH = lax.Precision.HIGHEST


def shift(x, step, axis):
    return pltpu.roll(x, step % x.shape[axis], axis)


def iota(shape, axis):
    return lax.broadcasted_iota(jnp.int32, shape, axis)


def product(a, b):
    return jnp.dot(a, b, precision=HIGH, preferred_element_type=F32)


def harmonic(a, b):
    return 2.0 * a * b / (a + b)


def near(x, below, above, cast, span, low, high):
    return (
        cast * shift(x, 1, 0)
        + shift(cast * x, -1, 0)
        + span * shift(x, 1, 1)
        + shift(span * x, -1, 1)
        + low * below
        + high * above
    )


def diagonal_of(cast, span, low, high):
    return cast + shift(cast, -1, 0) + span + shift(span, -1, 1) + low + high


class Level:
    def __init__(self, cast, span, height, diag, relax, source):
        self.cast, self.span, self.height = cast, span, height
        self.diag, self.relax, self.source = diag, relax, source
        self.depth = len(cast)

    def near(self, x, z):
        depth = self.depth
        return near(
            x[z],
            x[max(z - 1, 0)],
            x[min(z + 1, depth - 1)],
            self.cast[z],
            self.span[z],
            self.height[z],
            self.height[z + 1],
        )

    def start(self):
        return [self.relax[z] * self.source[z] for z in range(self.depth)]

    def sweep(self, x):
        return [
            (1.0 - WEIGHT) * x[z] + self.relax[z] * (self.near(x, z) + self.source[z])
            for z in range(self.depth)
        ]

    def residual(self, x):
        return [self.source[z] - self.diag[z] * x[z] + self.near(x, z) for z in range(self.depth)]


def height_faces(coeff):
    flat = jnp.zeros_like(coeff[0])
    inner = [harmonic(a, b) for a, b in zip(coeff[:-1], coeff[1:])]
    return [flat] + inner + [flat]


def whole_level(coeff, source):
    shape = coeff[0].shape
    row = iota(shape, 0)
    height = height_faces(coeff)
    cast, span, diag, relax = [], [], [], []
    for z, c in enumerate(coeff):
        lower = jnp.where(row == 0, 0.0, harmonic(shift(c, 1, 0), c))
        ends = jnp.where((row == 0) | (row == shape[0] - 1), c, 0.0)
        side = harmonic(shift(c, 1, 1), c)
        total = diagonal_of(lower, side, height[z], height[z + 1]) + ends
        cast.append(lower)
        span.append(side)
        diag.append(total)
        relax.append(WEIGHT / total)
    return Level(cast, span, height, diag, relax, source)


def pair_rows(value, scratch):
    rows = value.shape[0]
    scratch[...] = value
    return scratch[pl.ds(0, rows // 2, stride=2), :] + scratch[pl.ds(1, rows // 2, stride=2), :]


def stage_kernel(table, phase, source, out):
    for z in range(HZ):
        p = phase[z]
        out[0, z] = jnp.where(p == 0, table[0], jnp.where(p == 1, table[1], table[2]))
        out[1, z] = source[z]


def margin_kernel(own, before, after, first, last):
    lane = iota((ROWS, BS), 1)
    for a in range(2):
        for group in range(2):
            head = tail = None
            for k in range(8):
                z = group * 8 + k
                slab = jnp.concatenate([before[a, z], own[a, z], after[a, z]], axis=0)
                h = shift(slab, HALO * k, 1)
                t = shift(slab, HALO * k + HALO, 1)
                inside = (lane >= HALO * k) & (lane < HALO * k + HALO)
                head = h if head is None else jnp.where(inside, h, head)
                tail = t if tail is None else jnp.where(inside, t, tail)
            first[a, group] = head
            last[a, group] = tail


def descent_kernel(
    place,
    own,
    before,
    after,
    right,
    left,
    x0,
    b0,
    cast0,
    span0,
    height0,
    diag0,
    relax0,
    x1,
    b1,
    cast1,
    span1,
    height1,
    relax1,
    slots,
    visc,
    xa,
    pair,
    cpair,
    rows24,
    rows8,
):
    index, count = place[0], place[1]
    first, last = index == 0, index == count - 1
    lane = iota((ROWS, BS), 1)

    for z in range(HZ):
        for a, target in ((0, visc), (1, b0)):
            low, mid, high = before[a, z], own[a, z], after[a, z]
            if a == 0:
                low = jnp.where(first, jnp.broadcast_to(mid[:1], low.shape), low)
                high = jnp.where(last, jnp.broadcast_to(mid[-1:], high.shape), high)
            target[z, :, :BS] = jnp.concatenate([low, mid, high], axis=0)
            group, k = divmod(z, 8)
            r = shift(right[a, group], -HALO * k, 1)
            l = shift(left[a, group], BS - HALO - HALO * k, 1)
            fill = 1.0 if a == 0 else 0.0
            edge = jnp.where(lane < HALO, r, jnp.where(lane >= BS - HALO, l, fill))
            if a == 0:
                edge = jnp.concatenate(
                    [
                        jnp.where(first, jnp.broadcast_to(edge[HALO : HALO + 1], (HALO, BS)), edge[:HALO]),
                        edge[HALO : HALO + BC],
                        jnp.where(last, jnp.broadcast_to(edge[HALO + BC - 1 : HALO + BC], (HALO, BS)), edge[HALO + BC :]),
                    ],
                    axis=0,
                )
            target[z, :, BS:] = edge

    height0[0] = jnp.zeros((ROWS, LANES), F32)
    height0[HZ] = jnp.zeros((ROWS, LANES), F32)

    def faces(z, _):
        v = visc[z]
        cast0[z] = 2.0 / (v + shift(v, 1, 0))
        span0[z] = 2.0 / (v + shift(v, 1, 1))

        @pl.when(z > 0)
        def _():
            height0[z] = 2.0 / (v + visc[jnp.maximum(z - 1, 0)])

        return 0

    lax.fori_loop(0, HZ, faces, 0)

    row = iota((ROWS, LANES), 0)
    outside = (first & (row < HALO)) | (last & (row >= HALO + BC))
    weight = jnp.where(outside, 0.0, WEIGHT)

    def begin(z, _):
        total = diagonal_of(cast0[z], span0[z], height0[z], height0[z + 1])
        diag0[z] = total
        relax = weight / total
        relax0[z] = relax
        xa[z] = relax * b0[z]
        return 0

    lax.fori_loop(0, HZ, begin, 0)

    def near0(x, z):
        return near(
            x[z],
            x[jnp.maximum(z - 1, 0)],
            x[jnp.minimum(z + 1, HZ - 1)],
            cast0[z],
            span0[z],
            height0[z],
            height0[z + 1],
        )

    def sweep(z, _):
        x0[z] = (1.0 - WEIGHT) * xa[z] + relax0[z] * (near0(xa, z) + b0[z])
        return 0

    lax.fori_loop(0, HZ, sweep, 0)

    def remainder(k, _):
        total = None
        for z in (2 * k, 2 * k + 1):
            r = b0[z] - diag0[z] * x0[z] + near0(x0, z)
            total = r if total is None else total + r
        pair[k] = total
        cpair[k] = 1.0 / visc[2 * k] + 1.0 / visc[2 * k + 1]
        return 0

    lax.fori_loop(0, HZ // 2, remainder, 0)

    half = ROWS // 2
    merge = jnp.where(iota((LANES, BS), 0) // 2 == iota((LANES, BS), 1), 1.0, 0.0)
    depth = HZ // 2
    edge = HALO // 2
    for a, source in enumerate((cpair, pair)):
        for k in range(depth):
            rows24[a * depth + k] = product(source[k], merge)

    def halved(k):
        return rows24[k, pl.ds(0, half, stride=2), :] + rows24[k, pl.ds(1, half, stride=2), :]

    row = iota((half, BS), 0)
    coeff, sources = [], []
    for k in range(depth):
        c = 0.125 * halved(k)
        low = jnp.where(first, jnp.broadcast_to(c[edge : edge + 1], (edge, BS)), c[:edge])
        high = jnp.where(last, jnp.broadcast_to(c[half - edge - 1 : half - edge], (edge, BS)), c[half - edge :])
        coeff.append(jnp.concatenate([low, c[edge : half - edge], high], axis=0))
        sources.append(0.5 * halved(depth + k))
    outside = (first & (row < edge)) | (last & (row >= half - edge))
    weight = jnp.where(outside, 0.0, WEIGHT)
    height = height_faces(coeff)
    cast = [harmonic(shift(c, 1, 0), c) for c in coeff]
    span = [harmonic(shift(c, 1, 1), c) for c in coeff]
    diag = [diagonal_of(cast[z], span[z], height[z], height[z + 1]) for z in range(depth)]
    relax = [weight / d for d in diag]
    level = Level(cast, span, height, diag, relax, sources)
    x = level.sweep(level.start())
    for z in range(depth):
        x1[z] = x[z]
        b1[z] = sources[z]
        cast1[z] = cast[z]
        span1[z] = span[z]
        relax1[z] = relax[z]
    for z in range(depth + 1):
        height1[z] = height[z]
    remains = level.residual(x)

    total_c = total_b = None
    for k in range(depth // 2):
        source, target = iota((BS, BS), 0), iota((BS, BS), 1)
        place_k = jnp.where((source < BS // 2) & (source // 2 + 32 * k == target), 1.0, 0.0)
        c = coeff[2 * k][edge : edge + 8] + coeff[2 * k + 1][edge : edge + 8]
        r = remains[2 * k][edge : edge + 8] + remains[2 * k + 1][edge : edge + 8]
        part = product(jnp.concatenate([c, r], axis=0), place_k)
        total_c = part if total_c is None else total_c + part
    rows8[...] = total_c
    c = 0.125 * (rows8[pl.ds(0, 4, stride=2), :] + rows8[pl.ds(1, 4, stride=2), :])
    r = 0.5 * (rows8[pl.ds(8, 4, stride=2), :] + rows8[pl.ds(9, 4, stride=2), :])
    for d in range(slots.shape[0]):
        slots[d, 0:4] = c
        slots[d, 4:8] = r


def ascent_kernel(
    place,
    own,
    right,
    left,
    x0,
    b0,
    cast0,
    span0,
    height0,
    diag0,
    relax0,
    x1,
    b1,
    cast1,
    span1,
    height1,
    relax1,
    solution_out,
    residual_out,
    tiles,
    pairs,
    wide2,
    padded2,
    wide1,
    wide0,
    xa,
    xb,
):
    count = own.shape[0]
    rows = 4 * count
    lane = iota((rows, 128), 1)
    index = place[0]

    fields = []
    for part in range(2):
        for s, block in enumerate((own, right, left)):
            for d in range(count):
                tiles[s, 4 * d : 4 * d + 4] = block[d, 4 * part : 4 * part + 4]
        slabs = []
        for z in range(4):
            o = shift(tiles[0], -32 * z, 1)
            r = shift(tiles[1], 32 - 32 * z, 1)
            l = shift(tiles[2], 96 - 32 * z, 1)
            fill = 1.0 if part == 0 else 0.0
            slabs.append(jnp.where(lane < 32, o, jnp.where(lane < 64, r, jnp.where(lane >= 96, l, fill))))
        fields.append(slabs)
    coeff2, source2 = fields
    level2 = whole_level(coeff2, source2)
    x2 = level2.sweep(level2.start())
    remains = level2.residual(x2)

    a, b = iota((128, 128), 0), iota((128, 128), 1)
    narrow = jnp.where(((a < 64) & (a // 2 == b)) | ((a >= 96) & (a // 2 + 64 == b)), 1.0, 0.0)
    widen = jnp.where(((b < 64) & (b // 2 == a)) | ((b >= 96) & (b // 2 + 64 == a)), 1.0, 0.0)
    gathered = []
    for field in (coeff2, remains):
        for k in range(2):
            gathered.append(pair_rows(field[2 * k] + field[2 * k + 1], pairs))
    merged = product(jnp.concatenate(gathered, axis=0), narrow)
    half = rows // 2
    lane3 = iota((half, 128), 1)
    known = (lane3 < 32) | (lane3 >= 112)
    coeff3 = [jnp.where(known, 0.125 * merged[half * k : half * (k + 1)], 1.0) for k in range(2)]
    source3 = [0.5 * merged[half * (2 + k) : half * (3 + k)] for k in range(2)]
    level3 = whole_level(coeff3, source3)
    x3 = level3.start()
    for _ in range(SWEEPS_COARSE - 1):
        x3 = level3.sweep(x3)

    spread = product(jnp.concatenate(x3, axis=0), widen)
    for k in range(2):
        wide2[k, pl.ds(0, half, stride=2), :] = spread[half * k : half * (k + 1)]
        wide2[k, pl.ds(1, half, stride=2), :] = spread[half * k : half * (k + 1)]
    x2 = [x2[z] + wide2[z // 2] for z in range(4)]
    x2 = level2.sweep(level2.sweep(x2))

    for z in range(4):
        padded2[z, 0:8] = jnp.zeros((8, 128), F32)
        padded2[z, 8 : 8 + rows] = x2[z]
        padded2[z, 8 + rows : 16 + rows] = jnp.zeros((8, 128), F32)
    grow = jnp.where(((b < 96) & (b // 2 == a)) | ((b >= 96) & (b // 2 + 64 == a)), 1.0, 0.0)
    local = [padded2[z, pl.ds(4 * index + 4, 16), :] for z in range(4)]
    spread = product(jnp.concatenate(local, axis=0), grow)
    for z in range(4):
        wide1[z, pl.ds(0, 16, stride=2), :] = spread[16 * z : 16 * z + 16]
        wide1[z, pl.ds(1, 16, stride=2), :] = spread[16 * z : 16 * z + 16]
    depth = HZ // 2
    half = ROWS // 2
    level1 = Level(
        [cast1[z] for z in range(depth)],
        [span1[z] for z in range(depth)],
        [height1[z] for z in range(depth + 1)],
        None,
        [relax1[z] for z in range(depth)],
        [b1[z] for z in range(depth)],
    )
    x = [x1[z] + wide1[z // 2, 0:half] for z in range(depth)]
    x = level1.sweep(level1.sweep(x))

    double = jnp.where(iota((BS, LANES), 1) // 2 == iota((BS, LANES), 0), 1.0, 0.0)
    spread = product(jnp.concatenate(x, axis=0), double)
    for z in range(depth):
        for s in range(2):
            part = spread[half * z : half * (z + 1), BS * s : BS * (s + 1)]
            wide0[s, z, pl.ds(0, half, stride=2), :] = part
            wide0[s, z, pl.ds(1, half, stride=2), :] = part
    top, bottom = 8, ROWS - 8
    cut = slice(top, bottom)

    def correct(z, _):
        k = lax.div(z, 2)
        for s in range(2):
            lanes = slice(BS * s, BS * (s + 1))
            xa[z, :, lanes] = x0[z, cut, lanes] + wide0[s, k, cut]
        return 0

    lax.fori_loop(0, HZ, correct, 0)

    def near0(x, z):
        return near(
            x[z],
            x[jnp.maximum(z - 1, 0)],
            x[jnp.minimum(z + 1, HZ - 1)],
            cast0[z, cut],
            span0[z, cut],
            height0[z, cut],
            height0[z + 1, cut],
        )

    def sweep(source, target):
        def body(z, _):
            target[z] = (1.0 - WEIGHT) * source[z] + relax0[z, cut] * (near0(source, z) + b0[z, cut])
            return 0

        lax.fori_loop(0, HZ, body, 0)

    sweep(xa, xb)
    sweep(xb, xa)

    def finish(z, _):
        r = b0[z, cut] - diag0[z, cut] * xa[z] + near0(xa, z)
        solution_out[z] = xa[z, HALO - top : HALO - top + BC, :BS]
        residual_out[z] = r[HALO - top : HALO - top + BC, :BS]
        return 0

    lax.fori_loop(0, HZ, finish, 0)


VMEM = pl.BlockSpec(memory_space=pltpu.VMEM)
SMEM = pl.BlockSpec(memory_space=pltpu.SMEM)
PARAMS = pltpu.CompilerParams(vmem_limit_bytes=48 * 1024 * 1024)
INTERPRET = False


def call(kernel, in_specs, outs, scratch=()):
    single = not isinstance(outs, list)
    shapes = [outs] if single else outs
    shapes = [jax.ShapeDtypeStruct(s, F32) for s in shapes]
    run = pl.pallas_call(
        kernel,
        in_specs=in_specs,
        out_specs=VMEM if single else [VMEM] * len(shapes),
        out_shape=shapes[0] if single else shapes,
        scratch_shapes=[pltpu.VMEM(s, F32) for s in scratch],
        compiler_params=PARAMS,
        interpret=INTERPRET,
    )
    return run


def ring(value, axis, step):
    size = lax.axis_size(axis)
    return lax.ppermute(value, axis, [(i, (i + step) % size) for i in range(size)])


def shards(phase, viscosity_table, pressure_source):
    count = lax.axis_size("cast")
    place = jnp.stack([lax.axis_index("cast"), count]).astype(jnp.int32)
    block = (2, HZ, BC, BS)
    fine = (HZ, ROWS, LANES)
    mid = (HZ // 2, ROWS // 2, BS)
    packed = (2, 2, ROWS, BS)

    own = call(stage_kernel, [SMEM, VMEM, VMEM], block)(viscosity_table, phase, pressure_source)
    before = ring(own, "cast", 1)
    after = ring(own, "cast", -1)
    first, last = call(margin_kernel, [VMEM] * 3, [packed, packed])(own, before, after)
    right = ring(first, "span", -1)
    left = ring(last, "span", 1)

    state_shapes = [fine, fine, fine, fine, (HZ + 1, ROWS, LANES), fine, fine]
    state_shapes += [mid, mid, mid, mid, (HZ // 2 + 1, ROWS // 2, BS), mid]
    scratch = [fine, fine, (HZ // 2, ROWS, LANES), (HZ // 2, ROWS, LANES), (HZ, ROWS, BS), (16, BS)]
    *state, slots = call(
        descent_kernel,
        [SMEM] + [VMEM] * 5,
        state_shapes + [(count, 8, 128)],
        scratch,
    )(place, own, before, after, right, left)

    column = lax.all_to_all(slots, "cast", 0, 0)
    column_left = ring(column, "span", 1)
    column_right = ring(column, "span", -1)
    rows = 4 * count
    scratch = [
        (3, rows, 128),
        (rows, 128),
        (2, rows, 128),
        (4, rows + 16, 128),
        (4, 32, 128),
        (2, HZ // 2, ROWS, BS),
        (HZ, ROWS - 16, LANES),
        (HZ, ROWS - 16, LANES),
    ]
    out = (HZ, BC, BS)
    return tuple(
        call(ascent_kernel, [SMEM] + [VMEM] * (3 + len(state)), [out, out], scratch)(
            place, column, column_right, column_left, *state
        )
    )


def solution(mesh):
    blocks = P(None, "cast", "span")
    return jax.shard_map(
        shards,
        mesh=mesh,
        in_specs=(blocks, P(), blocks),
        out_specs=(blocks, blocks),
        check_vma=False,
    )
```

profile of v0, /device:TPU:1, one launch (start us, length us, event | category | flops | bytes accessed | tf_op | source)
XLA Modules:
  0.0 63.8 jit_solution(5052661382375144929)
XLA Ops:
  0.6 0.0 copy-start.1
  0.6 0.9 %copy-done.1 = s32[16,16,128]{2,1,0:T(8,128)S(1)} copy-done((s32[16,16,128]{2,1,0:T(8,128)S(1)}, s32[16,16,128]{2,1,0:T(8,128)}, u32[]{:S(2)}) %copy-start.1) | copy-done | bytes 131096
  1.5 0.0 copy-start.2
  1.5 0.9 %copy-done.2 = f32[16,16,128]{2,1,0:T(8,128)S(1)} copy-done((f32[16,16,128]{2,1,0:T(8,128)S(1)}, f32[16,16,128]{2,1,0:T(8,128)}, u32[]{:S(2)}) %copy-start.2) | copy-done | bytes 131096
  2.4 0.7 %copy-done.3 = f32[3]{0:T(128)S(1)} copy-done((f32[3]{0:T(128)S(1)}, f32[3]{0:T(128)}, u32[]{:S(2)}) %copy-start.3) | copy-done | bytes 36
  3.1 0.6 shard_map.50.own
  3.7 3.3 %collective-permute-start.1 = (f32[2,16,16,128]{3,2,1,0:T(8,128)S(1)}, f32[2,16,16,128]{3,2,1,0:T(8,128)S(1)}, u32[]{:S(2)}, u32[]{:S(2)}) collective-permute-start(f32[2,16,16,128]{3,2,1,0:T(8,128)S(1)} %shard_map.50.own), channel_id=1, source_target_pairs={{0,224},{32,0},{64,32},{96,64},{128,96},{160,128},{192,160},{224,1... | collective-permute-start | bytes 786440 | tf_op jit(solution)/shard_map/ppermute | solution.py:473
  6.9 0.0 collective-permute-start
  6.9 3.4 %collective-permute-done.1.after = f32[2,16,16,128]{3,2,1,0:T(8,128)S(1)} collective-permute-done((f32[2,16,16,128]{3,2,1,0:T(8,128)S(1)}, f32[2,16,16,128]{3,2,1,0:T(8,128)S(1)}, u32[]{:S(2)}, u32[]{:S(2)}) %collective-permute-start.1) | collective-permute-done | bytes 262176 | tf_op jit(solution)/shard_map/ppermute | solution.py:473
  10.3 0.0 collective-permute-done.before
  10.3 0.4 shard_map.51
  10.8 8.1 %collective-permute-start.2 = (f32[2,2,48,128]{3,2,1,0:T(8,128)S(1)}, f32[2,2,48,128]{3,2,1,0:T(8,128)S(1)}, u32[]{:S(2)}, u32[]{:S(2)}) collective-permute-start(f32[2,2,48,128]{3,2,1,0:T(8,128)S(1)} %get-tuple-element.18), channel_id=1, source_target_pairs={{0,31},{1,0},{2,1},{3,2},{4,3},{5,4},{6,5},{7,6},{8,7},{9,8},{10,9... | collective-permute-start | bytes 294920 | tf_op jit(solution)/shard_map/ppermute | solution.py:473
  18.9 0.0 collective-permute-start.3
  18.9 0.1 pad_add_fusion.place
  18.9 1.6 %collective-permute-done.2.right = f32[2,2,48,128]{3,2,1,0:T(8,128)S(1)} collective-permute-done((f32[2,2,48,128]{3,2,1,0:T(8,128)S(1)}, f32[2,2,48,128]{3,2,1,0:T(8,128)S(1)}, u32[]{:S(2)}, u32[]{:S(2)}) %collective-permute-start.2) | collective-permute-done | bytes 98336 | tf_op jit(solution)/shard_map/ppermute | solution.py:473
  20.5 5.1 %collective-permute-done.3.left = f32[2,2,48,128]{3,2,1,0:T(8,128)S(1)} collective-permute-done((f32[2,2,48,128]{3,2,1,0:T(8,128)S(1)}, f32[2,2,48,128]{3,2,1,0:T(8,128)S(1)}, u32[]{:S(2)}, u32[]{:S(2)}) %collective-permute-start.3) | collective-permute-done | bytes 98336 | tf_op jit(solution)/shard_map/ppermute | solution.py:473
  25.7 9.5 %shard_map.52 = (f32[16,48,256]{2,1,0:T(8,128)S(1)}, f32[16,48,256]{2,1,0:T(8,128)S(1)}, f32[16,48,256]{2,1,0:T(8,128)S(1)}, f32[16,48,256]{2,1,0:T(8,128)S(1)},...) custom-call(s32[2]{0:T(128)S(1)} %pad_add_fusion.place, ...), custom_call_target="tpu_custom_call" | custom-call | tf_op jit(solution)/shard_map/pallas_call | solution.py:494
  35.2 12.5 %all_to_all.5.own = f32[8,8,128]{2,1,0:T(8,128)S(1)} all-to-all(f32[8,8,128]{2,1,0:T(8,128)S(1)} %get-tuple-element.20), channel_id=1, replica_groups=mesh['cast'=8,'span'=32] {'cast'}, dimensions={0} | all-to-all | bytes 65536 | tf_op jit(solution)/shard_map/all_to_all | solution.py:501
  47.7 0.0 collective-permute-start.5
  47.7 4.8 %collective-permute-start.4 = (f32[8,8,128]{2,1,0:T(8,128)S(1)}, f32[8,8,128]{2,1,0:T(8,128)S(1)}, u32[]{:S(2)}, u32[]{:S(2)}) collective-permute-start(f32[8,8,128]{2,1,0:T(8,128)S(1)} %all_to_all.5.own), channel_id=1, source_target_pairs={{0,31},{1,0},{2,1},{3,2},{4,3},{5,4},{6,5},{7,6},{8,7},{9,8},{10,9... | collective-permute-start | bytes 98312 | tf_op jit(solution)/shard_map/ppermute | solution.py:473
  52.5 1.3 %collective-permute-done.5.left = f32[8,8,128]{2,1,0:T(8,128)S(1)} collective-permute-done((f32[8,8,128]{2,1,0:T(8,128)S(1)}, f32[8,8,128]{2,1,0:T(8,128)S(1)}, u32[]{:S(2)}, u32[]{:S(2)}) %collective-permute-start.5) | collective-permute-done | bytes 32800 | tf_op jit(solution)/shard_map/ppermute | solution.py:473
  53.8 0.0 collective-permute-done.4.right
  53.8 1.1 %copy-done = f32[16,48,256]{2,1,0:T(8,128)S(1)} copy-done((f32[16,48,256]{2,1,0:T(8,128)S(1)}, f32[16,48,256]{2,1,0:T(8,128)}, u32[]{:S(2)}) %copy-start) | copy-done | bytes 786456
  55.0 8.9 %shard_map.53 = (f32[16,16,128]{2,1,0:T(8,128)}, f32[16,16,128]{2,1,0:T(8,128)}) custom-call(s32[2]{0:T(128)S(1)} %pad_add_fusion.place, f32[8,8,128]{2,1,0:T(8,128)S(1)} %all_to_all.5.own, f32[8,8,128]{2,1,0:T(8,128)S(1)} %collective-permute-done.4.right, f32[8,8,128]{2,1,0:T(8,128)S(1)} %collective-permute-done.5.left, ...), custom_call_target="tpu_custom_call" | custom-call | tf_op jit(solution)/shard_map/pallas_call | solution.py:517
  (2 shorter events, 0.0 us)
Async XLA Ops:
  0.6 0.9 %copy-start.1 = (s32[16,16,128]{2,1,0:T(8,128)S(1)}, s32[16,16,128]{2,1,0:T(8,128)}, u32[]{:S(2)}) copy-start(s32[16,16,128]{2,1,0:T(8,128)} %phase.1) | copy-start | bytes 393220
  1.5 0.9 %copy-start.2 = (f32[16,16,128]{2,1,0:T(8,128)S(1)}, f32[16,16,128]{2,1,0:T(8,128)}, u32[]{:S(2)}) copy-start(f32[16,16,128]{2,1,0:T(8,128)} %source.1) | copy-start | bytes 393220
  2.4 0.7 %copy-start.3 = (f32[3]{0:T(128)S(1)}, f32[3]{0:T(128)}, u32[]{:S(2)}) copy-start(f32[3]{0:T(128)} %table.1) | copy-start | bytes 40
  3.7 6.7 %collective-permute-start.1 = (f32[2,16,16,128]{3,2,1,0:T(8,128)S(1)}, f32[2,16,16,128]{3,2,1,0:T(8,128)S(1)}, u32[]{:S(2)}, u32[]{:S(2)}) collective-permute-start(f32[2,16,16,128]{3,2,1,0:T(8,128)S(1)} %shard_map.50.own), channel_id=1, source_target_pairs={{0,224},{32,0},{64,32},{96,64},{128,96},{160,128},{192,160},{224,1... | collective-permute-start | bytes 786440 | tf_op jit(solution)/shard_map/ppermute | solution.py:473
  6.9 3.4 %collective-permute-start = (f32[2,16,16,128]{3,2,1,0:T(8,128)S(1)}, f32[2,16,16,128]{3,2,1,0:T(8,128)S(1)}, u32[]{:S(2)}, u32[]{:S(2)}) collective-permute-start(f32[2,16,16,128]{3,2,1,0:T(8,128)S(1)} %shard_map.50.own), channel_id=1, source_target_pairs={{0,32},{32,64},{64,96},{96,128},{128,160},{160,192},{192,224},{224... | collective-permute-start | bytes 786440 | tf_op jit(solution)/shard_map/ppermute | solution.py:473
  10.8 9.7 %collective-permute-start.2 = (f32[2,2,48,128]{3,2,1,0:T(8,128)S(1)}, f32[2,2,48,128]{3,2,1,0:T(8,128)S(1)}, u32[]{:S(2)}, u32[]{:S(2)}) collective-permute-start(f32[2,2,48,128]{3,2,1,0:T(8,128)S(1)} %get-tuple-element.18), channel_id=1, source_target_pairs={{0,31},{1,0},{2,1},{3,2},{4,3},{5,4},{6,5},{7,6},{8,7},{9,8},{10,9... | collective-permute-start | bytes 294920 | tf_op jit(solution)/shard_map/ppermute | solution.py:473
  18.9 6.8 %collective-permute-start.3 = (f32[2,2,48,128]{3,2,1,0:T(8,128)S(1)}, f32[2,2,48,128]{3,2,1,0:T(8,128)S(1)}, u32[]{:S(2)}, u32[]{:S(2)}) collective-permute-start(f32[2,2,48,128]{3,2,1,0:T(8,128)S(1)} %get-tuple-element.19), channel_id=1, source_target_pairs={{0,1},{1,2},{2,3},{3,4},{4,5},{5,6},{6,7},{7,8},{8,9},{9,10},{10,1... | collective-permute-start | bytes 294920 | tf_op jit(solution)/shard_map/ppermute | solution.py:473
  47.7 6.1 %collective-permute-start.5 = (f32[8,8,128]{2,1,0:T(8,128)S(1)}, f32[8,8,128]{2,1,0:T(8,128)S(1)}, u32[]{:S(2)}, u32[]{:S(2)}) collective-permute-start(f32[8,8,128]{2,1,0:T(8,128)S(1)} %all_to_all.5.own), channel_id=1, source_target_pairs={{0,1},{1,2},{2,3},{3,4},{4,5},{5,6},{6,7},{7,8},{8,9},{9,10},{10,1... | collective-permute-start | bytes 98312 | tf_op jit(solution)/shard_map/ppermute | solution.py:473
  47.7 6.1 %collective-permute-start.4 = (f32[8,8,128]{2,1,0:T(8,128)S(1)}, f32[8,8,128]{2,1,0:T(8,128)S(1)}, u32[]{:S(2)}, u32[]{:S(2)}) collective-permute-start(f32[8,8,128]{2,1,0:T(8,128)S(1)} %all_to_all.5.own), channel_id=1, source_target_pairs={{0,31},{1,0},{2,1},{3,2},{4,3},{5,4},{6,5},{7,6},{8,7},{9,8},{10,9... | collective-permute-start | bytes 98312 | tf_op jit(solution)/shard_map/ppermute | solution.py:473
  53.8 1.1 %copy-start = (f32[16,48,256]{2,1,0:T(8,128)S(1)}, f32[16,48,256]{2,1,0:T(8,128)}, u32[]{:S(2)}) copy-start(f32[16,48,256]{2,1,0:T(8,128)} %get-tuple-element.27.relax0) | copy-start | bytes 2359300
where the time goes:
time: 64.1 us; the launch traced here: 63.8 us
  Pallas kernels  19.4 us (30%)
  starting transfers between devices  16.1 us (25%)
  blocking collectives  12.5 us (20%)
  waiting for transfers between devices  11.4 us (18%)
  local copies, waits for them, and re-layouts  3.59 us (6%)
  between operations  0.67 us (1%)
    ppermute x6, starting transfers between devices, ring(): lax.ppermute(value, axis, [(i, (i + step) % size) for i in range(size)])  16.1 us
    all_to_all x1, blocking collectives, shards(): column = lax.all_to_all(slots, 'cast', 0, 0)  12.5 us
    ppermute x6, waiting for transfers between devices, ring(): lax.ppermute(value, axis, [(i, (i + step) % size) for i in range(size)])  11.4 us
    pallas_call x1, Pallas kernels, shards(): call(descent_kernel, [SMEM] + [VMEM] * 5, state_shapes + [(count, 8, 128)...  9.53 us
    pallas_call x1, Pallas kernels, shards(): call(ascent_kernel, [SMEM] + [VMEM] * (3 + len(state)), [out, out], scratch)  8.86 us
    unnamed x8, local copies, waits for them, and re-layouts  3.59 us
  transfers between devices with their start and end apart: 6, of which 4 were waited for; matrix products, arithmetic and copies ran while one was open for 0% of the time, Pallas kernels for 0%

commit v1 on v0

v1 whole, which is shorter than its diff:
```python
import jax
import jax.numpy as jnp
from jax import lax
from jax.experimental import pallas as pl
from jax.experimental.pallas import tpu as pltpu
from jax.sharding import PartitionSpec as P

HZ, BC, BS = 16, 16, 128
HALO = 16
ROWS = BC + 2 * HALO
CUT = slice(HALO - 4, HALO + BC + 4)
KEPT = BC + 8
HALF = ROWS // 2
PACK = HZ // 2
SWEEPS_COARSE = 8
WEIGHT = 0.8
F32 = jnp.float32
HIGH = lax.Precision.HIGHEST


def shift(x, step, axis):
    return pltpu.roll(x, step % x.shape[axis], axis)


def iota(shape, axis):
    return lax.broadcasted_iota(jnp.int32, shape, axis)


def product(a, b):
    return jnp.dot(a, b, precision=HIGH, preferred_element_type=F32)


def harmonic(a, b):
    return 2.0 * a * b / (a + b)


def near(x, below, above, cast, span, low, high):
    return (
        cast * shift(x, 1, 0)
        + shift(cast * x, -1, 0)
        + span * shift(x, 1, 1)
        + shift(span * x, -1, 1)
        + low * below
        + high * above
    )


def diagonal_of(cast, span, low, high):
    return cast + shift(cast, -1, 0) + span + shift(span, -1, 1) + low + high


class Level:
    def __init__(self, cast, span, height, diag, relax, source, depth, packed=False):
        self.cast, self.span, self.height = cast, span, height
        self.diag, self.relax, self.source = diag, relax, source
        self.depth, self.packed = depth, packed

    def near(self, x, z):
        last = self.depth - 1
        below, above = x[max(z - 1, 0)], x[min(z + 1, last)]
        if self.packed and z == 0:
            below = shift(x[last], 64, 1)
        if self.packed and z == last:
            above = shift(x[0], 64, 1)
        return near(x[z], below, above, self.cast[z], self.span[z], self.height[z], self.height[z + 1])

    def start(self):
        return [self.relax[z] * self.source[z] for z in range(self.depth)]

    def sweep(self, x):
        return [
            (1.0 - WEIGHT) * x[z] + self.relax[z] * (self.near(x, z) + self.source[z])
            for z in range(self.depth)
        ]

    def residual(self, x):
        return [self.source[z] - self.diag[z] * x[z] + self.near(x, z) for z in range(self.depth)]


def fine_level(visc, source, outside, packed):
    depth = len(visc)
    shape = visc[0].shape
    weight = jnp.where(outside, 0.0, WEIGHT)
    cast = [2.0 / (v + shift(v, 1, 0)) for v in visc]
    span = [2.0 / (v + shift(v, 1, 1)) for v in visc]
    inner = [2.0 / (a + b) for a, b in zip(visc[:-1], visc[1:])]
    if packed:
        bottom = jnp.where(iota(shape, 1) < 64, 0.0, 2.0 / (visc[0] + shift(visc[-1], 64, 1)))
        top = shift(bottom, 64, 1)
    else:
        bottom = top = jnp.zeros(shape, F32)
    height = [bottom] + inner + [top]
    diag = [diagonal_of(cast[z], span[z], height[z], height[z + 1]) for z in range(depth)]
    relax = [weight / d for d in diag]
    return Level(cast, span, height, diag, relax, source, depth, packed)


def keep(level, x, refs):
    for ref, values in zip(refs, (x, level.source, level.cast, level.span, level.height, level.diag, level.relax)):
        for z, value in enumerate(values):
            ref[z] = value[CUT]


def coarse_parts(visc, remains, scratch):
    parts = []
    count = len(visc) // 2
    for a, values in enumerate(([1.0 / v for v in visc], remains)):
        for k in range(count):
            scratch[a * count + k] = values[2 * k] + values[2 * k + 1]
            ref = scratch.at[a * count + k]
            parts.append(ref[pl.ds(0, HALF, stride=2), :] + ref[pl.ds(1, HALF, stride=2), :])
    return jnp.concatenate(parts, axis=0)


def ends(value, first, last, edge):
    rows = value.shape[0]
    low = jnp.where(first, jnp.broadcast_to(value[edge : edge + 1], (edge, BS)), value[:edge])
    high = jnp.where(last, jnp.broadcast_to(value[rows - edge - 1 : rows - edge], (edge, BS)), value[rows - edge :])
    return jnp.concatenate([low, value[edge : rows - edge], high], axis=0)


def beyond(place, rows, edge):
    row = iota((rows, BS), 0)
    first, last = place[0] == 0, place[0] == place[1] - 1
    return first, last, (first & (row < edge)) | (last & (row >= rows - edge))


def height_faces(coeff):
    flat = jnp.zeros_like(coeff[0])
    inner = [harmonic(a, b) for a, b in zip(coeff[:-1], coeff[1:])]
    return [flat] + inner + [flat]


def whole_level(coeff, source):
    shape = coeff[0].shape
    row = iota(shape, 0)
    height = height_faces(coeff)
    cast, span, diag, relax = [], [], [], []
    for z, c in enumerate(coeff):
        lower = jnp.where(row == 0, 0.0, harmonic(shift(c, 1, 0), c))
        ends = jnp.where((row == 0) | (row == shape[0] - 1), c, 0.0)
        side = harmonic(shift(c, 1, 1), c)
        total = diagonal_of(lower, side, height[z], height[z + 1]) + ends
        cast.append(lower)
        span.append(side)
        diag.append(total)
        relax.append(WEIGHT / total)
    return Level(cast, span, height, diag, relax, source, len(coeff))


def pair_rows(value, scratch):
    rows = value.shape[0]
    scratch[...] = value
    return scratch[pl.ds(0, rows // 2, stride=2), :] + scratch[pl.ds(1, rows // 2, stride=2), :]


def stage_kernel(table_in, phase_in, source_in, out, table, phase, sems):
    copies = [
        pltpu.make_async_copy(table_in, table, sems.at[0]),
        pltpu.make_async_copy(phase_in, phase, sems.at[1]),
        pltpu.make_async_copy(source_in, out.at[1], sems.at[2]),
    ]
    for copy in copies:
        copy.start()
    copies[0].wait()
    copies[1].wait()
    for z in range(HZ):
        p = phase[z]
        out[0, z] = jnp.where(p == 0, table[0], jnp.where(p == 1, table[1], table[2]))
    copies[2].wait()


def margin_kernel(own, before, after, first, last):
    lane = iota((ROWS, BS), 1)
    for a in range(2):
        for group in range(2):
            head = tail = None
            for sub in range(4):
                for half in range(2):
                    z = group * 4 + sub + 8 * half
                    start = 16 * sub + 64 * half
                    slab = jnp.concatenate([before[a, z], own[a, z], after[a, z]], axis=0)
                    h = shift(slab, start, 1)
                    t = shift(slab, start + HALO, 1)
                    inside = (lane >= start) & (lane < start + HALO)
                    head = h if head is None else jnp.where(inside, h, head)
                    tail = t if tail is None else jnp.where(inside, t, tail)
            first[a, group] = head
            last[a, group] = tail


def own_kernel(place, own, before, after, x, b, cast, span, height, diag, relax, merged, inner, scratch):
    first, last, outside = beyond(place, ROWS, HALO)
    visc, source = [], []
    for z in range(HZ):
        v, s = (jnp.concatenate([before[a, z], own[a, z], after[a, z]], axis=0) for a in range(2))
        visc.append(ends(v, first, last, HALO))
        source.append(s)
    lane = iota((ROWS, BS), 1)
    for a, field in enumerate((visc, source)):
        for k in range(PACK):
            low, high = field[k], field[k + PACK]
            inner[a, k] = jnp.where(
                lane < 32,
                shift(low, 16, 1),
                jnp.where(lane < 64, shift(low, 48, 1), jnp.where(lane < 96, shift(high, 80, 1), shift(high, 112, 1))),
            )
    level = fine_level(visc, source, outside, False)
    values = level.sweep(level.start())
    keep(level, values, (x, b, cast, span, height, diag, relax))
    parts = coarse_parts(visc, level.residual(values), scratch)
    i, j = iota((BS, BS), 0), iota((BS, BS), 1)
    merge = jnp.where((i // 2 == j) & (i >= 8) & (i < 120), 1.0, 0.0)
    total = product(parts, merge)
    for k in range(HZ):
        merged[k] = total[HALF * k : HALF * (k + 1)]


def edge_kernel(
    place, right, left, inner, merged, x, b, cast, span, height, diag, relax,
    x1, b1, cast1, span1, height1, relax1, slots, scratch, rows8,
):
    first, last, outside = beyond(place, ROWS, HALO)
    lane = iota((ROWS, BS), 1) % 64
    fields = []
    for a in range(2):
        slabs = []
        for k in range(PACK):
            group, sub = divmod(k, 4)
            l = shift(left[a, group], -16 * sub, 1)
            r = shift(right[a, group], 48 - 16 * sub, 1)
            value = jnp.where(lane < 16, l, jnp.where(lane >= 48, r, inner[a, k]))
            slabs.append(ends(value, first, last, HALO) if a == 0 else value)
        fields.append(slabs)
    visc, source = fields
    level = fine_level(visc, source, outside, True)
    values = level.sweep(level.start())
    keep(level, values, (x, b, cast, span, height, diag, relax))
    parts = coarse_parts(visc, level.residual(values), scratch)
    i, j = iota((BS, 2 * BS), 0), iota((BS, 2 * BS), 1)
    m, ring_lane = i % 64, j % BS
    target = jnp.where(m < 24, (m // 2 + 120) % BS, m // 2 + 40)
    used = (m < 24) | (m >= 40)
    merge = jnp.where(used & (target == ring_lane) & (i // 64 == j // BS), 1.0, 0.0)
    total = product(parts, merge)

    edge = HALO // 2
    first, last, outside = beyond(place, HALF, edge)
    weight = jnp.where(outside, 0.0, WEIGHT)
    coarse = []
    for k in range(HZ):
        a, z = divmod(k, 8)
        side, pos = divmod(z, 4)
        row = HALF * (4 * a + pos)
        coarse.append(merged[k] + total[row : row + HALF, BS * side : BS * (side + 1)])
    lane = iota((HALF, BS), 1)
    known = (lane < 72) | (lane >= 120)
    coeff = [jnp.where(known, 0.125 * ends(c, first, last, edge), 1.0) for c in coarse[:8]]
    source = [0.5 * c for c in coarse[8:]]
    height = height_faces(coeff)
    cast_faces = [harmonic(shift(c, 1, 0), c) for c in coeff]
    span_faces = [harmonic(shift(c, 1, 1), c) for c in coeff]
    diagonal = [diagonal_of(cast_faces[z], span_faces[z], height[z], height[z + 1]) for z in range(8)]
    level = Level(cast_faces, span_faces, height, diagonal, [weight / d for d in diagonal], source, 8)
    values = level.sweep(level.start())
    for ref, items in ((x1, values), (b1, source), (cast1, cast_faces), (span1, span_faces), (height1, height), (relax1, level.relax)):
        for z, item in enumerate(items):
            ref[z] = item
    remains = level.residual(values)

    total = None
    i, j = iota((BS, BS), 0), iota((BS, BS), 1)
    for k in range(4):
        move = jnp.where((i < 64) & (i // 2 + 32 * k == j), 1.0, 0.0)
        c = coeff[2 * k][edge : edge + 8] + coeff[2 * k + 1][edge : edge + 8]
        r = remains[2 * k][edge : edge + 8] + remains[2 * k + 1][edge : edge + 8]
        part = product(jnp.concatenate([c, r], axis=0), move)
        total = part if total is None else total + part
    rows8[...] = total
    c = 0.125 * (rows8[pl.ds(0, 4, stride=2), :] + rows8[pl.ds(1, 4, stride=2), :])
    r = 0.5 * (rows8[pl.ds(8, 4, stride=2), :] + rows8[pl.ds(9, 4, stride=2), :])
    for d in range(slots.shape[0]):
        slots[d, 0:4] = c
        slots[d, 4:8] = r


def ascent_kernel(
    place, own, right, left,
    xo, bo, casto, spano, heighto, diago, relaxo,
    xe, be, caste, spane, heighte, diage, relaxe,
    x1, b1, cast1, span1, height1, relax1,
    solution_out, residual_out, tiles, pairs, wide2, padded2, wide1, wide_own, wide_edge,
):
    count = own.shape[0]
    rows = 4 * count
    lane = iota((rows, 128), 1)
    index = place[0]

    fields = []
    for part in range(2):
        for s, block in enumerate((own, right, left)):
            for d in range(count):
                tiles[s, 4 * d : 4 * d + 4] = block[d, 4 * part : 4 * part + 4]
        slabs = []
        for z in range(4):
            o = shift(tiles[0], -32 * z, 1)
            r = shift(tiles[1], 32 - 32 * z, 1)
            l = shift(tiles[2], 96 - 32 * z, 1)
            fill = 1.0 if part == 0 else 0.0
            slabs.append(jnp.where(lane < 32, o, jnp.where(lane < 64, r, jnp.where(lane >= 96, l, fill))))
        fields.append(slabs)
    coeff2, source2 = fields
    level2 = whole_level(coeff2, source2)
    x2 = level2.sweep(level2.start())
    remains = level2.residual(x2)

    a, b = iota((128, 128), 0), iota((128, 128), 1)
    narrow = jnp.where(((a < 64) & (a // 2 == b)) | ((a >= 96) & (a // 2 + 64 == b)), 1.0, 0.0)
    widen = jnp.where(((b < 64) & (b // 2 == a)) | ((b >= 96) & (b // 2 + 64 == a)), 1.0, 0.0)
    gathered = []
    for field in (coeff2, remains):
        for k in range(2):
            gathered.append(pair_rows(field[2 * k] + field[2 * k + 1], pairs))
    merged = product(jnp.concatenate(gathered, axis=0), narrow)
    half = rows // 2
    lane3 = iota((half, 128), 1)
    known = (lane3 < 32) | (lane3 >= 112)
    coeff3 = [jnp.where(known, 0.125 * merged[half * k : half * (k + 1)], 1.0) for k in range(2)]
    source3 = [0.5 * merged[half * (2 + k) : half * (3 + k)] for k in range(2)]
    level3 = whole_level(coeff3, source3)
    x3 = level3.start()
    for _ in range(SWEEPS_COARSE - 1):
        x3 = level3.sweep(x3)

    spread = product(jnp.concatenate(x3, axis=0), widen)
    for k in range(2):
        wide2[k, pl.ds(0, half, stride=2), :] = spread[half * k : half * (k + 1)]
        wide2[k, pl.ds(1, half, stride=2), :] = spread[half * k : half * (k + 1)]
    x2 = [x2[z] + wide2[z // 2] for z in range(4)]
    x2 = level2.sweep(level2.sweep(x2))

    for z in range(4):
        padded2[z, 0:8] = jnp.zeros((8, 128), F32)
        padded2[z, 8 : 8 + rows] = x2[z]
        padded2[z, 8 + rows : 16 + rows] = jnp.zeros((8, 128), F32)
    grow = jnp.where(((b < 96) & (b // 2 == a)) | ((b >= 96) & (b // 2 + 64 == a)), 1.0, 0.0)
    local = [padded2[z, pl.ds(4 * index + 4, 16), :] for z in range(4)]
    spread = product(jnp.concatenate(local, axis=0), grow)
    for z in range(4):
        wide1[z, pl.ds(0, 16, stride=2), :] = spread[16 * z : 16 * z + 16]
        wide1[z, pl.ds(1, 16, stride=2), :] = spread[16 * z : 16 * z + 16]
    level1 = Level(cast1, span1, height1, None, relax1, b1, 8)
    x = [x1[z] + wide1[z // 2, 0:HALF] for z in range(8)]
    x = level1.sweep(level1.sweep(x))

    i, j = iota((BS, BS), 0), iota((BS, BS), 1)
    spread = product(jnp.concatenate(x, axis=0), jnp.where(j // 2 == i, 1.0, 0.0))
    for z in range(8):
        for s in range(2):
            wide_own[z, pl.ds(s, HALF, stride=2), :] = spread[HALF * z : HALF * (z + 1)]
    i, j = iota((2 * BS, BS), 0), iota((2 * BS, BS), 1)
    m = j % 64
    origin = jnp.where(m < 32, (m // 2 + 120) % BS, m // 2 + 40)
    expand = jnp.where((origin == i % BS) & (i // BS == j // 64), 1.0, 0.0)
    sides = [jnp.concatenate([x[k], x[k + 4]], axis=1) for k in range(4)]
    spread = product(jnp.concatenate(sides, axis=0), expand)
    for k in range(4):
        for s in range(2):
            wide_edge[k, pl.ds(s, HALF, stride=2), :] = spread[HALF * k : HALF * (k + 1)]
    level_own = Level(casto, spano, heighto, diago, relaxo, bo, HZ)
    level_edge = Level(caste, spane, heighte, diage, relaxe, be, PACK, True)
    own_x = [xo[z] + wide_own[z // 2, CUT] for z in range(HZ)]
    edge_x = [xe[k] + wide_edge[k // 2, CUT] for k in range(PACK)]
    edge_x = level_edge.sweep(level_edge.sweep(edge_x))
    edge_r = level_edge.residual(edge_x)
    own_x = level_own.sweep(level_own.sweep(own_x))
    own_r = level_own.residual(own_x)
    lane = iota((BC, BS), 1)
    rows = slice(4, 4 + BC)
    for out, mid, side in ((solution_out, own_x, edge_x), (residual_out, own_r, edge_r)):
        for z in range(HZ):
            half, k = divmod(z, PACK)
            low = shift(side[k][rows], -16 - 64 * half, 1)
            high = shift(side[k][rows], 80 - 64 * half, 1)
            out[z] = jnp.where(lane < 8, low, jnp.where(lane >= 120, high, mid[z][rows]))


VMEM = pl.BlockSpec(memory_space=pltpu.VMEM)
SMEM = pl.BlockSpec(memory_space=pltpu.SMEM)
HBM = pl.BlockSpec(memory_space=pltpu.HBM)
PARAMS = pltpu.CompilerParams(vmem_limit_bytes=16 * 1024 * 1024)
INTERPRET = False


def call(kernel, in_specs, outs, scratch=()):
    return pl.pallas_call(
        kernel,
        in_specs=in_specs,
        out_specs=[VMEM] * len(outs),
        out_shape=[jax.ShapeDtypeStruct(s, F32) for s in outs],
        scratch_shapes=[pltpu.VMEM(s, F32) if isinstance(s, tuple) else s for s in scratch],
        compiler_params=PARAMS,
        interpret=INTERPRET,
    )


def ring(value, axis, step):
    size = lax.axis_size(axis)
    return lax.ppermute(value, axis, [(i, (i + step) % size) for i in range(size)])


def shards(phase, viscosity_table, pressure_source):
    count = lax.axis_size("cast")
    place = jnp.stack([lax.axis_index("cast"), count]).astype(jnp.int32)
    packed = (2, 2, ROWS, BS)
    own_state = [(HZ, KEPT, BS)] * 4 + [(HZ + 1, KEPT, BS)] + [(HZ, KEPT, BS)] * 2
    edge_state = [(PACK, KEPT, BS)] * 4 + [(PACK + 1, KEPT, BS)] + [(PACK, KEPT, BS)] * 2
    level1_state = [(8, HALF, BS)] * 4 + [(9, HALF, BS), (8, HALF, BS)]

    stage_scratch = [pltpu.SMEM((3,), F32), pltpu.VMEM((HZ, BC, BS), jnp.int32), pltpu.SemaphoreType.DMA((3,))]
    (own,) = call(stage_kernel, [HBM] * 3, [(2, HZ, BC, BS)], stage_scratch)(viscosity_table, phase, pressure_source)
    before = ring(own, "cast", 1)
    after = ring(own, "cast", -1)
    first, last = call(margin_kernel, [VMEM] * 3, [packed, packed])(own, before, after)
    right = ring(first, "span", -1)
    left = ring(last, "span", 1)
    *kept_own, merged, inner = call(
        own_kernel,
        [SMEM] + [VMEM] * 3,
        own_state + [(HZ, HALF, BS), (2, PACK, ROWS, BS)],
        [(HZ, ROWS, BS)],
    )(place, own, before, after)
    *kept_edge, slots = call(
        edge_kernel,
        [SMEM] + [VMEM] * 4,
        edge_state + level1_state + [(count, 8, BS)],
        [(8, ROWS, BS), (16, BS)],
    )(place, right, left, inner, merged)

    column = lax.all_to_all(slots, "cast", 0, 0)
    column_left = ring(column, "span", 1)
    column_right = ring(column, "span", -1)
    rows = 4 * count
    scratch = [
        (3, rows, BS),
        (rows, BS),
        (2, rows, BS),
        (4, rows + 16, BS),
        (4, 32, BS),
        (8, ROWS, BS),
        (4, ROWS, BS),
    ]
    state = kept_own + kept_edge
    return tuple(
        call(ascent_kernel, [SMEM] + [VMEM] * (3 + len(state)), [(HZ, BC, BS)] * 2, scratch)(
            place, column, column_right, column_left, *state
        )
    )


def solution(mesh):
    blocks = P(None, "cast", "span")
    return jax.shard_map(
        shards,
        mesh=mesh,
        in_specs=(blocks, P(), blocks),
        out_specs=(blocks, blocks),
        check_vma=False,
    )
```

time: 64.1 us -> 51.4 us (0.80)
  Pallas kernels: 19.4 us -> 10.3 us
  waiting for transfers between devices: 11.4 us -> 9.04 us
  local copies, waits for them, and re-layouts: 3.59 us -> 2.46 us
    pallas_call x3 -> x4, Pallas kernels: 18.9 us -> 9.89 us  [the longest x1 4.61 us: shards(): call(ascent_kernel, [SMEM] + [VMEM] * (3 + len(state)), [(HZ, BC, BS)] *...]
    ppermute x6, waiting for transfers between devices: 11.4 us -> 9.04 us  [ring(): lax.ppermute(value, axis, [(i, (i + step) % size) for i in range(size)])]
    unnamed x8 -> x6, local copies, waits for them, and re-layouts: 3.59 us -> 2.46 us
  transfers between devices with their start and end apart: 6 -> 6, of which waited for: 4 -> 3; matrix products, arithmetic and copies ran while one was open for 0% -> 0% of each run, Pallas kernels for 0% -> 5%
where the time goes in v1:
time: 51.4 us; the launch traced here: 51.3 us
  starting transfers between devices  16.1 us (31%)
  blocking collectives  12.6 us (25%)
  Pallas kernels  10.3 us (20%)
  waiting for transfers between devices  9.04 us (18%)
  local copies, waits for them, and re-layouts  2.46 us (5%)
  between operations  0.68 us (1%)
    ppermute x6, starting transfers between devices, ring(): lax.ppermute(value, axis, [(i, (i + step) % size) for i in range(size)])  16.1 us
    all_to_all x1, blocking collectives, shards(): column = lax.all_to_all(slots, 'cast', 0, 0)  12.6 us
    ppermute x6, waiting for transfers between devices, ring(): lax.ppermute(value, axis, [(i, (i + step) % size) for i in range(size)])  9.04 us
    pallas_call x1, Pallas kernels, shards(): call(ascent_kernel, [SMEM] + [VMEM] * (3 + len(state)), [(HZ, BC, BS)] *...  4.61 us
    unnamed x6, local copies, waits for them, and re-layouts  2.46 us
    pallas_call x1, Pallas kernels, shards(): call(own_kernel, [SMEM] + [VMEM] * 3, own_state + [(HZ, HALF, BS), (2, PA...  2.37 us
    pallas_call x1, Pallas kernels, shards(): call(edge_kernel, [SMEM] + [VMEM] * 4, edge_state + level1_state + [(coun...  2.31 us
  transfers between devices with their start and end apart: 6, of which 3 were waited for; matrix products, arithmetic and copies ran while one was open for 0% of the time, Pallas kernels for 5%

profile of v1, /device:TPU:1, one launch (start us, length us, event | category | flops | bytes accessed | tf_op | source)
XLA Modules:
  0.0 51.3 jit_solution(3945192261770742266)
XLA Ops:
  0.6 0.0 copy-start
  0.6 0.9 %copy-done = s32[16,16,128]{2,1,0:T(8,128)S(1)} copy-done((s32[16,16,128]{2,1,0:T(8,128)S(1)}, s32[16,16,128]{2,1,0:T(8,128)}, u32[]{:S(2)}) %copy-start) | copy-done | bytes 131096
  1.5 0.0 copy-start.1
  1.5 0.9 %copy-done.1 = f32[16,16,128]{2,1,0:T(8,128)S(1)} copy-done((f32[16,16,128]{2,1,0:T(8,128)S(1)}, f32[16,16,128]{2,1,0:T(8,128)}, u32[]{:S(2)}) %copy-start.1) | copy-done | bytes 131096
  2.4 0.7 %copy-done.2 = f32[3]{0:T(128)S(1)} copy-done((f32[3]{0:T(128)S(1)}, f32[3]{0:T(128)}, u32[]{:S(2)}) %copy-start.2) | copy-done | bytes 36
  3.1 0.6 %shard_map.50.own = f32[2,16,16,128]{3,2,1,0:T(8,128)S(1)} custom-call(f32[3]{0:T(128)S(1)} %copy-done.2, s32[16,16,128]{2,1,0:T(8,128)S(1)} %copy-done, f32[16,16,128]{2,1,0:T(8,128)S(1)} %copy-done.1), custom_call_target="tpu_custom_call" | custom-call | tf_op jit(solution)/shard_map/pallas_call | solution.py:421
  3.7 3.3 %collective-permute-start.1 = (f32[2,16,16,128]{3,2,1,0:T(8,128)S(1)}, f32[2,16,16,128]{3,2,1,0:T(8,128)S(1)}, u32[]{:S(2)}, u32[]{:S(2)}) collective-permute-start(f32[2,16,16,128]{3,2,1,0:T(8,128)S(1)} %shard_map.50.own), channel_id=1, source_target_pairs={{0,224},{32,0},{64,32},{96,64},{128,96},{160,128},{192,160},{224,1... | collective-permute-start | bytes 786440 | tf_op jit(solution)/shard_map/ppermute | solution.py:409
  6.9 0.0 collective-permute-start
  6.9 3.4 %collective-permute-done.1.after = f32[2,16,16,128]{3,2,1,0:T(8,128)S(1)} collective-permute-done((f32[2,16,16,128]{3,2,1,0:T(8,128)S(1)}, f32[2,16,16,128]{3,2,1,0:T(8,128)S(1)}, u32[]{:S(2)}, u32[]{:S(2)}) %collective-permute-start.1) | collective-permute-done | bytes 262176 | tf_op jit(solution)/shard_map/ppermute | solution.py:409
  10.4 0.0 collective-permute-done.before
  10.4 0.4 shard_map.51
  10.8 8.1 %collective-permute-start.2 = (f32[2,2,48,128]{3,2,1,0:T(8,128)S(1)}, f32[2,2,48,128]{3,2,1,0:T(8,128)S(1)}, u32[]{:S(2)}, u32[]{:S(2)}) collective-permute-start(f32[2,2,48,128]{3,2,1,0:T(8,128)S(1)} %get-tuple-element.27), channel_id=1, source_target_pairs={{0,31},{1,0},{2,1},{3,2},{4,3},{5,4},{6,5},{7,6},{8,7},{9,8},{10,9... | collective-permute-start | bytes 294920 | tf_op jit(solution)/shard_map/ppermute | solution.py:409
  18.9 0.0 collective-permute-start.3
  18.9 0.1 pad_add_fusion.place
  19.0 2.4 %shard_map.52 = (f32[16,24,128]{2,1,0:T(8,128)S(1)}, f32[16,24,128]{2,1,0:T(8,128)S(1)}, f32[16,24,128]{2,1,0:T(8,128)S(1)}, f32[16,24,128]{2,1,0:T(8,128)S(1)},...) custom-call(s32[2]{0:T(128)S(1)} %pad_add_fusion.place, ...), custom_call_target="tpu_custom_call" | custom-call | tf_op jit(solution)/shard_map/pallas_call | solution.py:427
  21.3 0.0 collective-permute-done.2.right
  21.4 4.3 %collective-permute-done.3.left = f32[2,2,48,128]{3,2,1,0:T(8,128)S(1)} collective-permute-done((f32[2,2,48,128]{3,2,1,0:T(8,128)S(1)}, f32[2,2,48,128]{3,2,1,0:T(8,128)S(1)}, u32[]{:S(2)}, u32[]{:S(2)}) %collective-permute-start.3) | collective-permute-done | bytes 98336 | tf_op jit(solution)/shard_map/ppermute | solution.py:409
  25.7 2.3 %shard_map.53 = (f32[8,24,128]{2,1,0:T(8,128)S(1)}, f32[8,24,128]{2,1,0:T(8,128)S(1)}, f32[8,24,128]{2,1,0:T(8,128)S(1)}, f32[8,24,128]{2,1,0:T(8,128)S(1)}, f32...) custom-call(s32[2]{0:T(128)S(1)} %pad_add_fusion.place, ...), custom_call_target="tpu_custom_call" | custom-call | tf_op jit(solution)/shard_map/pallas_call | solution.py:433
  28.0 12.6 %all_to_all.5.own = f32[8,8,128]{2,1,0:T(8,128)S(1)} all-to-all(f32[8,8,128]{2,1,0:T(8,128)S(1)} %get-tuple-element.31), channel_id=1, replica_groups=mesh['cast'=8,'span'=32] {'cast'}, dimensions={0} | all-to-all | bytes 65536 | tf_op jit(solution)/shard_map/all_to_all | solution.py:440
  40.6 0.0 collective-permute-start.5
  40.6 4.8 %collective-permute-start.4 = (f32[8,8,128]{2,1,0:T(8,128)S(1)}, f32[8,8,128]{2,1,0:T(8,128)S(1)}, u32[]{:S(2)}, u32[]{:S(2)}) collective-permute-start(f32[8,8,128]{2,1,0:T(8,128)S(1)} %all_to_all.5.own), channel_id=1, source_target_pairs={{0,31},{1,0},{2,1},{3,2},{4,3},{5,4},{6,5},{7,6},{8,7},{9,8},{10,9... | collective-permute-start | bytes 98312 | tf_op jit(solution)/shard_map/ppermute | solution.py:409
  45.3 1.3 %collective-permute-done.5.left = f32[8,8,128]{2,1,0:T(8,128)S(1)} collective-permute-done((f32[8,8,128]{2,1,0:T(8,128)S(1)}, f32[8,8,128]{2,1,0:T(8,128)S(1)}, u32[]{:S(2)}, u32[]{:S(2)}) %collective-permute-start.5) | collective-permute-done | bytes 32800 | tf_op jit(solution)/shard_map/ppermute | solution.py:409
  46.6 0.0 collective-permute-done.4.right
  46.6 4.6 %shard_map.54 = (f32[16,16,128]{2,1,0:T(8,128)}, f32[16,16,128]{2,1,0:T(8,128)}) custom-call(s32[2]{0:T(128)S(1)} %pad_add_fusion.place, f32[8,8,128]{2,1,0:T(8,128)S(1)} %all_to_all.5.own, f32[8,8,128]{2,1,0:T(8,128)S(1)} %collective-permute-done.4.right, f32[8,8,128]{2,1,0:T(8,128)S(1)} %collective-permute-done.5.left, ...), custom_call_target="tpu_custom_call" | custom-call | tf_op jit(solution)/shard_map/pallas_call | solution.py:455
  (1 shorter events, 0.0 us)
Async XLA Ops:
  0.6 0.9 %copy-start = (s32[16,16,128]{2,1,0:T(8,128)S(1)}, s32[16,16,128]{2,1,0:T(8,128)}, u32[]{:S(2)}) copy-start(s32[16,16,128]{2,1,0:T(8,128)} %phase_in.1) | copy-start | bytes 393220
  1.5 0.9 %copy-start.1 = (f32[16,16,128]{2,1,0:T(8,128)S(1)}, f32[16,16,128]{2,1,0:T(8,128)}, u32[]{:S(2)}) copy-start(f32[16,16,128]{2,1,0:T(8,128)} %source_in.1) | copy-start | bytes 393220
  2.4 0.7 %copy-start.2 = (f32[3]{0:T(128)S(1)}, f32[3]{0:T(128)}, u32[]{:S(2)}) copy-start(f32[3]{0:T(128)} %table_in.1) | copy-start | bytes 40
  3.7 6.7 %collective-permute-start.1 = (f32[2,16,16,128]{3,2,1,0:T(8,128)S(1)}, f32[2,16,16,128]{3,2,1,0:T(8,128)S(1)}, u32[]{:S(2)}, u32[]{:S(2)}) collective-permute-start(f32[2,16,16,128]{3,2,1,0:T(8,128)S(1)} %shard_map.50.own), channel_id=1, source_target_pairs={{0,224},{32,0},{64,32},{96,64},{128,96},{160,128},{192,160},{224,1... | collective-permute-start | bytes 786440 | tf_op jit(solution)/shard_map/ppermute | solution.py:409
  6.9 3.4 %collective-permute-start = (f32[2,16,16,128]{3,2,1,0:T(8,128)S(1)}, f32[2,16,16,128]{3,2,1,0:T(8,128)S(1)}, u32[]{:S(2)}, u32[]{:S(2)}) collective-permute-start(f32[2,16,16,128]{3,2,1,0:T(8,128)S(1)} %shard_map.50.own), channel_id=1, source_target_pairs={{0,32},{32,64},{64,96},{96,128},{128,160},{160,192},{192,224},{224... | collective-permute-start | bytes 786440 | tf_op jit(solution)/shard_map/ppermute | solution.py:409
  10.8 10.6 %collective-permute-start.2 = (f32[2,2,48,128]{3,2,1,0:T(8,128)S(1)}, f32[2,2,48,128]{3,2,1,0:T(8,128)S(1)}, u32[]{:S(2)}, u32[]{:S(2)}) collective-permute-start(f32[2,2,48,128]{3,2,1,0:T(8,128)S(1)} %get-tuple-element.27), channel_id=1, source_target_pairs={{0,31},{1,0},{2,1},{3,2},{4,3},{5,4},{6,5},{7,6},{8,7},{9,8},{10,9... | collective-permute-start | bytes 294920 | tf_op jit(solution)/shard_map/ppermute | solution.py:409
  18.9 6.8 %collective-permute-start.3 = (f32[2,2,48,128]{3,2,1,0:T(8,128)S(1)}, f32[2,2,48,128]{3,2,1,0:T(8,128)S(1)}, u32[]{:S(2)}, u32[]{:S(2)}) collective-permute-start(f32[2,2,48,128]{3,2,1,0:T(8,128)S(1)} %get-tuple-element.28), channel_id=1, source_target_pairs={{0,1},{1,2},{2,3},{3,4},{4,5},{5,6},{6,7},{7,8},{8,9},{9,10},{10,1... | collective-permute-start | bytes 294920 | tf_op jit(solution)/shard_map/ppermute | solution.py:409
  40.6 6.1 %collective-permute-start.5 = (f32[8,8,128]{2,1,0:T(8,128)S(1)}, f32[8,8,128]{2,1,0:T(8,128)S(1)}, u32[]{:S(2)}, u32[]{:S(2)}) collective-permute-start(f32[8,8,128]{2,1,0:T(8,128)S(1)} %all_to_all.5.own), channel_id=1, source_target_pairs={{0,1},{1,2},{2,3},{3,4},{4,5},{5,6},{6,7},{7,8},{8,9},{9,10},{10,1... | collective-permute-start | bytes 98312 | tf_op jit(solution)/shard_map/ppermute | solution.py:409
  40.6 6.1 %collective-permute-start.4 = (f32[8,8,128]{2,1,0:T(8,128)S(1)}, f32[8,8,128]{2,1,0:T(8,128)S(1)}, u32[]{:S(2)}, u32[]{:S(2)}) collective-permute-start(f32[8,8,128]{2,1,0:T(8,128)S(1)} %all_to_all.5.own), channel_id=1, source_target_pairs={{0,31},{1,0},{2,1},{3,2},{4,3},{5,4},{6,5},{7,6},{8,7},{9,8},{10,9... | collective-permute-start | bytes 98312 | tf_op jit(solution)/shard_map/ppermute | solution.py:409

commit v2 on v1

--- a/solution.py
+++ b/solution.py
@@ -15,7 +15,7 @@
 SWEEPS_COARSE = 8
 WEIGHT = 0.8
 F32 = jnp.float32
-HIGH = lax.Precision.HIGHEST
+BF16 = jnp.bfloat16
 
 
 def shift(x, step, axis):
@@ -26,8 +26,11 @@
     return lax.broadcasted_iota(jnp.int32, shape, axis)
 
 
-def product(a, b):
-    return jnp.dot(a, b, precision=HIGH, preferred_element_type=F32)
+def product(a, where):
+    b = jnp.where(where, 1.0, 0.0).astype(BF16)
+    high = a.astype(BF16)
+    low = (a - high.astype(F32)).astype(BF16)
+    return jnp.dot(high, b, preferred_element_type=F32) + jnp.dot(low, b, preferred_element_type=F32)
 
 
 def harmonic(a, b):
@@ -119,9 +122,10 @@
     return jnp.concatenate([low, value[edge : rows - edge], high], axis=0)
 
 
-def beyond(place, rows, edge):
+def beyond(rows, edge):
     row = iota((rows, BS), 0)
-    first, last = place[0] == 0, place[0] == place[1] - 1
+    index = lax.axis_index("cast")
+    first, last = index == 0, index == lax.axis_size("cast") - 1
     return first, last, (first & (row < edge)) | (last & (row >= rows - edge))
 
 
@@ -189,8 +193,8 @@
             last[a, group] = tail
 
 
-def own_kernel(place, own, before, after, x, b, cast, span, height, diag, relax, merged, inner, scratch):
-    first, last, outside = beyond(place, ROWS, HALO)
+def own_kernel(own, before, after, x, b, cast, span, height, diag, relax, merged, inner, scratch):
+    first, last, outside = beyond(ROWS, HALO)
     visc, source = [], []
     for z in range(HZ):
         v, s = (jnp.concatenate([before[a, z], own[a, z], after[a, z]], axis=0) for a in range(2))
@@ -210,17 +214,17 @@
     keep(level, values, (x, b, cast, span, height, diag, relax))
     parts = coarse_parts(visc, level.residual(values), scratch)
     i, j = iota((BS, BS), 0), iota((BS, BS), 1)
-    merge = jnp.where((i // 2 == j) & (i >= 8) & (i < 120), 1.0, 0.0)
+    merge = (i // 2 == j) & (i >= 8) & (i < 120)
     total = product(parts, merge)
     for k in range(HZ):
         merged[k] = total[HALF * k : HALF * (k + 1)]
 
 
 def edge_kernel(
-    place, right, left, inner, merged, x, b, cast, span, height, diag, relax,
+    right, left, inner, merged, x, b, cast, span, height, diag, relax,
     x1, b1, cast1, span1, height1, relax1, slots, scratch, rows8,
 ):
-    first, last, outside = beyond(place, ROWS, HALO)
+    first, last, outside = beyond(ROWS, HALO)
     lane = iota((ROWS, BS), 1) % 64
     fields = []
     for a in range(2):
@@ -241,11 +245,11 @@
     m, ring_lane = i % 64, j % BS
     target = jnp.where(m < 24, (m // 2 + 120) % BS, m // 2 + 40)
     used = (m < 24) | (m >= 40)
-    merge = jnp.where(used & (target == ring_lane) & (i // 64 == j // BS), 1.0, 0.0)
+    merge = used & (target == ring_lane) & (i // 64 == j // BS)
     total = product(parts, merge)
 
     edge = HALO // 2
-    first, last, outside = beyond(place, HALF, edge)
+    first, last, outside = beyond(HALF, edge)
     weight = jnp.where(outside, 0.0, WEIGHT)
     coarse = []
     for k in range(HZ):
@@ -268,33 +272,31 @@
             ref[z] = item
     remains = level.residual(values)
 
-    total = None
-    i, j = iota((BS, BS), 0), iota((BS, BS), 1)
+    i, j = iota((4 * BS, BS), 0), iota((4 * BS, BS), 1)
+    move = (i % BS < 64) & (i % BS // 2 + 32 * (i // BS) == j)
+    fields = []
     for k in range(4):
-        move = jnp.where((i < 64) & (i // 2 + 32 * k == j), 1.0, 0.0)
-        c = coeff[2 * k][edge : edge + 8] + coeff[2 * k + 1][edge : edge + 8]
-        r = remains[2 * k][edge : edge + 8] + remains[2 * k + 1][edge : edge + 8]
-        part = product(jnp.concatenate([c, r], axis=0), move)
-        total = part if total is None else total + part
-    rows8[...] = total
-    c = 0.125 * (rows8[pl.ds(0, 4, stride=2), :] + rows8[pl.ds(1, 4, stride=2), :])
-    r = 0.5 * (rows8[pl.ds(8, 4, stride=2), :] + rows8[pl.ds(9, 4, stride=2), :])
+        rows = slice(edge, edge + 8)
+        c = coeff[2 * k][rows] + coeff[2 * k + 1][rows]
+        r = remains[2 * k][rows] + remains[2 * k + 1][rows]
+        rows8[k] = jnp.concatenate([0.125 * c, 0.5 * r], axis=0)
+        fields.append(rows8[k, pl.ds(0, 8, stride=2), :] + rows8[k, pl.ds(1, 8, stride=2), :])
+    total = product(jnp.concatenate(fields, axis=1), move)
     for d in range(slots.shape[0]):
-        slots[d, 0:4] = c
-        slots[d, 4:8] = r
+        slots[d] = total
 
 
 def ascent_kernel(
-    place, own, right, left,
+    own, right, left,
     xo, bo, casto, spano, heighto, diago, relaxo,
     xe, be, caste, spane, heighte, diage, relaxe,
     x1, b1, cast1, span1, height1, relax1,
-    solution_out, residual_out, tiles, pairs, wide2, padded2, wide1, wide_own, wide_edge,
+    solution_out, residual_out, tiles, pairs, wide2, padded2, wide1, wide_own, wide_edge, results, sems,
 ):
     count = own.shape[0]
     rows = 4 * count
     lane = iota((rows, 128), 1)
-    index = place[0]
+    index = lax.axis_index("cast")
 
     fields = []
     for part in range(2):
@@ -315,8 +317,8 @@
     remains = level2.residual(x2)
 
     a, b = iota((128, 128), 0), iota((128, 128), 1)
-    narrow = jnp.where(((a < 64) & (a // 2 == b)) | ((a >= 96) & (a // 2 + 64 == b)), 1.0, 0.0)
-    widen = jnp.where(((b < 64) & (b // 2 == a)) | ((b >= 96) & (b // 2 + 64 == a)), 1.0, 0.0)
+    narrow = ((a < 64) & (a // 2 == b)) | ((a >= 96) & (a // 2 + 64 == b))
+    widen = ((b < 64) & (b // 2 == a)) | ((b >= 96) & (b // 2 + 64 == a))
     gathered = []
     for field in (coeff2, remains):
         for k in range(2):
@@ -343,7 +345,7 @@
         padded2[z, 0:8] = jnp.zeros((8, 128), F32)
         padded2[z, 8 : 8 + rows] = x2[z]
         padded2[z, 8 + rows : 16 + rows] = jnp.zeros((8, 128), F32)
-    grow = jnp.where(((b < 96) & (b // 2 == a)) | ((b >= 96) & (b // 2 + 64 == a)), 1.0, 0.0)
+    grow = ((b < 96) & (b // 2 == a)) | ((b >= 96) & (b // 2 + 64 == a))
     local = [padded2[z, pl.ds(4 * index + 4, 16), :] for z in range(4)]
     spread = product(jnp.concatenate(local, axis=0), grow)
     for z in range(4):
@@ -354,14 +356,14 @@
     x = level1.sweep(level1.sweep(x))
 
     i, j = iota((BS, BS), 0), iota((BS, BS), 1)
-    spread = product(jnp.concatenate(x, axis=0), jnp.where(j // 2 == i, 1.0, 0.0))
+    spread = product(jnp.concatenate(x, axis=0), j // 2 == i)
     for z in range(8):
         for s in range(2):
             wide_own[z, pl.ds(s, HALF, stride=2), :] = spread[HALF * z : HALF * (z + 1)]
     i, j = iota((2 * BS, BS), 0), iota((2 * BS, BS), 1)
     m = j % 64
     origin = jnp.where(m < 32, (m // 2 + 120) % BS, m // 2 + 40)
-    expand = jnp.where((origin == i % BS) & (i // BS == j // 64), 1.0, 0.0)
+    expand = (origin == i % BS) & (i // BS == j // 64)
     sides = [jnp.concatenate([x[k], x[k + 4]], axis=1) for k in range(4)]
     spread = product(jnp.concatenate(sides, axis=0), expand)
     for k in range(4):
@@ -372,31 +374,37 @@
     own_x = [xo[z] + wide_own[z // 2, CUT] for z in range(HZ)]
     edge_x = [xe[k] + wide_edge[k // 2, CUT] for k in range(PACK)]
     edge_x = level_edge.sweep(level_edge.sweep(edge_x))
-    edge_r = level_edge.residual(edge_x)
     own_x = level_own.sweep(level_own.sweep(own_x))
-    own_r = level_own.residual(own_x)
     lane = iota((BC, BS), 1)
     rows = slice(4, 4 + BC)
-    for out, mid, side in ((solution_out, own_x, edge_x), (residual_out, own_r, edge_r)):
+
+    def give(number, out, mid, side):
         for z in range(HZ):
             half, k = divmod(z, PACK)
             low = shift(side[k][rows], -16 - 64 * half, 1)
             high = shift(side[k][rows], 80 - 64 * half, 1)
-            out[z] = jnp.where(lane < 8, low, jnp.where(lane >= 120, high, mid[z][rows]))
+            results[number, z] = jnp.where(lane < 8, low, jnp.where(lane >= 120, high, mid[z][rows]))
+        copy = pltpu.make_async_copy(results.at[number], out, sems.at[number])
+        copy.start()
+        return copy
+
+    first = give(0, solution_out, own_x, edge_x)
+    second = give(1, residual_out, level_own.residual(own_x), level_edge.residual(edge_x))
+    first.wait()
+    second.wait()
 
 
 VMEM = pl.BlockSpec(memory_space=pltpu.VMEM)
-SMEM = pl.BlockSpec(memory_space=pltpu.SMEM)
 HBM = pl.BlockSpec(memory_space=pltpu.HBM)
 PARAMS = pltpu.CompilerParams(vmem_limit_bytes=16 * 1024 * 1024)
 INTERPRET = False
 
 
-def call(kernel, in_specs, outs, scratch=()):
+def call(kernel, in_specs, outs, scratch=(), out_spec=VMEM):
     return pl.pallas_call(
         kernel,
         in_specs=in_specs,
-        out_specs=[VMEM] * len(outs),
+        out_specs=[out_spec] * len(outs),
         out_shape=[jax.ShapeDtypeStruct(s, F32) for s in outs],
         scratch_shapes=[pltpu.VMEM(s, F32) if isinstance(s, tuple) else s for s in scratch],
         compiler_params=PARAMS,
@@ -411,14 +419,14 @@
 
 def shards(phase, viscosity_table, pressure_source):
     count = lax.axis_size("cast")
-    place = jnp.stack([lax.axis_index("cast"), count]).astype(jnp.int32)
     packed = (2, 2, ROWS, BS)
     own_state = [(HZ, KEPT, BS)] * 4 + [(HZ + 1, KEPT, BS)] + [(HZ, KEPT, BS)] * 2
     edge_state = [(PACK, KEPT, BS)] * 4 + [(PACK + 1, KEPT, BS)] + [(PACK, KEPT, BS)] * 2
     level1_state = [(8, HALF, BS)] * 4 + [(9, HALF, BS), (8, HALF, BS)]
 
+    arguments = (pltpu.with_memory_space_constraint(a, pltpu.HBM) for a in (viscosity_table, phase, pressure_source))
     stage_scratch = [pltpu.SMEM((3,), F32), pltpu.VMEM((HZ, BC, BS), jnp.int32), pltpu.SemaphoreType.DMA((3,))]
-    (own,) = call(stage_kernel, [HBM] * 3, [(2, HZ, BC, BS)], stage_scratch)(viscosity_table, phase, pressure_source)
+    (own,) = call(stage_kernel, [HBM] * 3, [(2, HZ, BC, BS)], stage_scratch)(*arguments)
     before = ring(own, "cast", 1)
     after = ring(own, "cast", -1)
     first, last = call(margin_kernel, [VMEM] * 3, [packed, packed])(own, before, after)
@@ -426,16 +434,16 @@
     left = ring(last, "span", 1)
     *kept_own, merged, inner = call(
         own_kernel,
-        [SMEM] + [VMEM] * 3,
+        [VMEM] * 3,
         own_state + [(HZ, HALF, BS), (2, PACK, ROWS, BS)],
         [(HZ, ROWS, BS)],
-    )(place, own, before, after)
+    )(own, before, after)
     *kept_edge, slots = call(
         edge_kernel,
-        [SMEM] + [VMEM] * 4,
+        [VMEM] * 4,
         edge_state + level1_state + [(count, 8, BS)],
-        [(8, ROWS, BS), (16, BS)],
-    )(place, right, left, inner, merged)
+        [(8, ROWS, BS), (4, 16, BS)],
+    )(right, left, inner, merged)
 
     column = lax.all_to_all(slots, "cast", 0, 0)
     column_left = ring(column, "span", 1)
@@ -449,11 +457,13 @@
         (4, 32, BS),
         (8, ROWS, BS),
         (4, ROWS, BS),
+        (2, HZ, BC, BS),
+        pltpu.SemaphoreType.DMA((2,)),
     ]
     state = kept_own + kept_edge
     return tuple(
-        call(ascent_kernel, [SMEM] + [VMEM] * (3 + len(state)), [(HZ, BC, BS)] * 2, scratch)(
-            place, column, column_right, column_left, *state
+        call(ascent_kernel, [VMEM] * (3 + len(state)), [(HZ, BC, BS)] * 2, scratch, HBM)(
+            column, column_right, column_left, *state
         )
     )
 

time: 51.4 us -> 47.6 us (0.926)
  local copies, waits for them, and re-layouts: 2.46 us -> 0 us
  Pallas kernels: 10.3 us -> 8.31 us
  waiting for transfers between devices: 9.04 us -> 9.81 us
    unnamed x6 -> x0, local copies, waits for them, and re-layouts: 2.46 us -> none
    pallas_call x4, Pallas kernels: 9.89 us -> 7.89 us  [the longest x1 3.78 us: shards(): call(ascent_kernel, [VMEM] * (3 + len(state)), [(HZ, BC, BS)] * 2, scratc...]
    ppermute x6, waiting for transfers between devices: 9.04 us -> 9.81 us  [ring(): lax.ppermute(value, axis, [(i, (i + step) % size) for i in range(size)])]
  transfers between devices with their start and end apart: 6 -> 6, of which waited for: 3 -> 3; matrix products, arithmetic and copies ran while one was open for 0% -> 0% of each run, Pallas kernels for 5% -> 4%
where the time goes in v2:
time: 47.6 us; the launch traced here: 47.5 us
  starting transfers between devices  16.1 us (34%)
  blocking collectives  12.6 us (26%)
  waiting for transfers between devices  9.81 us (21%)
  Pallas kernels  8.31 us (17%)
  between operations  0.65 us (1%)
    ppermute x6, starting transfers between devices, ring(): lax.ppermute(value, axis, [(i, (i + step) % size) for i in range(size)])  16.1 us
    all_to_all x1, blocking collectives, shards(): column = lax.all_to_all(slots, 'cast', 0, 0)  12.6 us
    ppermute x6, waiting for transfers between devices, ring(): lax.ppermute(value, axis, [(i, (i + step) % size) for i in range(size)])  9.81 us
    pallas_call x1, Pallas kernels, shards(): call(ascent_kernel, [VMEM] * (3 + len(state)), [(HZ, BC, BS)] * 2, scratc...  3.78 us
    pallas_call x1, Pallas kernels, shards(): call(own_kernel, [VMEM] * 3, own_state + [(HZ, HALF, BS), (2, PACK, ROWS,...  1.7 us
    pallas_call x1, Pallas kernels, shards(): call(edge_kernel, [VMEM] * 4, edge_state + level1_state + [(count, 8, BS)...  1.41 us
    pallas_call x1, Pallas kernels, shards(): call(stage_kernel, [HBM] * 3, [(2, HZ, BC, BS)], stage_scratch)(*arguments)  1 us
  transfers between devices with their start and end apart: 6, of which 3 were waited for; matrix products, arithmetic and copies ran while one was open for 0% of the time, Pallas kernels for 4%

profile of v2, /device:TPU:1, one launch (start us, length us, event | category | flops | bytes accessed | tf_op | source)
XLA Modules:
  0.0 47.5 jit_solution(7512979930987760963)
XLA Ops:
  0.6 1.0 %shard_map.50.own = f32[2,16,16,128]{3,2,1,0:T(8,128)S(1)} custom-call(f32[3]{0:T(128)} %table_in.1, s32[16,16,128]{2,1,0:T(8,128)} %phase_in.1, f32[16,16,128]{2,1,0:T(8,128)} %source_in.1), custom_call_target="tpu_custom_call" | custom-call | tf_op jit(solution)/shard_map/pallas_call | solution.py:429
  1.6 3.3 %collective-permute-start.1 = (f32[2,16,16,128]{3,2,1,0:T(8,128)S(1)}, f32[2,16,16,128]{3,2,1,0:T(8,128)S(1)}, u32[]{:S(2)}, u32[]{:S(2)}) collective-permute-start(f32[2,16,16,128]{3,2,1,0:T(8,128)S(1)} %shard_map.50.own), channel_id=1, source_target_pairs={{0,224},{32,0},{64,32},{96,64},{128,96},{160,128},{192,160},{224,1... | collective-permute-start | bytes 786440 | tf_op jit(solution)/shard_map/ppermute | solution.py:417
  4.9 0.0 collective-permute-start
  4.9 3.4 %collective-permute-done.1.after = f32[2,16,16,128]{3,2,1,0:T(8,128)S(1)} collective-permute-done((f32[2,16,16,128]{3,2,1,0:T(8,128)S(1)}, f32[2,16,16,128]{3,2,1,0:T(8,128)S(1)}, u32[]{:S(2)}, u32[]{:S(2)}) %collective-permute-start.1) | collective-permute-done | bytes 262176 | tf_op jit(solution)/shard_map/ppermute | solution.py:417
  8.3 0.0 collective-permute-done.before
  8.3 0.4 shard_map.51
  8.7 8.1 %collective-permute-start.2 = (f32[2,2,48,128]{3,2,1,0:T(8,128)S(1)}, f32[2,2,48,128]{3,2,1,0:T(8,128)S(1)}, u32[]{:S(2)}, u32[]{:S(2)}) collective-permute-start(f32[2,2,48,128]{3,2,1,0:T(8,128)S(1)} %get-tuple-element.27), channel_id=1, source_target_pairs={{0,31},{1,0},{2,1},{3,2},{4,3},{5,4},{6,5},{7,6},{8,7},{9,8},{10,9... | collective-permute-start | bytes 294920 | tf_op jit(solution)/shard_map/ppermute | solution.py:417
  16.8 0.0 collective-permute-start.3
  16.8 1.7 %shard_map.52 = (f32[16,24,128]{2,1,0:T(8,128)S(1)}, f32[16,24,128]{2,1,0:T(8,128)S(1)}, f32[16,24,128]{2,1,0:T(8,128)S(1)}, f32[16,24,128]{2,1,0:T(8,128)S(1)},...) custom-call(f32[2,16,16,128]{3,2,1,0:T(8,128)S(1)} %shard_map.50.own, ...), custom_call_target="tpu_custom_call" | custom-call | tf_op jit(solution)/shard_map/pallas_call | solution.py:435
  18.5 0.0 collective-permute-done.2.right
  18.5 5.1 %collective-permute-done.3.left = f32[2,2,48,128]{3,2,1,0:T(8,128)S(1)} collective-permute-done((f32[2,2,48,128]{3,2,1,0:T(8,128)S(1)}, f32[2,2,48,128]{3,2,1,0:T(8,128)S(1)}, u32[]{:S(2)}, u32[]{:S(2)}) %collective-permute-start.3) | collective-permute-done | bytes 98336 | tf_op jit(solution)/shard_map/ppermute | solution.py:417
  23.6 1.4 %shard_map.53 = (f32[8,24,128]{2,1,0:T(8,128)S(1)}, f32[8,24,128]{2,1,0:T(8,128)S(1)}, f32[8,24,128]{2,1,0:T(8,128)S(1)}, f32[8,24,128]{2,1,0:T(8,128)S(1)}, f32...) custom-call(f32[2,2,48,128]{3,2,1,0:T(8,128)S(1)} %collective-permut, ...), custom_call_target="tpu_custom_call" | custom-call | tf_op jit(solution)/shard_map/pallas_call | solution.py:441
  25.0 12.6 %all_to_all.5.own = f32[8,8,128]{2,1,0:T(8,128)S(1)} all-to-all(f32[8,8,128]{2,1,0:T(8,128)S(1)} %get-tuple-element.31), channel_id=1, replica_groups=mesh['cast'=8,'span'=32] {'cast'}, dimensions={0} | all-to-all | bytes 65536 | tf_op jit(solution)/shard_map/all_to_all | solution.py:448
  37.6 0.0 collective-permute-start.5
  37.6 4.8 %collective-permute-start.4 = (f32[8,8,128]{2,1,0:T(8,128)S(1)}, f32[8,8,128]{2,1,0:T(8,128)S(1)}, u32[]{:S(2)}, u32[]{:S(2)}) collective-permute-start(f32[8,8,128]{2,1,0:T(8,128)S(1)} %all_to_all.5.own), channel_id=1, source_target_pairs={{0,31},{1,0},{2,1},{3,2},{4,3},{5,4},{6,5},{7,6},{8,7},{9,8},{10,9... | collective-permute-start | bytes 98312 | tf_op jit(solution)/shard_map/ppermute | solution.py:417
  42.4 1.3 %collective-permute-done.5.left = f32[8,8,128]{2,1,0:T(8,128)S(1)} collective-permute-done((f32[8,8,128]{2,1,0:T(8,128)S(1)}, f32[8,8,128]{2,1,0:T(8,128)S(1)}, u32[]{:S(2)}, u32[]{:S(2)}) %collective-permute-start.5) | collective-permute-done | bytes 32800 | tf_op jit(solution)/shard_map/ppermute | solution.py:417
  43.7 0.0 collective-permute-done.4.right
  43.7 3.8 %shard_map.54 = (f32[16,16,128]{2,1,0:T(8,128)}, f32[16,16,128]{2,1,0:T(8,128)}) custom-call(f32[8,8,128]{2,1,0:T(8,128)S(1)} %all_to_all.5.own, f32[8,8,128]{2,1,0:T(8,128)S(1)} %collective-permute-done.4.right, f32[8,8,128]{2,1,0:T(8,128)S(1)} %collective-permute-done.5.left, f32[16,24,128]{2,1,0:T(8,128)S(1)} %get-tuple-element.32.xo, ...), custom_call_target="tpu_custom_call" | custom-call | tf_op jit(solution)/shard_map/pallas_call | solution.py:465
Async XLA Ops:
  1.6 6.7 %collective-permute-start.1 = (f32[2,16,16,128]{3,2,1,0:T(8,128)S(1)}, f32[2,16,16,128]{3,2,1,0:T(8,128)S(1)}, u32[]{:S(2)}, u32[]{:S(2)}) collective-permute-start(f32[2,16,16,128]{3,2,1,0:T(8,128)S(1)} %shard_map.50.own), channel_id=1, source_target_pairs={{0,224},{32,0},{64,32},{96,64},{128,96},{160,128},{192,160},{224,1... | collective-permute-start | bytes 786440 | tf_op jit(solution)/shard_map/ppermute | solution.py:417
  4.9 3.4 %collective-permute-start = (f32[2,16,16,128]{3,2,1,0:T(8,128)S(1)}, f32[2,16,16,128]{3,2,1,0:T(8,128)S(1)}, u32[]{:S(2)}, u32[]{:S(2)}) collective-permute-start(f32[2,16,16,128]{3,2,1,0:T(8,128)S(1)} %shard_map.50.own), channel_id=1, source_target_pairs={{0,32},{32,64},{64,96},{96,128},{128,160},{160,192},{192,224},{224... | collective-permute-start | bytes 786440 | tf_op jit(solution)/shard_map/ppermute | solution.py:417
  8.7 9.8 %collective-permute-start.2 = (f32[2,2,48,128]{3,2,1,0:T(8,128)S(1)}, f32[2,2,48,128]{3,2,1,0:T(8,128)S(1)}, u32[]{:S(2)}, u32[]{:S(2)}) collective-permute-start(f32[2,2,48,128]{3,2,1,0:T(8,128)S(1)} %get-tuple-element.27), channel_id=1, source_target_pairs={{0,31},{1,0},{2,1},{3,2},{4,3},{5,4},{6,5},{7,6},{8,7},{9,8},{10,9... | collective-permute-start | bytes 294920 | tf_op jit(solution)/shard_map/ppermute | solution.py:417
  16.8 6.8 %collective-permute-start.3 = (f32[2,2,48,128]{3,2,1,0:T(8,128)S(1)}, f32[2,2,48,128]{3,2,1,0:T(8,128)S(1)}, u32[]{:S(2)}, u32[]{:S(2)}) collective-permute-start(f32[2,2,48,128]{3,2,1,0:T(8,128)S(1)} %get-tuple-element.28), channel_id=1, source_target_pairs={{0,1},{1,2},{2,3},{3,4},{4,5},{5,6},{6,7},{7,8},{8,9},{9,10},{10,1... | collective-permute-start | bytes 294920 | tf_op jit(solution)/shard_map/ppermute | solution.py:417
  37.6 6.1 %collective-permute-start.5 = (f32[8,8,128]{2,1,0:T(8,128)S(1)}, f32[8,8,128]{2,1,0:T(8,128)S(1)}, u32[]{:S(2)}, u32[]{:S(2)}) collective-permute-start(f32[8,8,128]{2,1,0:T(8,128)S(1)} %all_to_all.5.own), channel_id=1, source_target_pairs={{0,1},{1,2},{2,3},{3,4},{4,5},{5,6},{6,7},{7,8},{8,9},{9,10},{10,1... | collective-permute-start | bytes 98312 | tf_op jit(solution)/shard_map/ppermute | solution.py:417
  37.6 6.1 %collective-permute-start.4 = (f32[8,8,128]{2,1,0:T(8,128)S(1)}, f32[8,8,128]{2,1,0:T(8,128)S(1)}, u32[]{:S(2)}, u32[]{:S(2)}) collective-permute-start(f32[8,8,128]{2,1,0:T(8,128)S(1)} %all_to_all.5.own), channel_id=1, source_target_pairs={{0,31},{1,0},{2,1},{3,2},{4,3},{5,4},{6,5},{7,6},{8,7},{9,8},{10,9... | collective-permute-start | bytes 98312 | tf_op jit(solution)/shard_map/ppermute | solution.py:417

commit v3 on v2

--- a/solution.py
+++ b/solution.py
@@ -158,6 +158,16 @@
     return scratch[pl.ds(0, rows // 2, stride=2), :] + scratch[pl.ds(1, rows // 2, stride=2), :]
 
 
+def by_side(axis, near_pair, far_pair):
+    even = lax.rem(lax.axis_index(axis), 2) == 0
+    return jnp.where(even, far_pair, near_pair), jnp.where(even, near_pair, far_pair)
+
+
+def extended(own, near_pair, far_pair, a, z):
+    before, after = by_side("cast", near_pair[a, z], far_pair[a, z])
+    return jnp.concatenate([before, own[a, z], after], axis=0)
+
+
 def stage_kernel(table_in, phase_in, source_in, out, table, phase, sems):
     copies = [
         pltpu.make_async_copy(table_in, table, sems.at[0]),
@@ -174,7 +184,7 @@
     copies[2].wait()
 
 
-def margin_kernel(own, before, after, first, last):
+def margin_kernel(own, near_cast, far_cast, far_span, near_span):
     lane = iota((ROWS, BS), 1)
     for a in range(2):
         for group in range(2):
@@ -183,21 +193,20 @@
                 for half in range(2):
                     z = group * 4 + sub + 8 * half
                     start = 16 * sub + 64 * half
-                    slab = jnp.concatenate([before[a, z], own[a, z], after[a, z]], axis=0)
+                    slab = extended(own, near_cast, far_cast, a, z)
                     h = shift(slab, start, 1)
                     t = shift(slab, start + HALO, 1)
                     inside = (lane >= start) & (lane < start + HALO)
                     head = h if head is None else jnp.where(inside, h, head)
                     tail = t if tail is None else jnp.where(inside, t, tail)
-            first[a, group] = head
-            last[a, group] = tail
-
-
-def own_kernel(own, before, after, x, b, cast, span, height, diag, relax, merged, inner, scratch):
+            far_span[a, group], near_span[a, group] = by_side("span", tail, head)
+
+
+def own_kernel(own, near_cast, far_cast, x, b, cast, span, height, diag, relax, merged, inner, scratch):
     first, last, outside = beyond(ROWS, HALO)
     visc, source = [], []
     for z in range(HZ):
-        v, s = (jnp.concatenate([before[a, z], own[a, z], after[a, z]], axis=0) for a in range(2))
+        v, s = (extended(own, near_cast, far_cast, a, z) for a in range(2))
         visc.append(ends(v, first, last, HALO))
         source.append(s)
     lane = iota((ROWS, BS), 1)
@@ -221,7 +230,7 @@
 
 
 def edge_kernel(
-    right, left, inner, merged, x, b, cast, span, height, diag, relax,
+    far_span, near_span, inner, merged, x, b, cast, span, height, diag, relax,
     x1, b1, cast1, span1, height1, relax1, slots, scratch, rows8,
 ):
     first, last, outside = beyond(ROWS, HALO)
@@ -231,8 +240,9 @@
         slabs = []
         for k in range(PACK):
             group, sub = divmod(k, 4)
-            l = shift(left[a, group], -16 * sub, 1)
-            r = shift(right[a, group], 48 - 16 * sub, 1)
+            left, right = by_side("span", near_span[a, group], far_span[a, group])
+            l = shift(left, -16 * sub, 1)
+            r = shift(right, 48 - 16 * sub, 1)
             value = jnp.where(lane < 16, l, jnp.where(lane >= 48, r, inner[a, k]))
             slabs.append(ends(value, first, last, HALO) if a == 0 else value)
         fields.append(slabs)
@@ -287,7 +297,7 @@
 
 
 def ascent_kernel(
-    own, right, left,
+    own, near_column, far_column,
     xo, bo, casto, spano, heighto, diago, relaxo,
     xe, be, caste, spane, heighte, diage, relaxe,
     x1, b1, cast1, span1, height1, relax1,
@@ -300,9 +310,11 @@
 
     fields = []
     for part in range(2):
-        for s, block in enumerate((own, right, left)):
-            for d in range(count):
-                tiles[s, 4 * d : 4 * d + 4] = block[d, 4 * part : 4 * part + 4]
+        for d in range(count):
+            rows_d = slice(4 * part, 4 * part + 4)
+            left, right = by_side("span", near_column[d, rows_d], far_column[d, rows_d])
+            for s, block in enumerate((own[d, rows_d], right, left)):
+                tiles[s, 4 * d : 4 * d + 4] = block
         slabs = []
         for z in range(4):
             o = shift(tiles[0], -32 * z, 1)
@@ -412,9 +424,15 @@
     )
 
 
-def ring(value, axis, step):
+def swap(value, axis, far, periodic):
     size = lax.axis_size(axis)
-    return lax.ppermute(value, axis, [(i, (i + step) % size) for i in range(size)])
+    partner = [i ^ 1 for i in range(size)]
+    if far:
+        partner = [((i - 1) ^ 1) + 1 for i in range(size)]
+        partner = [p % size if periodic or 0 <= p < size else i for i, p in enumerate(partner)]
+        if not periodic:
+            partner[0], partner[-1] = 0, size - 1
+    return lax.ppermute(value, axis, list(enumerate(partner)))
 
 
 def shards(phase, viscosity_table, pressure_source):
@@ -427,27 +445,27 @@
     arguments = (pltpu.with_memory_space_constraint(a, pltpu.HBM) for a in (viscosity_table, phase, pressure_source))
     stage_scratch = [pltpu.SMEM((3,), F32), pltpu.VMEM((HZ, BC, BS), jnp.int32), pltpu.SemaphoreType.DMA((3,))]
     (own,) = call(stage_kernel, [HBM] * 3, [(2, HZ, BC, BS)], stage_scratch)(*arguments)
-    before = ring(own, "cast", 1)
-    after = ring(own, "cast", -1)
-    first, last = call(margin_kernel, [VMEM] * 3, [packed, packed])(own, before, after)
-    right = ring(first, "span", -1)
-    left = ring(last, "span", 1)
+    far_cast = swap(own, "cast", True, False)
+    near_cast = swap(own, "cast", False, False)
+    far_span, near_span = call(margin_kernel, [VMEM] * 3, [packed, packed])(own, near_cast, far_cast)
+    far_span = swap(far_span, "span", True, True)
+    near_span = swap(near_span, "span", False, True)
     *kept_own, merged, inner = call(
         own_kernel,
         [VMEM] * 3,
         own_state + [(HZ, HALF, BS), (2, PACK, ROWS, BS)],
         [(HZ, ROWS, BS)],
-    )(own, before, after)
+    )(own, near_cast, far_cast)
     *kept_edge, slots = call(
         edge_kernel,
         [VMEM] * 4,
         edge_state + level1_state + [(count, 8, BS)],
         [(8, ROWS, BS), (4, 16, BS)],
-    )(right, left, inner, merged)
+    )(far_span, near_span, inner, merged)
 
     column = lax.all_to_all(slots, "cast", 0, 0)
-    column_left = ring(column, "span", 1)
-    column_right = ring(column, "span", -1)
+    far_column = swap(column, "span", True, True)
+    near_column = swap(column, "span", False, True)
     rows = 4 * count
     scratch = [
         (3, rows, BS),
@@ -463,7 +481,7 @@
     state = kept_own + kept_edge
     return tuple(
         call(ascent_kernel, [VMEM] * (3 + len(state)), [(HZ, BC, BS)] * 2, scratch, HBM)(
-            column, column_right, column_left, *state
+            column, near_column, far_column, *state
         )
     )
 

time: 47.6 us -> 44.8 us (0.941)
  blocking collectives: 12.6 us -> 10.9 us
  waiting for transfers between devices: 9.81 us -> 8.74 us
    all_to_all x1, blocking collectives: 12.6 us -> 10.9 us  [shards(): column = lax.all_to_all(slots, 'cast', 0, 0)]
    ppermute x6, waiting for transfers between devices: 9.81 us -> 8.74 us  [swap(): return lax.ppermute(value, axis, list(enumerate(partner)))]
  transfers between devices with their start and end apart: 6 -> 6, of which waited for: 3 -> 5; matrix products, arithmetic and copies ran while one was open for 0% -> 0% of each run, Pallas kernels for 4% -> 4%
where the time goes in v3:
time: 44.8 us; the launch traced here: 44.6 us
  starting transfers between devices  16 us (36%)
  blocking collectives  10.9 us (24%)
  waiting for transfers between devices  8.74 us (20%)
  Pallas kernels  8.36 us (19%)
  between operations  0.67 us (1%)
    ppermute x6, starting transfers between devices, swap(): return lax.ppermute(value, axis, list(enumerate(partner)))  16 us
    all_to_all x1, blocking collectives, shards(): column = lax.all_to_all(slots, 'cast', 0, 0)  10.9 us
    ppermute x6, waiting for transfers between devices, swap(): return lax.ppermute(value, axis, list(enumerate(partner)))  8.74 us
    pallas_call x1, Pallas kernels, shards(): call(ascent_kernel, [VMEM] * (3 + len(state)), [(HZ, BC, BS)] * 2, scratc...  3.79 us
    pallas_call x1, Pallas kernels, shards(): call(own_kernel, [VMEM] * 3, own_state + [(HZ, HALF, BS), (2, PACK, ROWS,...  1.72 us
    pallas_call x1, Pallas kernels, shards(): call(edge_kernel, [VMEM] * 4, edge_state + level1_state + [(count, 8, BS)...  1.42 us
    pallas_call x1, Pallas kernels, shards(): call(stage_kernel, [HBM] * 3, [(2, HZ, BC, BS)], stage_scratch)(*arguments)  1 us
  transfers between devices with their start and end apart: 6, of which 5 were waited for; matrix products, arithmetic and copies ran while one was open for 0% of the time, Pallas kernels for 4%

profile of v3, /device:TPU:1, one launch (start us, length us, event | category | flops | bytes accessed | tf_op | source)
XLA Modules:
  0.0 44.6 jit_solution(12851051962318178222)
XLA Ops:
  0.6 1.0 %shard_map.50.own = f32[2,16,16,128]{3,2,1,0:T(8,128)S(1)} custom-call(f32[3]{0:T(128)} %table_in.1, s32[16,16,128]{2,1,0:T(8,128)} %phase_in.1, f32[16,16,128]{2,1,0:T(8,128)} %source_in.1), custom_call_target="tpu_custom_call" | custom-call | tf_op jit(solution)/shard_map/pallas_call | solution.py:447
  1.6 4.5 %collective-permute-start.1 = (f32[2,16,16,128]{3,2,1,0:T(8,128)S(1)}, f32[2,16,16,128]{3,2,1,0:T(8,128)S(1)}, u32[]{:S(2)}, u32[]{:S(2)}) collective-permute-start(f32[2,16,16,128]{3,2,1,0:T(8,128)S(1)} %shard_map.50.own), channel_id=1, source_target_pairs={{0,0},{32,64},{64,32},{96,128},{128,96},{160,192},{192,160},{224,2... | collective-permute-start | bytes 786440 | tf_op jit(solution)/shard_map/ppermute | solution.py:435
  6.2 0.1 collective-permute-start
  6.3 3.9 %collective-permute-done.1.far_cast = f32[2,16,16,128]{3,2,1,0:T(8,128)S(1)} collective-permute-done((f32[2,16,16,128]{3,2,1,0:T(8,128)S(1)}, f32[2,16,16,128]{3,2,1,0:T(8,128)S(1)}, u32[]{:S(2)}, u32[]{:S(2)}) %collective-permute-start.1) | collective-permute-done | bytes 262176 | tf_op jit(solution)/shard_map/ppermute | solution.py:435
  10.2 0.0 collective-permute-done.near_cast
  10.2 0.4 shard_map.51
  10.6 8.1 %collective-permute-start.2 = (f32[2,2,48,128]{3,2,1,0:T(8,128)S(1)}, f32[2,2,48,128]{3,2,1,0:T(8,128)S(1)}, u32[]{:S(2)}, u32[]{:S(2)}) collective-permute-start(f32[2,2,48,128]{3,2,1,0:T(8,128)S(1)} %get-tuple-element.27), channel_id=1, source_target_pairs={{0,31},{1,2},{2,1},{3,4},{4,3},{5,6},{6,5},{7,8},{8,7},{9,10},{10,... | collective-permute-start | bytes 294920 | tf_op jit(solution)/shard_map/ppermute | solution.py:435
  18.8 0.0 collective-permute-start.3
  18.8 1.7 %shard_map.52 = (f32[16,24,128]{2,1,0:T(8,128)S(1)}, f32[16,24,128]{2,1,0:T(8,128)S(1)}, f32[16,24,128]{2,1,0:T(8,128)S(1)}, f32[16,24,128]{2,1,0:T(8,128)S(1)},...) custom-call(f32[2,16,16,128]{3,2,1,0:T(8,128)S(1)} %shard_map.50.own, ...), custom_call_target="tpu_custom_call" | custom-call | tf_op jit(solution)/shard_map/pallas_call | solution.py:453
  20.5 0.3 collective-permute-done.2.far_span
  20.8 1.5 %collective-permute-done.3.near_span = f32[2,2,48,128]{3,2,1,0:T(8,128)S(1)} collective-permute-done((f32[2,2,48,128]{3,2,1,0:T(8,128)S(1)}, f32[2,2,48,128]{3,2,1,0:T(8,128)S(1)}, u32[]{:S(2)}, u32[]{:S(2)}) %collective-permute-start.3) | collective-permute-done | bytes 98336 | tf_op jit(solution)/shard_map/ppermute | solution.py:435
  22.2 1.4 %shard_map.53 = (f32[8,24,128]{2,1,0:T(8,128)S(1)}, f32[8,24,128]{2,1,0:T(8,128)S(1)}, f32[8,24,128]{2,1,0:T(8,128)S(1)}, f32[8,24,128]{2,1,0:T(8,128)S(1)}, f32...) custom-call(f32[2,2,48,128]{3,2,1,0:T(8,128)S(1)} %collective-permut, ...), custom_call_target="tpu_custom_call" | custom-call | tf_op jit(solution)/shard_map/pallas_call | solution.py:459
  23.6 10.9 %all_to_all.5.own = f32[8,8,128]{2,1,0:T(8,128)S(1)} all-to-all(f32[8,8,128]{2,1,0:T(8,128)S(1)} %get-tuple-element.31), channel_id=1, replica_groups=mesh['cast'=8,'span'=32] {'cast'}, dimensions={0} | all-to-all | bytes 65536 | tf_op jit(solution)/shard_map/all_to_all | solution.py:466
  34.5 3.2 %collective-permute-start.5 = (f32[8,8,128]{2,1,0:T(8,128)S(1)}, f32[8,8,128]{2,1,0:T(8,128)S(1)}, u32[]{:S(2)}, u32[]{:S(2)}) collective-permute-start(f32[8,8,128]{2,1,0:T(8,128)S(1)} %all_to_all.5.own), channel_id=1, source_target_pairs={{0,31},{1,2},{2,1},{3,4},{4,3},{5,6},{6,5},{7,8},{8,7},{9,10},{10,... | collective-permute-start | bytes 98312 | tf_op jit(solution)/shard_map/ppermute | solution.py:435
  37.8 0.0 collective-permute-start.4
  37.8 2.8 %collective-permute-done.5.far_column = f32[8,8,128]{2,1,0:T(8,128)S(1)} collective-permute-done((f32[8,8,128]{2,1,0:T(8,128)S(1)}, f32[8,8,128]{2,1,0:T(8,128)S(1)}, u32[]{:S(2)}, u32[]{:S(2)}) %collective-permute-start.5) | collective-permute-done | bytes 32800 | tf_op jit(solution)/shard_map/ppermute | solution.py:435
  40.6 0.2 collective-permute-done.4.near_column
  40.8 3.8 %shard_map.54 = (f32[16,16,128]{2,1,0:T(8,128)}, f32[16,16,128]{2,1,0:T(8,128)}) custom-call(f32[8,8,128]{2,1,0:T(8,128)S(1)} %all_to_all.5.own, f32[8,8,128]{2,1,0:T(8,128)S(1)} %collective-permute-done.4.near_column, f32[8,8,128]{2,1,0:T(8,128)S(1)} %collective-permute-done.5.far_column, f32[16,24,128]{2,1,0:T(8,128)S(1)} %get-tuple-element.32.xo, ...), custom_call_target="tpu_custom_call" | custom-call | tf_op jit(solution)/shard_map/pallas_call | solution.py:483
Async XLA Ops:
  1.6 8.6 %collective-permute-start.1 = (f32[2,16,16,128]{3,2,1,0:T(8,128)S(1)}, f32[2,16,16,128]{3,2,1,0:T(8,128)S(1)}, u32[]{:S(2)}, u32[]{:S(2)}) collective-permute-start(f32[2,16,16,128]{3,2,1,0:T(8,128)S(1)} %shard_map.50.own), channel_id=1, source_target_pairs={{0,0},{32,64},{64,32},{96,128},{128,96},{160,192},{192,160},{224,2... | collective-permute-start | bytes 786440 | tf_op jit(solution)/shard_map/ppermute | solution.py:435
  6.2 4.0 %collective-permute-start = (f32[2,16,16,128]{3,2,1,0:T(8,128)S(1)}, f32[2,16,16,128]{3,2,1,0:T(8,128)S(1)}, u32[]{:S(2)}, u32[]{:S(2)}) collective-permute-start(f32[2,16,16,128]{3,2,1,0:T(8,128)S(1)} %shard_map.50.own), channel_id=1, source_target_pairs={{0,32},{32,0},{64,96},{96,64},{128,160},{160,128},{192,224},{224,1... | collective-permute-start | bytes 786440 | tf_op jit(solution)/shard_map/ppermute | solution.py:435
  10.6 10.1 %collective-permute-start.2 = (f32[2,2,48,128]{3,2,1,0:T(8,128)S(1)}, f32[2,2,48,128]{3,2,1,0:T(8,128)S(1)}, u32[]{:S(2)}, u32[]{:S(2)}) collective-permute-start(f32[2,2,48,128]{3,2,1,0:T(8,128)S(1)} %get-tuple-element.27), channel_id=1, source_target_pairs={{0,31},{1,2},{2,1},{3,4},{4,3},{5,6},{6,5},{7,8},{8,7},{9,10},{10,... | collective-permute-start | bytes 294920 | tf_op jit(solution)/shard_map/ppermute | solution.py:435
  18.8 3.5 %collective-permute-start.3 = (f32[2,2,48,128]{3,2,1,0:T(8,128)S(1)}, f32[2,2,48,128]{3,2,1,0:T(8,128)S(1)}, u32[]{:S(2)}, u32[]{:S(2)}) collective-permute-start(f32[2,2,48,128]{3,2,1,0:T(8,128)S(1)} %get-tuple-element.28), channel_id=1, source_target_pairs={{0,1},{1,0},{2,3},{3,2},{4,5},{5,4},{6,7},{7,6},{8,9},{9,8},{10,11... | collective-permute-start | bytes 294920 | tf_op jit(solution)/shard_map/ppermute | solution.py:435
  34.5 6.1 %collective-permute-start.5 = (f32[8,8,128]{2,1,0:T(8,128)S(1)}, f32[8,8,128]{2,1,0:T(8,128)S(1)}, u32[]{:S(2)}, u32[]{:S(2)}) collective-permute-start(f32[8,8,128]{2,1,0:T(8,128)S(1)} %all_to_all.5.own), channel_id=1, source_target_pairs={{0,31},{1,2},{2,1},{3,4},{4,3},{5,6},{6,5},{7,8},{8,7},{9,10},{10,... | collective-permute-start | bytes 98312 | tf_op jit(solution)/shard_map/ppermute | solution.py:435
  37.8 3.1 %collective-permute-start.4 = (f32[8,8,128]{2,1,0:T(8,128)S(1)}, f32[8,8,128]{2,1,0:T(8,128)S(1)}, u32[]{:S(2)}, u32[]{:S(2)}) collective-permute-start(f32[8,8,128]{2,1,0:T(8,128)S(1)} %all_to_all.5.own), channel_id=1, source_target_pairs={{0,1},{1,0},{2,3},{3,2},{4,5},{5,4},{6,7},{7,6},{8,9},{9,8},{10,11... | collective-permute-start | bytes 98312 | tf_op jit(solution)/shard_map/ppermute | solution.py:435

commit v4 on v3

--- a/solution.py
+++ b/solution.py
@@ -11,6 +11,7 @@
 CUT = slice(HALO - 4, HALO + BC + 4)
 KEPT = BC + 8
 HALF = ROWS // 2
+SENT = BC + 16
 PACK = HZ // 2
 SWEEPS_COARSE = 8
 WEIGHT = 0.8
@@ -184,8 +185,10 @@
     copies[2].wait()
 
 
-def margin_kernel(own, near_cast, far_cast, far_span, near_span):
-    lane = iota((ROWS, BS), 1)
+def margin_kernel(own, near_cast, far_cast, near_span, far_span):
+    lane = iota((SENT, BS), 1)
+    outer = (iota((SENT, BS), 0) < 8) | (iota((SENT, BS), 0) >= SENT - 8)
+    seg = lane % HALO
     for a in range(2):
         for group in range(2):
             head = tail = None
@@ -194,12 +197,18 @@
                     z = group * 4 + sub + 8 * half
                     start = 16 * sub + 64 * half
                     slab = extended(own, near_cast, far_cast, a, z)
-                    h = shift(slab, start, 1)
-                    t = shift(slab, start + HALO, 1)
+                    inner, far = slab[8 : ROWS - 8], jnp.concatenate([slab[:8], slab[8:24], slab[ROWS - 8 :]], axis=0)
+                    h = jnp.where(outer & (seg >= 12), shift(far, start + 12, 1), shift(inner, start, 1))
+                    t = jnp.where(outer & (seg < 4), shift(far, start + HALO - 12, 1), shift(inner, start + HALO, 1))
                     inside = (lane >= start) & (lane < start + HALO)
                     head = h if head is None else jnp.where(inside, h, head)
                     tail = t if tail is None else jnp.where(inside, t, tail)
             far_span[a, group], near_span[a, group] = by_side("span", tail, head)
+
+
+def spread_rows(sent, step, more):
+    moved = shift(sent, step, 1)
+    return jnp.concatenate([shift(sent[:8], step + more, 1), moved, shift(sent[-8:], step + more, 1)], axis=0)
 
 
 def own_kernel(own, near_cast, far_cast, x, b, cast, span, height, diag, relax, merged, inner, scratch):
@@ -230,7 +239,7 @@
 
 
 def edge_kernel(
-    far_span, near_span, inner, merged, x, b, cast, span, height, diag, relax,
+    near_span, far_span, inner, merged, x, b, cast, span, height, diag, relax,
     x1, b1, cast1, span1, height1, relax1, slots, scratch, rows8,
 ):
     first, last, outside = beyond(ROWS, HALO)
@@ -241,8 +250,7 @@
         for k in range(PACK):
             group, sub = divmod(k, 4)
             left, right = by_side("span", near_span[a, group], far_span[a, group])
-            l = shift(left, -16 * sub, 1)
-            r = shift(right, 48 - 16 * sub, 1)
+            l, r = spread_rows(left, -16 * sub, 12), spread_rows(right, 48 - 16 * sub, -12)
             value = jnp.where(lane < 16, l, jnp.where(lane >= 48, r, inner[a, k]))
             slabs.append(ends(value, first, last, HALO) if a == 0 else value)
         fields.append(slabs)
@@ -297,7 +305,7 @@
 
 
 def ascent_kernel(
-    own, near_column, far_column,
+    own, far_column, near_column,
     xo, bo, casto, spano, heighto, diago, relaxo,
     xe, be, caste, spane, heighte, diage, relaxe,
     x1, b1, cast1, span1, height1, relax1,
@@ -424,20 +432,15 @@
     )
 
 
-def swap(value, axis, far, periodic):
+def swap(value, axis, far):
     size = lax.axis_size(axis)
-    partner = [i ^ 1 for i in range(size)]
-    if far:
-        partner = [((i - 1) ^ 1) + 1 for i in range(size)]
-        partner = [p % size if periodic or 0 <= p < size else i for i, p in enumerate(partner)]
-        if not periodic:
-            partner[0], partner[-1] = 0, size - 1
+    partner = [(((i - 1) ^ 1) + 1) % size if far else i ^ 1 for i in range(size)]
     return lax.ppermute(value, axis, list(enumerate(partner)))
 
 
 def shards(phase, viscosity_table, pressure_source):
     count = lax.axis_size("cast")
-    packed = (2, 2, ROWS, BS)
+    packed = (2, 2, SENT, BS)
     own_state = [(HZ, KEPT, BS)] * 4 + [(HZ + 1, KEPT, BS)] + [(HZ, KEPT, BS)] * 2
     edge_state = [(PACK, KEPT, BS)] * 4 + [(PACK + 1, KEPT, BS)] + [(PACK, KEPT, BS)] * 2
     level1_state = [(8, HALF, BS)] * 4 + [(9, HALF, BS), (8, HALF, BS)]
@@ -445,11 +448,11 @@
     arguments = (pltpu.with_memory_space_constraint(a, pltpu.HBM) for a in (viscosity_table, phase, pressure_source))
     stage_scratch = [pltpu.SMEM((3,), F32), pltpu.VMEM((HZ, BC, BS), jnp.int32), pltpu.SemaphoreType.DMA((3,))]
     (own,) = call(stage_kernel, [HBM] * 3, [(2, HZ, BC, BS)], stage_scratch)(*arguments)
-    far_cast = swap(own, "cast", True, False)
-    near_cast = swap(own, "cast", False, False)
-    far_span, near_span = call(margin_kernel, [VMEM] * 3, [packed, packed])(own, near_cast, far_cast)
-    far_span = swap(far_span, "span", True, True)
-    near_span = swap(near_span, "span", False, True)
+    far_cast = swap(own, "cast", True)
+    near_cast = swap(own, "cast", False)
+    near_span, far_span = call(margin_kernel, [VMEM] * 3, [packed, packed])(own, near_cast, far_cast)
+    near_span = swap(near_span, "span", False)
+    far_span = swap(far_span, "span", True)
     *kept_own, merged, inner = call(
         own_kernel,
         [VMEM] * 3,
@@ -461,11 +464,11 @@
         [VMEM] * 4,
         edge_state + level1_state + [(count, 8, BS)],
         [(8, ROWS, BS), (4, 16, BS)],
-    )(far_span, near_span, inner, merged)
+    )(near_span, far_span, inner, merged)
 
     column = lax.all_to_all(slots, "cast", 0, 0)
-    far_column = swap(column, "span", True, True)
-    near_column = swap(column, "span", False, True)
+    near_column = swap(column, "span", False)
+    far_column = swap(column, "span", True)
     rows = 4 * count
     scratch = [
         (3, rows, BS),
@@ -481,7 +484,7 @@
     state = kept_own + kept_edge
     return tuple(
         call(ascent_kernel, [VMEM] * (3 + len(state)), [(HZ, BC, BS)] * 2, scratch, HBM)(
-            column, near_column, far_column, *state
+            column, far_column, near_column, *state
         )
     )
 

time: 44.8 us -> 41.6 us (0.929)
  waiting for transfers between devices: 8.74 us -> 4.27 us
  starting transfers between devices: 16 us -> 17.6 us
    ppermute x6, waiting for transfers between devices: 8.74 us -> 4.27 us  [swap(): return lax.ppermute(value, axis, list(enumerate(partner)))]
    ppermute x6, starting transfers between devices: 16 us -> 17.6 us  [swap(): return lax.ppermute(value, axis, list(enumerate(partner)))]
  transfers between devices with their start and end apart: 6 -> 6, of which waited for: 5 -> 2; matrix products, arithmetic and copies ran while one was open for 0% -> 0% of each run, Pallas kernels for 4% -> 4%
where the time goes in v4:
time: 41.6 us; the launch traced here: 41.5 us
  starting transfers between devices  17.6 us (42%)
  blocking collectives  10.6 us (25%)
  Pallas kernels  8.38 us (20%)
  waiting for transfers between devices  4.27 us (10%)
  between operations  0.66 us (2%)
    ppermute x6, starting transfers between devices, swap(): return lax.ppermute(value, axis, list(enumerate(partner)))  17.6 us
    all_to_all x1, blocking collectives, shards(): column = lax.all_to_all(slots, 'cast', 0, 0)  10.6 us
    ppermute x6, waiting for transfers between devices, swap(): return lax.ppermute(value, axis, list(enumerate(partner)))  4.27 us
    pallas_call x1, Pallas kernels, shards(): call(ascent_kernel, [VMEM] * (3 + len(state)), [(HZ, BC, BS)] * 2, scratc...  3.79 us
    pallas_call x1, Pallas kernels, shards(): call(own_kernel, [VMEM] * 3, own_state + [(HZ, HALF, BS), (2, PACK, ROWS,...  1.72 us
    pallas_call x1, Pallas kernels, shards(): call(edge_kernel, [VMEM] * 4, edge_state + level1_state + [(count, 8, BS)...  1.43 us
    pallas_call x1, Pallas kernels, shards(): call(stage_kernel, [HBM] * 3, [(2, HZ, BC, BS)], stage_scratch)(*arguments)  1 us
  transfers between devices with their start and end apart: 6, of which 2 were waited for; matrix products, arithmetic and copies ran while one was open for 0% of the time, Pallas kernels for 4%

profile of v4, /device:TPU:1, one launch (start us, length us, event | category | flops | bytes accessed | tf_op | source)
XLA Modules:
  0.0 41.5 jit_solution(4081870720637436813)
XLA Ops:
  0.6 1.0 %shard_map.50.own = f32[2,16,16,128]{3,2,1,0:T(8,128)S(1)} custom-call(f32[3]{0:T(128)} %table_in.1, s32[16,16,128]{2,1,0:T(8,128)} %phase_in.1, f32[16,16,128]{2,1,0:T(8,128)} %source_in.1), custom_call_target="tpu_custom_call" | custom-call | tf_op jit(solution)/shard_map/pallas_call | solution.py:450
  1.6 2.7 %collective-permute-start.1 = (f32[2,16,16,128]{3,2,1,0:T(8,128)S(1)}, f32[2,16,16,128]{3,2,1,0:T(8,128)S(1)}, u32[]{:S(2)}, u32[]{:S(2)}) collective-permute-start(f32[2,16,16,128]{3,2,1,0:T(8,128)S(1)} %shard_map.50.own), channel_id=1, source_target_pairs={{0,224},{32,64},{64,32},{96,128},{128,96},{160,192},{192,160},{224... | collective-permute-start | bytes 786440 | tf_op jit(solution)/shard_map/ppermute | solution.py:438
  4.3 1.1 %collective-permute-start = (f32[2,16,16,128]{3,2,1,0:T(8,128)S(1)}, f32[2,16,16,128]{3,2,1,0:T(8,128)S(1)}, u32[]{:S(2)}, u32[]{:S(2)}) collective-permute-start(f32[2,16,16,128]{3,2,1,0:T(8,128)S(1)} %shard_map.50.own), channel_id=1, source_target_pairs={{0,32},{32,0},{64,96},{96,64},{128,160},{160,128},{192,224},{224,1... | collective-permute-start | bytes 786440 | tf_op jit(solution)/shard_map/ppermute | solution.py:438
  5.4 3.0 %collective-permute-done.1.far_cast = f32[2,16,16,128]{3,2,1,0:T(8,128)S(1)} collective-permute-done((f32[2,16,16,128]{3,2,1,0:T(8,128)S(1)}, f32[2,16,16,128]{3,2,1,0:T(8,128)S(1)}, u32[]{:S(2)}, u32[]{:S(2)}) %collective-permute-start.1) | collective-permute-done | bytes 262176 | tf_op jit(solution)/shard_map/ppermute | solution.py:438
  8.4 0.0 collective-permute-done.near_cast
  8.4 0.4 %shard_map.51 = (f32[2,2,32,128]{3,2,1,0:T(8,128)S(1)}, f32[2,2,32,128]{3,2,1,0:T(8,128)S(1)}) custom-call(f32[2,16,16,128]{3,2,1,0:T(8,128)S(1)} %shard_map.50.own, f32[2,16,16,128]{3,2,1,0:T(8,128)S(1)} %collective-permute-done.near_cast, f32[2,16,16,128]{3,2,1,0:T(8,128)S(1)} %collective-permute-done.1.far_cast), custom_call_target="tpu_custom_call" | custom-call | tf_op jit(solution)/shard_map/pallas_call | solution.py:453
  8.8 1.7 %collective-permute-start.2 = (f32[2,2,32,128]{3,2,1,0:T(8,128)S(1)}, f32[2,2,32,128]{3,2,1,0:T(8,128)S(1)}, u32[]{:S(2)}, u32[]{:S(2)}) collective-permute-start(f32[2,2,32,128]{3,2,1,0:T(8,128)S(1)} %get-tuple-element.27), channel_id=1, source_target_pairs={{0,1},{1,0},{2,3},{3,2},{4,5},{5,4},{6,7},{7,6},{8,9},{9,8},{10,11... | collective-permute-start | bytes 196616 | tf_op jit(solution)/shard_map/ppermute | solution.py:438
  10.5 7.2 %collective-permute-start.3 = (f32[2,2,32,128]{3,2,1,0:T(8,128)S(1)}, f32[2,2,32,128]{3,2,1,0:T(8,128)S(1)}, u32[]{:S(2)}, u32[]{:S(2)}) collective-permute-start(f32[2,2,32,128]{3,2,1,0:T(8,128)S(1)} %get-tuple-element.28), channel_id=1, source_target_pairs={{0,31},{1,2},{2,1},{3,4},{4,3},{5,6},{6,5},{7,8},{8,7},{9,10},{10,... | collective-permute-start | bytes 196616 | tf_op jit(solution)/shard_map/ppermute | solution.py:438
  17.7 1.7 %shard_map.52 = (f32[16,24,128]{2,1,0:T(8,128)S(1)}, f32[16,24,128]{2,1,0:T(8,128)S(1)}, f32[16,24,128]{2,1,0:T(8,128)S(1)}, f32[16,24,128]{2,1,0:T(8,128)S(1)},...) custom-call(f32[2,16,16,128]{3,2,1,0:T(8,128)S(1)} %shard_map.50.own, ...), custom_call_target="tpu_custom_call" | custom-call | tf_op jit(solution)/shard_map/pallas_call | solution.py:456
  19.4 0.0 collective-permute-done.2.near_span
  19.4 0.0 collective-permute-done.3.far_span
  19.5 1.4 %shard_map.53 = (f32[8,24,128]{2,1,0:T(8,128)S(1)}, f32[8,24,128]{2,1,0:T(8,128)S(1)}, f32[8,24,128]{2,1,0:T(8,128)S(1)}, f32[8,24,128]{2,1,0:T(8,128)S(1)}, f32...) custom-call(f32[2,2,32,128]{3,2,1,0:T(8,128)S(1)} %collective-permut, ...), custom_call_target="tpu_custom_call" | custom-call | tf_op jit(solution)/shard_map/pallas_call | solution.py:462
  20.9 10.6 %all_to_all.5.own = f32[8,8,128]{2,1,0:T(8,128)S(1)} all-to-all(f32[8,8,128]{2,1,0:T(8,128)S(1)} %get-tuple-element.31), channel_id=1, replica_groups=mesh['cast'=8,'span'=32] {'cast'}, dimensions={0} | all-to-all | bytes 65536 | tf_op jit(solution)/shard_map/all_to_all | solution.py:469
  31.5 0.0 collective-permute-start.5
  31.5 4.9 %collective-permute-start.4 = (f32[8,8,128]{2,1,0:T(8,128)S(1)}, f32[8,8,128]{2,1,0:T(8,128)S(1)}, u32[]{:S(2)}, u32[]{:S(2)}) collective-permute-start(f32[8,8,128]{2,1,0:T(8,128)S(1)} %all_to_all.5.own), channel_id=1, source_target_pairs={{0,31},{1,2},{2,1},{3,4},{4,3},{5,6},{6,5},{7,8},{8,7},{9,10},{10,... | collective-permute-start | bytes 98312 | tf_op jit(solution)/shard_map/ppermute | solution.py:438
  36.4 0.0 collective-permute-done.5.near_column
  36.4 1.3 %collective-permute-done.4.far_column = f32[8,8,128]{2,1,0:T(8,128)S(1)} collective-permute-done((f32[8,8,128]{2,1,0:T(8,128)S(1)}, f32[8,8,128]{2,1,0:T(8,128)S(1)}, u32[]{:S(2)}, u32[]{:S(2)}) %collective-permute-start.4) | collective-permute-done | bytes 32800 | tf_op jit(solution)/shard_map/ppermute | solution.py:438
  37.7 3.8 %shard_map.54 = (f32[16,16,128]{2,1,0:T(8,128)}, f32[16,16,128]{2,1,0:T(8,128)}) custom-call(f32[8,8,128]{2,1,0:T(8,128)S(1)} %all_to_all.5.own, f32[8,8,128]{2,1,0:T(8,128)S(1)} %collective-permute-done.4.far_column, f32[8,8,128]{2,1,0:T(8,128)S(1)} %collective-permute-done.5.near_column, f32[16,24,128]{2,1,0:T(8,128)S(1)} %get-tuple-element.32.xo, ...), custom_call_target="tpu_custom_call" | custom-call | tf_op jit(solution)/shard_map/pallas_call | solution.py:486
Async XLA Ops:
  1.6 6.7 %collective-permute-start.1 = (f32[2,16,16,128]{3,2,1,0:T(8,128)S(1)}, f32[2,16,16,128]{3,2,1,0:T(8,128)S(1)}, u32[]{:S(2)}, u32[]{:S(2)}) collective-permute-start(f32[2,16,16,128]{3,2,1,0:T(8,128)S(1)} %shard_map.50.own), channel_id=1, source_target_pairs={{0,224},{32,64},{64,32},{96,128},{128,96},{160,192},{192,160},{224... | collective-permute-start | bytes 786440 | tf_op jit(solution)/shard_map/ppermute | solution.py:438
  4.3 4.1 %collective-permute-start = (f32[2,16,16,128]{3,2,1,0:T(8,128)S(1)}, f32[2,16,16,128]{3,2,1,0:T(8,128)S(1)}, u32[]{:S(2)}, u32[]{:S(2)}) collective-permute-start(f32[2,16,16,128]{3,2,1,0:T(8,128)S(1)} %shard_map.50.own), channel_id=1, source_target_pairs={{0,32},{32,0},{64,96},{96,64},{128,160},{160,128},{192,224},{224,1... | collective-permute-start | bytes 786440 | tf_op jit(solution)/shard_map/ppermute | solution.py:438
  8.8 10.6 %collective-permute-start.2 = (f32[2,2,32,128]{3,2,1,0:T(8,128)S(1)}, f32[2,2,32,128]{3,2,1,0:T(8,128)S(1)}, u32[]{:S(2)}, u32[]{:S(2)}) collective-permute-start(f32[2,2,32,128]{3,2,1,0:T(8,128)S(1)} %get-tuple-element.27), channel_id=1, source_target_pairs={{0,1},{1,0},{2,3},{3,2},{4,5},{5,4},{6,7},{7,6},{8,9},{9,8},{10,11... | collective-permute-start | bytes 196616 | tf_op jit(solution)/shard_map/ppermute | solution.py:438
  10.5 8.9 %collective-permute-start.3 = (f32[2,2,32,128]{3,2,1,0:T(8,128)S(1)}, f32[2,2,32,128]{3,2,1,0:T(8,128)S(1)}, u32[]{:S(2)}, u32[]{:S(2)}) collective-permute-start(f32[2,2,32,128]{3,2,1,0:T(8,128)S(1)} %get-tuple-element.28), channel_id=1, source_target_pairs={{0,31},{1,2},{2,1},{3,4},{4,3},{5,6},{6,5},{7,8},{8,7},{9,10},{10,... | collective-permute-start | bytes 196616 | tf_op jit(solution)/shard_map/ppermute | solution.py:438
  31.5 4.9 %collective-permute-start.5 = (f32[8,8,128]{2,1,0:T(8,128)S(1)}, f32[8,8,128]{2,1,0:T(8,128)S(1)}, u32[]{:S(2)}, u32[]{:S(2)}) collective-permute-start(f32[8,8,128]{2,1,0:T(8,128)S(1)} %all_to_all.5.own), channel_id=1, source_target_pairs={{0,1},{1,0},{2,3},{3,2},{4,5},{5,4},{6,7},{7,6},{8,9},{9,8},{10,11... | collective-permute-start | bytes 98312 | tf_op jit(solution)/shard_map/ppermute | solution.py:438
  31.5 6.2 %collective-permute-start.4 = (f32[8,8,128]{2,1,0:T(8,128)S(1)}, f32[8,8,128]{2,1,0:T(8,128)S(1)}, u32[]{:S(2)}, u32[]{:S(2)}) collective-permute-start(f32[8,8,128]{2,1,0:T(8,128)S(1)} %all_to_all.5.own), channel_id=1, source_target_pairs={{0,31},{1,2},{2,1},{3,4},{4,3},{5,6},{6,5},{7,8},{8,7},{9,10},{10,... | collective-permute-start | bytes 98312 | tf_op jit(solution)/shard_map/ppermute | solution.py:438

commit v5 on v4

--- a/solution.py
+++ b/solution.py
@@ -27,8 +27,7 @@
     return lax.broadcasted_iota(jnp.int32, shape, axis)
 
 
-def product(a, where):
-    b = jnp.where(where, 1.0, 0.0).astype(BF16)
+def product(a, b):
     high = a.astype(BF16)
     low = (a - high.astype(F32)).astype(BF16)
     return jnp.dot(high, b, preferred_element_type=F32) + jnp.dot(low, b, preferred_element_type=F32)
@@ -76,6 +75,27 @@
             (1.0 - WEIGHT) * x[z] + self.relax[z] * (self.near(x, z) + self.source[z])
             for z in range(self.depth)
         ]
+
+    def solve(self, sweeps):
+        part = [
+            (
+                relax * self.cast[z],
+                relax * shift(self.cast[z], -1, 0),
+                relax * self.span[z],
+                relax * shift(self.span[z], -1, 1),
+                relax * self.height[1],
+            )
+            for z, relax in enumerate(self.relax)
+        ]
+        first = x = self.start()
+        for _ in range(sweeps):
+            x = [
+                ((1.0 - WEIGHT) * x[z] + first[z] + part[z][4] * x[1 - z])
+                + (part[z][0] * shift(x[z], 1, 0) + part[z][1] * shift(x[z], -1, 0))
+                + (part[z][2] * shift(x[z], 1, 1) + part[z][3] * shift(x[z], -1, 1))
+                for z in range(2)
+            ]
+        return x
 
     def residual(self, x):
         return [self.source[z] - self.diag[z] * x[z] + self.near(x, z) for z in range(self.depth)]
@@ -185,25 +205,63 @@
     copies[2].wait()
 
 
-def margin_kernel(own, near_cast, far_cast, near_span, far_span):
-    lane = iota((SENT, BS), 1)
-    outer = (iota((SENT, BS), 0) < 8) | (iota((SENT, BS), 0) >= SENT - 8)
+def ones(where):
+    return jnp.where(where, 1.0, 0.0).astype(BF16)
+
+
+def prepare_kernel(own, near_own, far_own, own_merge, edge_merge, move, narrow, widen, grow, double, expand):
+    lane = iota((BC, BS), 1)
+    for a in range(2):
+        for group in range(2):
+            head = tail = None
+            for start, z in places(group):
+                h, t = shift(own[a, z], start, 1), shift(own[a, z], start + HALO, 1)
+                inside = (lane >= start) & (lane < start + HALO)
+                head = h if head is None else jnp.where(inside, h, head)
+                tail = t if tail is None else jnp.where(inside, t, tail)
+            far_own[a, group], near_own[a, group] = by_side("span", tail, head)
+    i, j = iota((BS, BS), 0), iota((BS, BS), 1)
+    own_merge[...] = ones((i // 2 == j) & (i >= 8) & (i < 120))
+    narrow[...] = ones(((i < 64) & (i // 2 == j)) | ((i >= 96) & (i // 2 + 64 == j)))
+    widen[...] = ones(((j < 64) & (j // 2 == i)) | ((j >= 96) & (j // 2 + 64 == i)))
+    grow[...] = ones(((j < 96) & (j // 2 == i)) | ((j >= 96) & (j // 2 + 64 == i)))
+    double[...] = ones(j // 2 == i)
+    i, j = iota((BS, 2 * BS), 0), iota((BS, 2 * BS), 1)
+    m = i % 64
+    target = jnp.where(m < 24, (m // 2 + 120) % BS, m // 2 + 40)
+    edge_merge[...] = ones(((m < 24) | (m >= 40)) & (target == j % BS) & (i // 64 == j // BS))
+    i, j = iota((4 * BS, BS), 0), iota((4 * BS, BS), 1)
+    move[...] = ones((i % BS < 64) & (i % BS // 2 + 32 * (i // BS) == j))
+    i, j = iota((2 * BS, BS), 0), iota((2 * BS, BS), 1)
+    m = j % 64
+    origin = jnp.where(m < 32, (m // 2 + 120) % BS, m // 2 + 40)
+    expand[...] = ones((origin == i % BS) & (i // BS == j // 64))
+
+
+def places(group):
+    return [(16 * sub + 64 * half, group * 4 + sub + 8 * half) for sub in range(4) for half in range(2)]
+
+
+def margin_kernel(near_own, far_own, near_cast, far_cast, near_span, far_span):
+    lane = iota((16, BS), 1)
     seg = lane % HALO
     for a in range(2):
         for group in range(2):
             head = tail = None
-            for sub in range(4):
-                for half in range(2):
-                    z = group * 4 + sub + 8 * half
-                    start = 16 * sub + 64 * half
-                    slab = extended(own, near_cast, far_cast, a, z)
-                    inner, far = slab[8 : ROWS - 8], jnp.concatenate([slab[:8], slab[8:24], slab[ROWS - 8 :]], axis=0)
-                    h = jnp.where(outer & (seg >= 12), shift(far, start + 12, 1), shift(inner, start, 1))
-                    t = jnp.where(outer & (seg < 4), shift(far, start + HALO - 12, 1), shift(inner, start + HALO, 1))
-                    inside = (lane >= start) & (lane < start + HALO)
-                    head = h if head is None else jnp.where(inside, h, head)
-                    tail = t if tail is None else jnp.where(inside, t, tail)
-            far_span[a, group], near_span[a, group] = by_side("span", tail, head)
+            for start, z in places(group):
+                before, after = by_side("cast", near_cast[a, z], far_cast[a, z])
+                inner = jnp.concatenate([before[8:], after[:8]], axis=0)
+                far = jnp.concatenate([before[:8], after[8:]], axis=0)
+                h = jnp.where(seg >= 12, shift(far, start + 12, 1), shift(inner, start, 1))
+                t = jnp.where(seg < 4, shift(far, start + HALO - 12, 1), shift(inner, start + HALO, 1))
+                inside = (lane >= start) & (lane < start + HALO)
+                head = h if head is None else jnp.where(inside, h, head)
+                tail = t if tail is None else jnp.where(inside, t, tail)
+            sides = by_side("span", tail, head)
+            for out, packed, value in ((far_span, far_own, sides[0]), (near_span, near_own, sides[1])):
+                out[a, group, :8] = value[:8]
+                out[a, group, 8:24] = packed[a, group]
+                out[a, group, 24:] = value[8:]
 
 
 def spread_rows(sent, step, more):
@@ -211,7 +269,7 @@
     return jnp.concatenate([shift(sent[:8], step + more, 1), moved, shift(sent[-8:], step + more, 1)], axis=0)
 
 
-def own_kernel(own, near_cast, far_cast, x, b, cast, span, height, diag, relax, merged, inner, scratch):
+def own_kernel(own, near_cast, far_cast, own_merge, x, b, cast, span, height, diag, relax, merged, inner, scratch):
     first, last, outside = beyond(ROWS, HALO)
     visc, source = [], []
     for z in range(HZ):
@@ -231,17 +289,12 @@
     values = level.sweep(level.start())
     keep(level, values, (x, b, cast, span, height, diag, relax))
     parts = coarse_parts(visc, level.residual(values), scratch)
-    i, j = iota((BS, BS), 0), iota((BS, BS), 1)
-    merge = (i // 2 == j) & (i >= 8) & (i < 120)
-    total = product(parts, merge)
+    total = product(parts, own_merge[...])
     for k in range(HZ):
         merged[k] = total[HALF * k : HALF * (k + 1)]
 
 
-def edge_kernel(
-    near_span, far_span, inner, merged, x, b, cast, span, height, diag, relax,
-    x1, b1, cast1, span1, height1, relax1, slots, scratch, rows8,
-):
+def edge_levels(near_span, far_span, inner, merged, edge_merge, scratch):
     first, last, outside = beyond(ROWS, HALO)
     lane = iota((ROWS, BS), 1) % 64
     fields = []
@@ -257,14 +310,9 @@
     visc, source = fields
     level = fine_level(visc, source, outside, True)
     values = level.sweep(level.start())
-    keep(level, values, (x, b, cast, span, height, diag, relax))
+    fine = level, values
     parts = coarse_parts(visc, level.residual(values), scratch)
-    i, j = iota((BS, 2 * BS), 0), iota((BS, 2 * BS), 1)
-    m, ring_lane = i % 64, j % BS
-    target = jnp.where(m < 24, (m // 2 + 120) % BS, m // 2 + 40)
-    used = (m < 24) | (m >= 40)
-    merge = used & (target == ring_lane) & (i // 64 == j // BS)
-    total = product(parts, merge)
+    total = product(parts, edge_merge[...])
 
     edge = HALO // 2
     first, last, outside = beyond(HALF, edge)
@@ -284,14 +332,26 @@
     span_faces = [harmonic(shift(c, 1, 1), c) for c in coeff]
     diagonal = [diagonal_of(cast_faces[z], span_faces[z], height[z], height[z + 1]) for z in range(8)]
     level = Level(cast_faces, span_faces, height, diagonal, [weight / d for d in diagonal], source, 8)
-    values = level.sweep(level.start())
-    for ref, items in ((x1, values), (b1, source), (cast1, cast_faces), (span1, span_faces), (height1, height), (relax1, level.relax)):
+    return fine, (level, level.sweep(level.start()), coeff)
+
+
+def state_kernel(
+    near_span, far_span, inner, merged, edge_merge, x, b, cast, span, height, diag, relax,
+    x1, b1, cast1, span1, height1, relax1, scratch,
+):
+    fine, (level, values, _) = edge_levels(near_span, far_span, inner, merged, edge_merge, scratch)
+    keep(*fine, (x, b, cast, span, height, diag, relax))
+    kept = (x1, values), (b1, level.source), (cast1, level.cast), (span1, level.span), (height1, level.height), (relax1, level.relax)
+    for ref, items in kept:
         for z, item in enumerate(items):
             ref[z] = item
+
+
+def edge_kernel(near_span, far_span, inner, merged, edge_merge, move, slots, scratch, rows8):
+    _, (level, values, coeff) = edge_levels(near_span, far_span, inner, merged, edge_merge, scratch)
     remains = level.residual(values)
-
-    i, j = iota((4 * BS, BS), 0), iota((4 * BS, BS), 1)
-    move = (i % BS < 64) & (i % BS // 2 + 32 * (i // BS) == j)
+    edge = HALO // 2
+
     fields = []
     for k in range(4):
         rows = slice(edge, edge + 8)
@@ -299,13 +359,13 @@
         r = remains[2 * k][rows] + remains[2 * k + 1][rows]
         rows8[k] = jnp.concatenate([0.125 * c, 0.5 * r], axis=0)
         fields.append(rows8[k, pl.ds(0, 8, stride=2), :] + rows8[k, pl.ds(1, 8, stride=2), :])
-    total = product(jnp.concatenate(fields, axis=1), move)
+    total = product(jnp.concatenate(fields, axis=1), move[...])
     for d in range(slots.shape[0]):
         slots[d] = total
 
 
 def ascent_kernel(
-    own, far_column, near_column,
+    own, far_column, near_column, narrow, widen, grow, double, expand,
     xo, bo, casto, spano, heighto, diago, relaxo,
     xe, be, caste, spane, heighte, diage, relaxe,
     x1, b1, cast1, span1, height1, relax1,
@@ -336,25 +396,20 @@
     x2 = level2.sweep(level2.start())
     remains = level2.residual(x2)
 
-    a, b = iota((128, 128), 0), iota((128, 128), 1)
-    narrow = ((a < 64) & (a // 2 == b)) | ((a >= 96) & (a // 2 + 64 == b))
-    widen = ((b < 64) & (b // 2 == a)) | ((b >= 96) & (b // 2 + 64 == a))
     gathered = []
     for field in (coeff2, remains):
         for k in range(2):
             gathered.append(pair_rows(field[2 * k] + field[2 * k + 1], pairs))
-    merged = product(jnp.concatenate(gathered, axis=0), narrow)
+    merged = product(jnp.concatenate(gathered, axis=0), narrow[...])
     half = rows // 2
     lane3 = iota((half, 128), 1)
     known = (lane3 < 32) | (lane3 >= 112)
     coeff3 = [jnp.where(known, 0.125 * merged[half * k : half * (k + 1)], 1.0) for k in range(2)]
     source3 = [0.5 * merged[half * (2 + k) : half * (3 + k)] for k in range(2)]
     level3 = whole_level(coeff3, source3)
-    x3 = level3.start()
-    for _ in range(SWEEPS_COARSE - 1):
-        x3 = level3.sweep(x3)
-
-    spread = product(jnp.concatenate(x3, axis=0), widen)
+    x3 = level3.solve(SWEEPS_COARSE - 1)
+
+    spread = product(jnp.concatenate(x3, axis=0), widen[...])
     for k in range(2):
         wide2[k, pl.ds(0, half, stride=2), :] = spread[half * k : half * (k + 1)]
         wide2[k, pl.ds(1, half, stride=2), :] = spread[half * k : half * (k + 1)]
@@ -365,9 +420,8 @@
         padded2[z, 0:8] = jnp.zeros((8, 128), F32)
         padded2[z, 8 : 8 + rows] = x2[z]
         padded2[z, 8 + rows : 16 + rows] = jnp.zeros((8, 128), F32)
-    grow = ((b < 96) & (b // 2 == a)) | ((b >= 96) & (b // 2 + 64 == a))
     local = [padded2[z, pl.ds(4 * index + 4, 16), :] for z in range(4)]
-    spread = product(jnp.concatenate(local, axis=0), grow)
+    spread = product(jnp.concatenate(local, axis=0), grow[...])
     for z in range(4):
         wide1[z, pl.ds(0, 16, stride=2), :] = spread[16 * z : 16 * z + 16]
         wide1[z, pl.ds(1, 16, stride=2), :] = spread[16 * z : 16 * z + 16]
@@ -375,17 +429,12 @@
     x = [x1[z] + wide1[z // 2, 0:HALF] for z in range(8)]
     x = level1.sweep(level1.sweep(x))
 
-    i, j = iota((BS, BS), 0), iota((BS, BS), 1)
-    spread = product(jnp.concatenate(x, axis=0), j // 2 == i)
+    spread = product(jnp.concatenate(x, axis=0), double[...])
     for z in range(8):
         for s in range(2):
             wide_own[z, pl.ds(s, HALF, stride=2), :] = spread[HALF * z : HALF * (z + 1)]
-    i, j = iota((2 * BS, BS), 0), iota((2 * BS, BS), 1)
-    m = j % 64
-    origin = jnp.where(m < 32, (m // 2 + 120) % BS, m // 2 + 40)
-    expand = (origin == i % BS) & (i // BS == j // 64)
     sides = [jnp.concatenate([x[k], x[k + 4]], axis=1) for k in range(4)]
-    spread = product(jnp.concatenate(sides, axis=0), expand)
+    spread = product(jnp.concatenate(sides, axis=0), expand[...])
     for k in range(4):
         for s in range(2):
             wide_edge[k, pl.ds(s, HALF, stride=2), :] = spread[HALF * k : HALF * (k + 1)]
@@ -398,20 +447,27 @@
     lane = iota((BC, BS), 1)
     rows = slice(4, 4 + BC)
 
-    def give(number, out, mid, side):
-        for z in range(HZ):
-            half, k = divmod(z, PACK)
-            low = shift(side[k][rows], -16 - 64 * half, 1)
-            high = shift(side[k][rows], 80 - 64 * half, 1)
-            results[number, z] = jnp.where(lane < 8, low, jnp.where(lane >= 120, high, mid[z][rows]))
-        copy = pltpu.make_async_copy(results.at[number], out, sems.at[number])
-        copy.start()
-        return copy
-
-    first = give(0, solution_out, own_x, edge_x)
-    second = give(1, residual_out, level_own.residual(own_x), level_edge.residual(edge_x))
-    first.wait()
-    second.wait()
+    copies = []
+
+    def give(number, out, z, mid, side):
+        half, k = divmod(z, PACK)
+        low = shift(side[rows], -16 - 64 * half, 1)
+        high = shift(side[rows], 80 - 64 * half, 1)
+        results[number, z] = jnp.where(lane < 8, low, jnp.where(lane >= 120, high, mid[rows]))
+        if z % 4 == 3:
+            quarter = pl.ds(z - 3, 4)
+            copy = pltpu.make_async_copy(results.at[number, quarter], out.at[quarter], sems.at[number, z // 4])
+            copy.start()
+            copies.append(copy)
+
+    for z in range(HZ):
+        give(0, solution_out, z, own_x[z], edge_x[z % PACK])
+    edge_r = level_edge.residual(edge_x)
+    own_r = level_own.residual(own_x)
+    for z in range(HZ):
+        give(1, residual_out, z, own_r[z], edge_r[z % PACK])
+    for copy in copies:
+        copy.wait()
 
 
 VMEM = pl.BlockSpec(memory_space=pltpu.VMEM)
@@ -425,7 +481,7 @@
         kernel,
         in_specs=in_specs,
         out_specs=[out_spec] * len(outs),
-        out_shape=[jax.ShapeDtypeStruct(s, F32) for s in outs],
+        out_shape=[jax.ShapeDtypeStruct(s, F32) if isinstance(s, tuple) else s for s in outs],
         scratch_shapes=[pltpu.VMEM(s, F32) if isinstance(s, tuple) else s for s in scratch],
         compiler_params=PARAMS,
         interpret=INTERPRET,
@@ -450,21 +506,27 @@
     (own,) = call(stage_kernel, [HBM] * 3, [(2, HZ, BC, BS)], stage_scratch)(*arguments)
     far_cast = swap(own, "cast", True)
     near_cast = swap(own, "cast", False)
-    near_span, far_span = call(margin_kernel, [VMEM] * 3, [packed, packed])(own, near_cast, far_cast)
+    square = (BS, BS)
+    tables = [square, (BS, 2 * BS), (4 * BS, BS), square, square, square, square, (2 * BS, BS)]
+    tables = [jax.ShapeDtypeStruct(t, BF16) for t in tables]
+    near_own, far_own, own_merge, edge_merge, move, *spreads = call(
+        prepare_kernel, [VMEM], [(2, 2, BC, BS)] * 2 + tables
+    )(own)
+    near_span, far_span = call(margin_kernel, [VMEM] * 4, [packed, packed])(near_own, far_own, near_cast, far_cast)
     near_span = swap(near_span, "span", False)
     far_span = swap(far_span, "span", True)
     *kept_own, merged, inner = call(
         own_kernel,
-        [VMEM] * 3,
+        [VMEM] * 4,
         own_state + [(HZ, HALF, BS), (2, PACK, ROWS, BS)],
         [(HZ, ROWS, BS)],
-    )(own, near_cast, far_cast)
-    *kept_edge, slots = call(
-        edge_kernel,
-        [VMEM] * 4,
-        edge_state + level1_state + [(count, 8, BS)],
-        [(8, ROWS, BS), (4, 16, BS)],
-    )(near_span, far_span, inner, merged)
+    )(own, near_cast, far_cast, own_merge)
+    (slots,) = call(
+        edge_kernel, [VMEM] * 6, [(count, 8, BS)], [(8, ROWS, BS), (4, 16, BS)]
+    )(near_span, far_span, inner, merged, edge_merge, move)
+    kept_edge = call(state_kernel, [VMEM] * 5, edge_state + level1_state, [(8, ROWS, BS)])(
+        near_span, far_span, inner, merged, edge_merge
+    )
 
     column = lax.all_to_all(slots, "cast", 0, 0)
     near_column = swap(column, "span", False)
@@ -479,9 +541,9 @@
         (8, ROWS, BS),
         (4, ROWS, BS),
         (2, HZ, BC, BS),
-        pltpu.SemaphoreType.DMA((2,)),
+        pltpu.SemaphoreType.DMA((2, 4)),
     ]
-    state = kept_own + kept_edge
+    state = spreads + kept_own + list(kept_edge)
     return tuple(
         call(ascent_kernel, [VMEM] * (3 + len(state)), [(HZ, BC, BS)] * 2, scratch, HBM)(
             column, far_column, near_column, *state

time: 41.6 us -> 41.4 us (level)
  waiting for transfers between devices: 4.27 us -> 2.9 us
  Pallas kernels: 8.38 us -> 9.42 us
    ppermute x6, waiting for transfers between devices: 4.27 us -> 2.9 us  [swap(): return lax.ppermute(value, axis, list(enumerate(partner)))]
    pallas_call x3 -> x5, Pallas kernels: 3.6 us -> 4.65 us  [the longest x1 1.68 us: shards(): call(own_kernel, [VMEM] * 4, own_state + [(HZ, HALF, BS), (2, PACK, ROWS,...]
  transfers between devices with their start and end apart: 6 -> 6, of which waited for: 2 -> 2; matrix products, arithmetic and copies ran while one was open for 0% -> 0% of each run, Pallas kernels for 4% -> 7%
where the time goes in v5:
time: 41.4 us; the launch traced here: 41.2 us
  starting transfers between devices  17.6 us (43%)
  blocking collectives  10.6 us (26%)
  Pallas kernels  9.42 us (23%)
  waiting for transfers between devices  2.9 us (7%)
  between operations  0.68 us (2%)
    ppermute x6, starting transfers between devices, swap(): return lax.ppermute(value, axis, list(enumerate(partner)))  17.6 us
    all_to_all x1, blocking collectives, shards(): column = lax.all_to_all(slots, 'cast', 0, 0)  10.6 us
    pallas_call x1, Pallas kernels, shards(): call(ascent_kernel, [VMEM] * (3 + len(state)), [(HZ, BC, BS)] * 2, scratc...  3.78 us
    ppermute x6, waiting for transfers between devices, swap(): return lax.ppermute(value, axis, list(enumerate(partner)))  2.9 us
    pallas_call x1, Pallas kernels, shards(): call(own_kernel, [VMEM] * 4, own_state + [(HZ, HALF, BS), (2, PACK, ROWS,...  1.68 us
    pallas_call x1, Pallas kernels, shards(): call(edge_kernel, [VMEM] * 6, [(count, 8, BS)], [(8, ROWS, BS), (4, 16, B...  1.29 us
    pallas_call x1, Pallas kernels, shards(): call(state_kernel, [VMEM] * 5, edge_state + level1_state, [(8, ROWS, BS)])  1.12 us
    pallas_call x1, Pallas kernels, shards(): call(stage_kernel, [HBM] * 3, [(2, HZ, BC, BS)], stage_scratch)(*arguments)  1 us
  transfers between devices with their start and end apart: 6, of which 2 were waited for; matrix products, arithmetic and copies ran while one was open for 0% of the time, Pallas kernels for 7%

profile of v5, /device:TPU:1, one launch (start us, length us, event | category | flops | bytes accessed | tf_op | source)
XLA Modules:
  0.0 41.2 jit_solution(3473037151266231805)
XLA Ops:
  0.6 1.0 %shard_map.50.own = f32[2,16,16,128]{3,2,1,0:T(8,128)S(1)} custom-call(f32[3]{0:T(128)} %table_in.1, s32[16,16,128]{2,1,0:T(8,128)} %phase_in.1, f32[16,16,128]{2,1,0:T(8,128)} %source_in.1), custom_call_target="tpu_custom_call" | custom-call | tf_op jit(solution)/shard_map/pallas_call | solution.py:506
  1.6 2.7 %collective-permute-start.1 = (f32[2,16,16,128]{3,2,1,0:T(8,128)S(1)}, f32[2,16,16,128]{3,2,1,0:T(8,128)S(1)}, u32[]{:S(2)}, u32[]{:S(2)}) collective-permute-start(f32[2,16,16,128]{3,2,1,0:T(8,128)S(1)} %shard_map.50.own), channel_id=1, source_target_pairs={{0,224},{32,64},{64,32},{96,128},{128,96},{160,192},{192,160},{224... | collective-permute-start | bytes 786440 | tf_op jit(solution)/shard_map/ppermute | solution.py:494
  4.3 1.1 %collective-permute-start = (f32[2,16,16,128]{3,2,1,0:T(8,128)S(1)}, f32[2,16,16,128]{3,2,1,0:T(8,128)S(1)}, u32[]{:S(2)}, u32[]{:S(2)}) collective-permute-start(f32[2,16,16,128]{3,2,1,0:T(8,128)S(1)} %shard_map.50.own), channel_id=1, source_target_pairs={{0,32},{32,0},{64,96},{96,64},{128,160},{160,128},{192,224},{224,1... | collective-permute-start | bytes 786440 | tf_op jit(solution)/shard_map/ppermute | solution.py:494
  5.4 0.2 shard_map.51
  5.7 2.7 %collective-permute-done.1.far_cast = f32[2,16,16,128]{3,2,1,0:T(8,128)S(1)} collective-permute-done((f32[2,16,16,128]{3,2,1,0:T(8,128)S(1)}, f32[2,16,16,128]{3,2,1,0:T(8,128)S(1)}, u32[]{:S(2)}, u32[]{:S(2)}) %collective-permute-start.1) | collective-permute-done | bytes 262176 | tf_op jit(solution)/shard_map/ppermute | solution.py:494
  8.4 0.0 collective-permute-done.near_cast
  8.4 0.3 shard_map.52
  8.7 1.7 %collective-permute-start.2 = (f32[2,2,32,128]{3,2,1,0:T(8,128)S(1)}, f32[2,2,32,128]{3,2,1,0:T(8,128)S(1)}, u32[]{:S(2)}, u32[]{:S(2)}) collective-permute-start(f32[2,2,32,128]{3,2,1,0:T(8,128)S(1)} %get-tuple-element.38), channel_id=1, source_target_pairs={{0,1},{1,0},{2,3},{3,2},{4,5},{5,4},{6,7},{7,6},{8,9},{9,8},{10,11... | collective-permute-start | bytes 196616 | tf_op jit(solution)/shard_map/ppermute | solution.py:494
  10.4 7.2 %collective-permute-start.3 = (f32[2,2,32,128]{3,2,1,0:T(8,128)S(1)}, f32[2,2,32,128]{3,2,1,0:T(8,128)S(1)}, u32[]{:S(2)}, u32[]{:S(2)}) collective-permute-start(f32[2,2,32,128]{3,2,1,0:T(8,128)S(1)} %get-tuple-element.39), channel_id=1, source_target_pairs={{0,31},{1,2},{2,1},{3,4},{4,3},{5,6},{6,5},{7,8},{8,7},{9,10},{10,... | collective-permute-start | bytes 196616 | tf_op jit(solution)/shard_map/ppermute | solution.py:494
  17.6 1.7 %shard_map.53 = (f32[16,24,128]{2,1,0:T(8,128)S(1)}, f32[16,24,128]{2,1,0:T(8,128)S(1)}, f32[16,24,128]{2,1,0:T(8,128)S(1)}, f32[16,24,128]{2,1,0:T(8,128)S(1)},...) custom-call(f32[2,16,16,128]{3,2,1,0:T(8,128)S(1)} %shard_map.50.own, ...), custom_call_target="tpu_custom_call" | custom-call | tf_op jit(solution)/shard_map/pallas_call | solution.py:518
  19.3 0.0 collective-permute-done.2.near_span
  19.3 0.0 collective-permute-done.3.far_span
  19.3 1.3 %shard_map.54 = f32[8,8,128]{2,1,0:T(8,128)S(1)} custom-call(f32[2,2,32,128]{3,2,1,0:T(8,128)S(1)} %collective-permute-done.2.near_span, f32[2,2,32,128]{3,2,1,0:T(8,128)S(1)} %collective-permute-done.3.far_span, f32[2,8,48,128]{3,2,1,0:T(8,128)S(1)} %get-tuple-element.41.inner, f32[16,24,128]{2,1,0:T(8,128)S(1)} %get-tuple-element.42.merged, ...), custom_call_target="tpu_custom_call" | custom-call | tf_op jit(solution)/shard_map/pallas_call | solution.py:524
  20.6 10.6 %all_to_all.5.own = f32[8,8,128]{2,1,0:T(8,128)S(1)} all-to-all(f32[8,8,128]{2,1,0:T(8,128)S(1)} %shard_map.54), channel_id=1, replica_groups=mesh['cast'=8,'span'=32] {'cast'}, dimensions={0} | all-to-all | bytes 65536 | tf_op jit(solution)/shard_map/all_to_all | solution.py:531
  31.2 0.0 collective-permute-start.5
  31.2 4.9 %collective-permute-start.4 = (f32[8,8,128]{2,1,0:T(8,128)S(1)}, f32[8,8,128]{2,1,0:T(8,128)S(1)}, u32[]{:S(2)}, u32[]{:S(2)}) collective-permute-start(f32[8,8,128]{2,1,0:T(8,128)S(1)} %all_to_all.5.own), channel_id=1, source_target_pairs={{0,31},{1,2},{2,1},{3,4},{4,3},{5,6},{6,5},{7,8},{8,7},{9,10},{10,... | collective-permute-start | bytes 98312 | tf_op jit(solution)/shard_map/ppermute | solution.py:494
  36.2 1.1 %shard_map.55 = (f32[8,24,128]{2,1,0:T(8,128)S(1)}, f32[8,24,128]{2,1,0:T(8,128)S(1)}, f32[8,24,128]{2,1,0:T(8,128)S(1)}, f32[8,24,128]{2,1,0:T(8,128)S(1)}, f32...) custom-call(f32[2,2,32,128]{3,2,1,0:T(8,128)S(1)} %collective-permut, ...), custom_call_target="tpu_custom_call" | custom-call | tf_op jit(solution)/shard_map/pallas_call | solution.py:527
  37.3 0.0 collective-permute-done.5.near_column
  37.3 0.2 collective-permute-done.4.far_column
  37.5 3.8 %shard_map.56 = (f32[16,16,128]{2,1,0:T(8,128)}, f32[16,16,128]{2,1,0:T(8,128)}) custom-call(f32[8,8,128]{2,1,0:T(8,128)S(1)} %all_to_all.5.own, f32[8,8,128]{2,1,0:T(8,128)S(1)} %collective-permute-done.4.far_column, f32[8,8,128]{2,1,0:T(8,128)S(1)} %collective-permute-done.5.near_column, bf16[128,128]{1,0:T(8,128)(2,1)S(1)} %get-tuple-element.45.narrow, ...), custom_call_target="tpu_custom_call" | custom-call | tf_op jit(solution)/shard_map/pallas_call | solution.py:548
Async XLA Ops:
  1.6 6.7 %collective-permute-start.1 = (f32[2,16,16,128]{3,2,1,0:T(8,128)S(1)}, f32[2,16,16,128]{3,2,1,0:T(8,128)S(1)}, u32[]{:S(2)}, u32[]{:S(2)}) collective-permute-start(f32[2,16,16,128]{3,2,1,0:T(8,128)S(1)} %shard_map.50.own), channel_id=1, source_target_pairs={{0,224},{32,64},{64,32},{96,128},{128,96},{160,192},{192,160},{224... | collective-permute-start | bytes 786440 | tf_op jit(solution)/shard_map/ppermute | solution.py:494
  4.3 4.1 %collective-permute-start = (f32[2,16,16,128]{3,2,1,0:T(8,128)S(1)}, f32[2,16,16,128]{3,2,1,0:T(8,128)S(1)}, u32[]{:S(2)}, u32[]{:S(2)}) collective-permute-start(f32[2,16,16,128]{3,2,1,0:T(8,128)S(1)} %shard_map.50.own), channel_id=1, source_target_pairs={{0,32},{32,0},{64,96},{96,64},{128,160},{160,128},{192,224},{224,1... | collective-permute-start | bytes 786440 | tf_op jit(solution)/shard_map/ppermute | solution.py:494
  8.7 10.6 %collective-permute-start.2 = (f32[2,2,32,128]{3,2,1,0:T(8,128)S(1)}, f32[2,2,32,128]{3,2,1,0:T(8,128)S(1)}, u32[]{:S(2)}, u32[]{:S(2)}) collective-permute-start(f32[2,2,32,128]{3,2,1,0:T(8,128)S(1)} %get-tuple-element.38), channel_id=1, source_target_pairs={{0,1},{1,0},{2,3},{3,2},{4,5},{5,4},{6,7},{7,6},{8,9},{9,8},{10,11... | collective-permute-start | bytes 196616 | tf_op jit(solution)/shard_map/ppermute | solution.py:494
  10.4 8.9 %collective-permute-start.3 = (f32[2,2,32,128]{3,2,1,0:T(8,128)S(1)}, f32[2,2,32,128]{3,2,1,0:T(8,128)S(1)}, u32[]{:S(2)}, u32[]{:S(2)}) collective-permute-start(f32[2,2,32,128]{3,2,1,0:T(8,128)S(1)} %get-tuple-element.39), channel_id=1, source_target_pairs={{0,31},{1,2},{2,1},{3,4},{4,3},{5,6},{6,5},{7,8},{8,7},{9,10},{10,... | collective-permute-start | bytes 196616 | tf_op jit(solution)/shard_map/ppermute | solution.py:494
  31.2 6.1 %collective-permute-start.5 = (f32[8,8,128]{2,1,0:T(8,128)S(1)}, f32[8,8,128]{2,1,0:T(8,128)S(1)}, u32[]{:S(2)}, u32[]{:S(2)}) collective-permute-start(f32[8,8,128]{2,1,0:T(8,128)S(1)} %all_to_all.5.own), channel_id=1, source_target_pairs={{0,1},{1,0},{2,3},{3,2},{4,5},{5,4},{6,7},{7,6},{8,9},{9,8},{10,11... | collective-permute-start | bytes 98312 | tf_op jit(solution)/shard_map/ppermute | solution.py:494
  31.2 6.2 %collective-permute-start.4 = (f32[8,8,128]{2,1,0:T(8,128)S(1)}, f32[8,8,128]{2,1,0:T(8,128)S(1)}, u32[]{:S(2)}, u32[]{:S(2)}) collective-permute-start(f32[8,8,128]{2,1,0:T(8,128)S(1)} %all_to_all.5.own), channel_id=1, source_target_pairs={{0,31},{1,2},{2,1},{3,4},{4,3},{5,6},{6,5},{7,8},{8,7},{9,10},{10,... | collective-permute-start | bytes 98312 | tf_op jit(solution)/shard_map/ppermute | solution.py:494

commit v6 on v5

--- a/solution.py
+++ b/solution.py
@@ -8,9 +8,9 @@
 HZ, BC, BS = 16, 16, 128
 HALO = 16
 ROWS = BC + 2 * HALO
-CUT = slice(HALO - 4, HALO + BC + 4)
+HALF = ROWS // 2
 KEPT = BC + 8
-HALF = ROWS // 2
+KEPT1 = HALF - 8
 SENT = BC + 16
 PACK = HZ // 2
 SWEEPS_COARSE = 8
@@ -119,28 +119,39 @@
     return Level(cast, span, height, diag, relax, source, depth, packed)
 
 
+def kept_rows(value):
+    edge = jnp.where(iota((8, BS), 0) < 4, value[HALO + BC : HALO + BC + 8], value[HALO - 8 : HALO])
+    return jnp.concatenate([value[HALO : HALO + BC], edge], axis=0)
+
+
+def kept_rows1(value):
+    return jnp.concatenate([value[8:16], jnp.where(iota((8, BS), 0) < 4, value[16:], value[:8])], axis=0)
+
+
 def keep(level, x, refs):
     for ref, values in zip(refs, (x, level.source, level.cast, level.span, level.height, level.diag, level.relax)):
         for z, value in enumerate(values):
-            ref[z] = value[CUT]
+            ref[z] = kept_rows(value)
 
 
 def coarse_parts(visc, remains, scratch):
     parts = []
     count = len(visc) // 2
+    half = visc[0].shape[0] // 2
     for a, values in enumerate(([1.0 / v for v in visc], remains)):
         for k in range(count):
             scratch[a * count + k] = values[2 * k] + values[2 * k + 1]
             ref = scratch.at[a * count + k]
-            parts.append(ref[pl.ds(0, HALF, stride=2), :] + ref[pl.ds(1, HALF, stride=2), :])
+            parts.append(ref[pl.ds(0, half, stride=2), :] + ref[pl.ds(1, half, stride=2), :])
     return jnp.concatenate(parts, axis=0)
 
 
 def ends(value, first, last, edge):
     rows = value.shape[0]
-    low = jnp.where(first, jnp.broadcast_to(value[edge : edge + 1], (edge, BS)), value[:edge])
-    high = jnp.where(last, jnp.broadcast_to(value[rows - edge - 1 : rows - edge], (edge, BS)), value[rows - edge :])
-    return jnp.concatenate([low, value[edge : rows - edge], high], axis=0)
+    row = iota((rows, BS), 0)
+    value = jnp.where(first & (row < edge), jnp.broadcast_to(value[edge : edge + 1], (rows, BS)), value)
+    stop = rows - edge
+    return jnp.where(last & (row >= stop), jnp.broadcast_to(value[stop - 1 : stop], (rows, BS)), value)
 
 
 def beyond(rows, edge):
@@ -269,7 +280,7 @@
     return jnp.concatenate([shift(sent[:8], step + more, 1), moved, shift(sent[-8:], step + more, 1)], axis=0)
 
 
-def own_kernel(own, near_cast, far_cast, own_merge, x, b, cast, span, height, diag, relax, merged, inner, scratch):
+def own_kernel(own, near_cast, far_cast, own_merge, x, b, cast, span, height, diag, relax, merged, merged_mid, inner, scratch):
     first, last, outside = beyond(ROWS, HALO)
     visc, source = [], []
     for z in range(HZ):
@@ -292,20 +303,26 @@
     total = product(parts, own_merge[...])
     for k in range(HZ):
         merged[k] = total[HALF * k : HALF * (k + 1)]
-
-
-def edge_levels(near_span, far_span, inner, merged, edge_merge, scratch):
-    first, last, outside = beyond(ROWS, HALO)
-    lane = iota((ROWS, BS), 1) % 64
+        merged_mid[k] = total[HALF * k + 4 : HALF * (k + 1) - 4]
+
+
+def edge_levels(near_span, far_span, inner, merged, edge_merge, scratch, halo):
+    rows = BC + 2 * halo
+    first, last, outside = beyond(rows, halo)
+    lane = iota((rows, BS), 1) % 64
     fields = []
     for a in range(2):
         slabs = []
         for k in range(PACK):
             group, sub = divmod(k, 4)
             left, right = by_side("span", near_span[a, group], far_span[a, group])
-            l, r = spread_rows(left, -16 * sub, 12), spread_rows(right, 48 - 16 * sub, -12)
-            value = jnp.where(lane < 16, l, jnp.where(lane >= 48, r, inner[a, k]))
-            slabs.append(ends(value, first, last, HALO) if a == 0 else value)
+            if halo == HALO:
+                l, r = spread_rows(left, -16 * sub, 12), spread_rows(right, 48 - 16 * sub, -12)
+            else:
+                l, r = shift(left, -16 * sub, 1), shift(right, 48 - 16 * sub, 1)
+            own = inner[a, k, HALO - halo : HALO + BC + halo]
+            value = jnp.where(lane < 16, l, jnp.where(lane >= 48, r, own))
+            slabs.append(ends(value, first, last, halo) if a == 0 else value)
         fields.append(slabs)
     visc, source = fields
     level = fine_level(visc, source, outside, True)
@@ -314,16 +331,16 @@
     parts = coarse_parts(visc, level.residual(values), scratch)
     total = product(parts, edge_merge[...])
 
-    edge = HALO // 2
-    first, last, outside = beyond(HALF, edge)
+    edge, half = halo // 2, rows // 2
+    first, last, outside = beyond(half, edge)
     weight = jnp.where(outside, 0.0, WEIGHT)
     coarse = []
     for k in range(HZ):
         a, z = divmod(k, 8)
         side, pos = divmod(z, 4)
-        row = HALF * (4 * a + pos)
-        coarse.append(merged[k] + total[row : row + HALF, BS * side : BS * (side + 1)])
-    lane = iota((HALF, BS), 1)
+        row = half * (4 * a + pos)
+        coarse.append(merged[k] + total[row : row + half, BS * side : BS * (side + 1)])
+    lane = iota((half, BS), 1)
     known = (lane < 72) | (lane >= 120)
     coeff = [jnp.where(known, 0.125 * ends(c, first, last, edge), 1.0) for c in coarse[:8]]
     source = [0.5 * c for c in coarse[8:]]
@@ -339,18 +356,18 @@
     near_span, far_span, inner, merged, edge_merge, x, b, cast, span, height, diag, relax,
     x1, b1, cast1, span1, height1, relax1, scratch,
 ):
-    fine, (level, values, _) = edge_levels(near_span, far_span, inner, merged, edge_merge, scratch)
+    fine, (level, values, _) = edge_levels(near_span, far_span, inner, merged, edge_merge, scratch, HALO)
     keep(*fine, (x, b, cast, span, height, diag, relax))
     kept = (x1, values), (b1, level.source), (cast1, level.cast), (span1, level.span), (height1, level.height), (relax1, level.relax)
     for ref, items in kept:
         for z, item in enumerate(items):
-            ref[z] = item
+            ref[z] = kept_rows1(item)
 
 
 def edge_kernel(near_span, far_span, inner, merged, edge_merge, move, slots, scratch, rows8):
-    _, (level, values, coeff) = edge_levels(near_span, far_span, inner, merged, edge_merge, scratch)
+    _, (level, values, coeff) = edge_levels(near_span, far_span, inner, merged, edge_merge, scratch, 8)
     remains = level.residual(values)
-    edge = HALO // 2
+    edge = 4
 
     fields = []
     for k in range(4):
@@ -420,32 +437,39 @@
         padded2[z, 0:8] = jnp.zeros((8, 128), F32)
         padded2[z, 8 : 8 + rows] = x2[z]
         padded2[z, 8 + rows : 16 + rows] = jnp.zeros((8, 128), F32)
-    local = [padded2[z, pl.ds(4 * index + 4, 16), :] for z in range(4)]
+    local = [shift(padded2[z, pl.ds(4 * index + 6, 8), :], -2, 0) for z in range(4)]
     spread = product(jnp.concatenate(local, axis=0), grow[...])
     for z in range(4):
-        wide1[z, pl.ds(0, 16, stride=2), :] = spread[16 * z : 16 * z + 16]
-        wide1[z, pl.ds(1, 16, stride=2), :] = spread[16 * z : 16 * z + 16]
+        for s in range(2):
+            wide1[z, pl.ds(s, 8, stride=2), :] = spread[8 * z : 8 * z + 8]
     level1 = Level(cast1, span1, height1, None, relax1, b1, 8)
-    x = [x1[z] + wide1[z // 2, 0:HALF] for z in range(8)]
+    x = [x1[z] + wide1[z // 2] for z in range(8)]
     x = level1.sweep(level1.sweep(x))
 
     spread = product(jnp.concatenate(x, axis=0), double[...])
     for z in range(8):
         for s in range(2):
-            wide_own[z, pl.ds(s, HALF, stride=2), :] = spread[HALF * z : HALF * (z + 1)]
+            wide_own[z, pl.ds(s, KEPT1, stride=2), :] = spread[KEPT1 * z : KEPT1 * (z + 1)]
     sides = [jnp.concatenate([x[k], x[k + 4]], axis=1) for k in range(4)]
     spread = product(jnp.concatenate(sides, axis=0), expand[...])
     for k in range(4):
         for s in range(2):
-            wide_edge[k, pl.ds(s, HALF, stride=2), :] = spread[HALF * k : HALF * (k + 1)]
+            wide_edge[k, pl.ds(s, KEPT1, stride=2), :] = spread[KEPT1 * k : KEPT1 * (k + 1)]
     level_own = Level(casto, spano, heighto, diago, relaxo, bo, HZ)
     level_edge = Level(caste, spane, heighte, diage, relaxe, be, PACK, True)
-    own_x = [xo[z] + wide_own[z // 2, CUT] for z in range(HZ)]
-    edge_x = [xe[k] + wide_edge[k // 2, CUT] for k in range(PACK)]
+
+    def refined(wide, k):
+        edge = jnp.where(iota((8, BS), 0) < 4, wide[k, BC : BC + 8], wide[k, BC + 8 :])
+        return jnp.concatenate([wide[k, :BC], edge], axis=0)
+
+    own_wide = [refined(wide_own, k) for k in range(8)]
+    edge_wide = [refined(wide_edge, k) for k in range(4)]
+    own_x = [xo[z] + own_wide[z // 2] for z in range(HZ)]
+    edge_x = [xe[k] + edge_wide[k // 2] for k in range(PACK)]
     edge_x = level_edge.sweep(level_edge.sweep(edge_x))
     own_x = level_own.sweep(level_own.sweep(own_x))
     lane = iota((BC, BS), 1)
-    rows = slice(4, 4 + BC)
+    rows = slice(0, BC)
 
     copies = []
 
@@ -499,7 +523,7 @@
     packed = (2, 2, SENT, BS)
     own_state = [(HZ, KEPT, BS)] * 4 + [(HZ + 1, KEPT, BS)] + [(HZ, KEPT, BS)] * 2
     edge_state = [(PACK, KEPT, BS)] * 4 + [(PACK + 1, KEPT, BS)] + [(PACK, KEPT, BS)] * 2
-    level1_state = [(8, HALF, BS)] * 4 + [(9, HALF, BS), (8, HALF, BS)]
+    level1_state = [(8, KEPT1, BS)] * 4 + [(9, KEPT1, BS), (8, KEPT1, BS)]
 
     arguments = (pltpu.with_memory_space_constraint(a, pltpu.HBM) for a in (viscosity_table, phase, pressure_source))
     stage_scratch = [pltpu.SMEM((3,), F32), pltpu.VMEM((HZ, BC, BS), jnp.int32), pltpu.SemaphoreType.DMA((3,))]
@@ -515,15 +539,15 @@
     near_span, far_span = call(margin_kernel, [VMEM] * 4, [packed, packed])(near_own, far_own, near_cast, far_cast)
     near_span = swap(near_span, "span", False)
     far_span = swap(far_span, "span", True)
-    *kept_own, merged, inner = call(
+    *kept_own, merged, merged_mid, inner = call(
         own_kernel,
         [VMEM] * 4,
-        own_state + [(HZ, HALF, BS), (2, PACK, ROWS, BS)],
+        own_state + [(HZ, HALF, BS), (HZ, HALF - 8, BS), (2, PACK, ROWS, BS)],
         [(HZ, ROWS, BS)],
     )(own, near_cast, far_cast, own_merge)
     (slots,) = call(
-        edge_kernel, [VMEM] * 6, [(count, 8, BS)], [(8, ROWS, BS), (4, 16, BS)]
-    )(near_span, far_span, inner, merged, edge_merge, move)
+        edge_kernel, [VMEM] * 6, [(count, 8, BS)], [(8, SENT, BS), (4, 16, BS)]
+    )(near_span, far_span, inner, merged_mid, edge_merge, move)
     kept_edge = call(state_kernel, [VMEM] * 5, edge_state + level1_state, [(8, ROWS, BS)])(
         near_span, far_span, inner, merged, edge_merge
     )
@@ -537,9 +561,9 @@
         (rows, BS),
         (2, rows, BS),
         (4, rows + 16, BS),
-        (4, 32, BS),
-        (8, ROWS, BS),
-        (4, ROWS, BS),
+        (4, KEPT1, BS),
+        (8, 2 * KEPT1, BS),
+        (4, 2 * KEPT1, BS),
         (2, HZ, BC, BS),
         pltpu.SemaphoreType.DMA((2, 4)),
     ]

time: 41.4 us -> 41.3 us (level)
  no operation moved by 1% of the time
where the time goes in v6:
time: 41.3 us; the launch traced here: 41.1 us
  starting transfers between devices  17.6 us (43%)
  blocking collectives  10.6 us (26%)
  Pallas kernels  9.3 us (23%)
  waiting for transfers between devices  2.91 us (7%)
  between operations  0.68 us (2%)
    ppermute x6, starting transfers between devices, swap(): return lax.ppermute(value, axis, list(enumerate(partner)))  17.6 us
    all_to_all x1, blocking collectives, shards(): column = lax.all_to_all(slots, 'cast', 0, 0)  10.6 us
    pallas_call x1, Pallas kernels, shards(): call(ascent_kernel, [VMEM] * (3 + len(state)), [(HZ, BC, BS)] * 2, scratc...  3.67 us
    ppermute x6, waiting for transfers between devices, swap(): return lax.ppermute(value, axis, list(enumerate(partner)))  2.91 us
    pallas_call x1, Pallas kernels, shards(): call(own_kernel, [VMEM] * 4, own_state + [(HZ, HALF, BS), (HZ, HALF - 8,...  1.68 us
    pallas_call x1, Pallas kernels, shards(): call(edge_kernel, [VMEM] * 6, [(count, 8, BS)], [(8, SENT, BS), (4, 16, B...  1.28 us
    pallas_call x1, Pallas kernels, shards(): call(state_kernel, [VMEM] * 5, edge_state + level1_state, [(8, ROWS, BS)])  1.11 us
    pallas_call x1, Pallas kernels, shards(): call(stage_kernel, [HBM] * 3, [(2, HZ, BC, BS)], stage_scratch)(*arguments)  1 us
  transfers between devices with their start and end apart: 6, of which 2 were waited for; matrix products, arithmetic and copies ran while one was open for 0% of the time, Pallas kernels for 7%

profile of v6, /device:TPU:1, one launch (start us, length us, event | category | flops | bytes accessed | tf_op | source)
XLA Modules:
  0.0 41.1 jit_solution(17585162923288240328)
XLA Ops:
  0.6 1.0 %shard_map.50.own = f32[2,16,16,128]{3,2,1,0:T(8,128)S(1)} custom-call(f32[3]{0:T(128)} %table_in.1, s32[16,16,128]{2,1,0:T(8,128)} %phase_in.1, f32[16,16,128]{2,1,0:T(8,128)} %source_in.1), custom_call_target="tpu_custom_call" | custom-call | tf_op jit(solution)/shard_map/pallas_call | solution.py:530
  1.6 2.7 %collective-permute-start.1 = (f32[2,16,16,128]{3,2,1,0:T(8,128)S(1)}, f32[2,16,16,128]{3,2,1,0:T(8,128)S(1)}, u32[]{:S(2)}, u32[]{:S(2)}) collective-permute-start(f32[2,16,16,128]{3,2,1,0:T(8,128)S(1)} %shard_map.50.own), channel_id=1, source_target_pairs={{0,224},{32,64},{64,32},{96,128},{128,96},{160,192},{192,160},{224... | collective-permute-start | bytes 786440 | tf_op jit(solution)/shard_map/ppermute | solution.py:518
  4.3 1.1 %collective-permute-start = (f32[2,16,16,128]{3,2,1,0:T(8,128)S(1)}, f32[2,16,16,128]{3,2,1,0:T(8,128)S(1)}, u32[]{:S(2)}, u32[]{:S(2)}) collective-permute-start(f32[2,16,16,128]{3,2,1,0:T(8,128)S(1)} %shard_map.50.own), channel_id=1, source_target_pairs={{0,32},{32,0},{64,96},{96,64},{128,160},{160,128},{192,224},{224,1... | collective-permute-start | bytes 786440 | tf_op jit(solution)/shard_map/ppermute | solution.py:518
  5.4 0.2 shard_map.51
  5.7 2.7 %collective-permute-done.1.far_cast = f32[2,16,16,128]{3,2,1,0:T(8,128)S(1)} collective-permute-done((f32[2,16,16,128]{3,2,1,0:T(8,128)S(1)}, f32[2,16,16,128]{3,2,1,0:T(8,128)S(1)}, u32[]{:S(2)}, u32[]{:S(2)}) %collective-permute-start.1) | collective-permute-done | bytes 262176 | tf_op jit(solution)/shard_map/ppermute | solution.py:518
  8.4 0.0 collective-permute-done.near_cast
  8.4 0.3 shard_map.52
  8.7 1.7 %collective-permute-start.2 = (f32[2,2,32,128]{3,2,1,0:T(8,128)S(1)}, f32[2,2,32,128]{3,2,1,0:T(8,128)S(1)}, u32[]{:S(2)}, u32[]{:S(2)}) collective-permute-start(f32[2,2,32,128]{3,2,1,0:T(8,128)S(1)} %get-tuple-element.39), channel_id=1, source_target_pairs={{0,1},{1,0},{2,3},{3,2},{4,5},{5,4},{6,7},{7,6},{8,9},{9,8},{10,11... | collective-permute-start | bytes 196616 | tf_op jit(solution)/shard_map/ppermute | solution.py:518
  10.4 7.2 %collective-permute-start.3 = (f32[2,2,32,128]{3,2,1,0:T(8,128)S(1)}, f32[2,2,32,128]{3,2,1,0:T(8,128)S(1)}, u32[]{:S(2)}, u32[]{:S(2)}) collective-permute-start(f32[2,2,32,128]{3,2,1,0:T(8,128)S(1)} %get-tuple-element.40), channel_id=1, source_target_pairs={{0,31},{1,2},{2,1},{3,4},{4,3},{5,6},{6,5},{7,8},{8,7},{9,10},{10,... | collective-permute-start | bytes 196616 | tf_op jit(solution)/shard_map/ppermute | solution.py:518
  17.6 1.7 %shard_map.53 = (f32[16,24,128]{2,1,0:T(8,128)S(1)}, f32[16,24,128]{2,1,0:T(8,128)S(1)}, f32[16,24,128]{2,1,0:T(8,128)S(1)}, f32[16,24,128]{2,1,0:T(8,128)S(1)},...) custom-call(f32[2,16,16,128]{3,2,1,0:T(8,128)S(1)} %shard_map.50.own, ...), custom_call_target="tpu_custom_call" | custom-call | tf_op jit(solution)/shard_map/pallas_call | solution.py:542
  19.3 0.0 collective-permute-done.2.near_span
  19.3 0.0 collective-permute-done.3.far_span
  19.3 1.3 %shard_map.54 = f32[8,8,128]{2,1,0:T(8,128)S(1)} custom-call(f32[2,2,32,128]{3,2,1,0:T(8,128)S(1)} %collective-permute-done.2.near_span, f32[2,2,32,128]{3,2,1,0:T(8,128)S(1)} %collective-permute-done.3.far_span, f32[2,8,48,128]{3,2,1,0:T(8,128)S(1)} %get-tuple-element.42.inner, f32[16,16,128]{2,1,0:T(8,128)S(1)} %get-tuple-element.43.merged, ...), custom_call_target="tpu_custom_call" | custom-call | tf_op jit(solution)/shard_map/pallas_call | solution.py:548
  20.6 10.6 %all_to_all.5.own = f32[8,8,128]{2,1,0:T(8,128)S(1)} all-to-all(f32[8,8,128]{2,1,0:T(8,128)S(1)} %shard_map.54), channel_id=1, replica_groups=mesh['cast'=8,'span'=32] {'cast'}, dimensions={0} | all-to-all | bytes 65536 | tf_op jit(solution)/shard_map/all_to_all | solution.py:555
  31.2 0.0 collective-permute-start.5
  31.2 4.9 %collective-permute-start.4 = (f32[8,8,128]{2,1,0:T(8,128)S(1)}, f32[8,8,128]{2,1,0:T(8,128)S(1)}, u32[]{:S(2)}, u32[]{:S(2)}) collective-permute-start(f32[8,8,128]{2,1,0:T(8,128)S(1)} %all_to_all.5.own), channel_id=1, source_target_pairs={{0,31},{1,2},{2,1},{3,4},{4,3},{5,6},{6,5},{7,8},{8,7},{9,10},{10,... | collective-permute-start | bytes 98312 | tf_op jit(solution)/shard_map/ppermute | solution.py:518
  36.1 1.1 %shard_map.55 = (f32[8,24,128]{2,1,0:T(8,128)S(1)}, f32[8,24,128]{2,1,0:T(8,128)S(1)}, f32[8,24,128]{2,1,0:T(8,128)S(1)}, f32[8,24,128]{2,1,0:T(8,128)S(1)}, f32...) custom-call(f32[2,2,32,128]{3,2,1,0:T(8,128)S(1)} %collective-permut, ...), custom_call_target="tpu_custom_call" | custom-call | tf_op jit(solution)/shard_map/pallas_call | solution.py:551
  37.3 0.0 collective-permute-done.5.near_column
  37.3 0.2 collective-permute-done.4.far_column
  37.4 3.7 %shard_map.56 = (f32[16,16,128]{2,1,0:T(8,128)}, f32[16,16,128]{2,1,0:T(8,128)}) custom-call(f32[8,8,128]{2,1,0:T(8,128)S(1)} %all_to_all.5.own, f32[8,8,128]{2,1,0:T(8,128)S(1)} %collective-permute-done.4.far_column, f32[8,8,128]{2,1,0:T(8,128)S(1)} %collective-permute-done.5.near_column, bf16[128,128]{1,0:T(8,128)(2,1)S(1)} %get-tuple-element.46.narrow, ...), custom_call_target="tpu_custom_call" | custom-call | tf_op jit(solution)/shard_map/pallas_call | solution.py:572
Async XLA Ops:
  1.6 6.7 %collective-permute-start.1 = (f32[2,16,16,128]{3,2,1,0:T(8,128)S(1)}, f32[2,16,16,128]{3,2,1,0:T(8,128)S(1)}, u32[]{:S(2)}, u32[]{:S(2)}) collective-permute-start(f32[2,16,16,128]{3,2,1,0:T(8,128)S(1)} %shard_map.50.own), channel_id=1, source_target_pairs={{0,224},{32,64},{64,32},{96,128},{128,96},{160,192},{192,160},{224... | collective-permute-start | bytes 786440 | tf_op jit(solution)/shard_map/ppermute | solution.py:518
  4.3 4.1 %collective-permute-start = (f32[2,16,16,128]{3,2,1,0:T(8,128)S(1)}, f32[2,16,16,128]{3,2,1,0:T(8,128)S(1)}, u32[]{:S(2)}, u32[]{:S(2)}) collective-permute-start(f32[2,16,16,128]{3,2,1,0:T(8,128)S(1)} %shard_map.50.own), channel_id=1, source_target_pairs={{0,32},{32,0},{64,96},{96,64},{128,160},{160,128},{192,224},{224,1... | collective-permute-start | bytes 786440 | tf_op jit(solution)/shard_map/ppermute | solution.py:518
  8.7 10.6 %collective-permute-start.2 = (f32[2,2,32,128]{3,2,1,0:T(8,128)S(1)}, f32[2,2,32,128]{3,2,1,0:T(8,128)S(1)}, u32[]{:S(2)}, u32[]{:S(2)}) collective-permute-start(f32[2,2,32,128]{3,2,1,0:T(8,128)S(1)} %get-tuple-element.39), channel_id=1, source_target_pairs={{0,1},{1,0},{2,3},{3,2},{4,5},{5,4},{6,7},{7,6},{8,9},{9,8},{10,11... | collective-permute-start | bytes 196616 | tf_op jit(solution)/shard_map/ppermute | solution.py:518
  10.4 8.9 %collective-permute-start.3 = (f32[2,2,32,128]{3,2,1,0:T(8,128)S(1)}, f32[2,2,32,128]{3,2,1,0:T(8,128)S(1)}, u32[]{:S(2)}, u32[]{:S(2)}) collective-permute-start(f32[2,2,32,128]{3,2,1,0:T(8,128)S(1)} %get-tuple-element.40), channel_id=1, source_target_pairs={{0,31},{1,2},{2,1},{3,4},{4,3},{5,6},{6,5},{7,8},{8,7},{9,10},{10,... | collective-permute-start | bytes 196616 | tf_op jit(solution)/shard_map/ppermute | solution.py:518
  31.2 6.1 %collective-permute-start.5 = (f32[8,8,128]{2,1,0:T(8,128)S(1)}, f32[8,8,128]{2,1,0:T(8,128)S(1)}, u32[]{:S(2)}, u32[]{:S(2)}) collective-permute-start(f32[8,8,128]{2,1,0:T(8,128)S(1)} %all_to_all.5.own), channel_id=1, source_target_pairs={{0,1},{1,0},{2,3},{3,2},{4,5},{5,4},{6,7},{7,6},{8,9},{9,8},{10,11... | collective-permute-start | bytes 98312 | tf_op jit(solution)/shard_map/ppermute | solution.py:518
  31.2 6.2 %collective-permute-start.4 = (f32[8,8,128]{2,1,0:T(8,128)S(1)}, f32[8,8,128]{2,1,0:T(8,128)S(1)}, u32[]{:S(2)}, u32[]{:S(2)}) collective-permute-start(f32[8,8,128]{2,1,0:T(8,128)S(1)} %all_to_all.5.own), channel_id=1, source_target_pairs={{0,31},{1,2},{2,1},{3,4},{4,3},{5,6},{6,5},{7,8},{8,7},{9,10},{10,... | collective-permute-start | bytes 98312 | tf_op jit(solution)/shard_map/ppermute | solution.py:518

commit v7 on v6

--- a/solution.py
+++ b/solution.py
@@ -12,6 +12,9 @@
 KEPT = BC + 8
 KEPT1 = HALF - 8
 SENT = BC + 16
+REACH = (13, 12)
+BASE = (0, REACH[0] * HZ)
+CAST_ROWS = sum(REACH) * HZ
 PACK = HZ // 2
 SWEEPS_COARSE = 8
 WEIGHT = 0.8
@@ -20,6 +23,8 @@
 
 
 def shift(x, step, axis):
+    if step == 0:
+        return x
     return pltpu.roll(x, step % x.shape[axis], axis)
 
 
@@ -195,12 +200,37 @@
     return jnp.where(even, far_pair, near_pair), jnp.where(even, near_pair, far_pair)
 
 
-def extended(own, near_pair, far_pair, a, z):
-    before, after = by_side("cast", near_pair[a, z], far_pair[a, z])
+def beyond_rows(near_cast, far_cast, a, z):
+    reach, base = REACH[a], BASE[a]
+    start = base + reach * z
+
+    stop = base + reach * HZ
+    even = lax.rem(lax.axis_index("cast"), 2) == 0
+
+    def window(first, one, other):
+        at = min(max(first, base), stop - HALO)
+        rows = slice(at, at + HALO)
+        return shift(jnp.where(even, one[rows], other[rows]), at - first, 0)
+
+    return window(start - (HALO - reach), far_cast, near_cast), window(start, near_cast, far_cast)
+
+
+def extended(own, near_cast, far_cast, a, z):
+    before, after = beyond_rows(near_cast, far_cast, a, z)
     return jnp.concatenate([before, own[a, z], after], axis=0)
 
 
-def stage_kernel(table_in, phase_in, source_in, out, table, phase, sems):
+def stage_kernel(table_in, phase_in, source_in, out, far_out, near_out, table, phase, sems):
+    even = lax.rem(lax.axis_index("cast"), 2) == 0
+
+    def put(a, z, value):
+        reach = REACH[a]
+        first, last = value, shift(value, reach - HALO, 0)
+        rows = HALO if a == 0 or z < HZ - 1 else reach
+        place = slice(BASE[a] + reach * z, BASE[a] + reach * z + rows)
+        near_out[place] = jnp.where(even, last, first)[:rows]
+        far_out[place] = jnp.where(even, first, last)[:rows]
+
     copies = [
         pltpu.make_async_copy(table_in, table, sems.at[0]),
         pltpu.make_async_copy(phase_in, phase, sems.at[1]),
@@ -212,8 +242,12 @@
     copies[1].wait()
     for z in range(HZ):
         p = phase[z]
-        out[0, z] = jnp.where(p == 0, table[0], jnp.where(p == 1, table[1], table[2]))
+        value = jnp.where(p == 0, table[0], jnp.where(p == 1, table[1], table[2]))
+        out[0, z] = value
+        put(0, z, value)
     copies[2].wait()
+    for z in range(HZ):
+        put(1, z, out[1, z])
 
 
 def ones(where):
@@ -260,7 +294,7 @@
         for group in range(2):
             head = tail = None
             for start, z in places(group):
-                before, after = by_side("cast", near_cast[a, z], far_cast[a, z])
+                before, after = beyond_rows(near_cast, far_cast, a, z)
                 inner = jnp.concatenate([before[8:], after[:8]], axis=0)
                 far = jnp.concatenate([before[:8], after[8:]], axis=0)
                 h = jnp.where(seg >= 12, shift(far, start + 12, 1), shift(inner, start, 1))
@@ -527,9 +561,11 @@
 
     arguments = (pltpu.with_memory_space_constraint(a, pltpu.HBM) for a in (viscosity_table, phase, pressure_source))
     stage_scratch = [pltpu.SMEM((3,), F32), pltpu.VMEM((HZ, BC, BS), jnp.int32), pltpu.SemaphoreType.DMA((3,))]
-    (own,) = call(stage_kernel, [HBM] * 3, [(2, HZ, BC, BS)], stage_scratch)(*arguments)
-    far_cast = swap(own, "cast", True)
-    near_cast = swap(own, "cast", False)
+    own, far_cast, near_cast = call(
+        stage_kernel, [HBM] * 3, [(2, HZ, BC, BS), (CAST_ROWS, BS), (CAST_ROWS, BS)], stage_scratch
+    )(*arguments)
+    far_cast = swap(far_cast, "cast", True)
+    near_cast = swap(near_cast, "cast", False)
     square = (BS, BS)
     tables = [square, (BS, 2 * BS), (4 * BS, BS), square, square, square, square, (2 * BS, BS)]
     tables = [jax.ShapeDtypeStruct(t, BF16) for t in tables]

time: 41.3 us -> 40.7 us (0.985)
  waiting for transfers between devices: 2.91 us -> 5.43 us
  starting transfers between devices: 17.6 us -> 15.2 us
  blocking collectives: 10.6 us -> 9.88 us
    ppermute x6, waiting for transfers between devices: 2.91 us -> 5.43 us  [swap(): return lax.ppermute(value, axis, list(enumerate(partner)))]
    ppermute x6, starting transfers between devices: 17.6 us -> 15.2 us  [swap(): return lax.ppermute(value, axis, list(enumerate(partner)))]
    all_to_all x1, blocking collectives: 10.6 us -> 9.88 us  [shards(): column = lax.all_to_all(slots, 'cast', 0, 0)]
  transfers between devices with their start and end apart: 6 -> 6, of which waited for: 2 -> 3; matrix products, arithmetic and copies ran while one was open for 0% -> 0% of each run, Pallas kernels for 7% -> 7%
where the time goes in v7:
time: 40.7 us; the launch traced here: 40.5 us
  starting transfers between devices  15.2 us (37%)
  blocking collectives  9.88 us (24%)
  Pallas kernels  9.32 us (23%)
  waiting for transfers between devices  5.43 us (13%)
  between operations  0.69 us (2%)
    ppermute x6, starting transfers between devices, swap(): return lax.ppermute(value, axis, list(enumerate(partner)))  15.2 us
    all_to_all x1, blocking collectives, shards(): column = lax.all_to_all(slots, 'cast', 0, 0)  9.88 us
    ppermute x6, waiting for transfers between devices, swap(): return lax.ppermute(value, axis, list(enumerate(partner)))  5.43 us
    pallas_call x1, Pallas kernels, shards(): call(ascent_kernel, [VMEM] * (3 + len(state)), [(HZ, BC, BS)] * 2, scratc...  3.66 us
    pallas_call x1, Pallas kernels, shards(): call(own_kernel, [VMEM] * 4, own_state + [(HZ, HALF, BS), (HZ, HALF - 8,...  1.68 us
    pallas_call x1, Pallas kernels, shards(): call(edge_kernel, [VMEM] * 6, [(count, 8, BS)], [(8, SENT, BS), (4, 16, B...  1.28 us
    pallas_call x1, Pallas kernels, shards(): call(state_kernel, [VMEM] * 5, edge_state + level1_state, [(8, ROWS, BS)])  1.11 us
    pallas_call x1, Pallas kernels, shards(): call(stage_kernel, [HBM] * 3, [(2, HZ, BC, BS), (CAST_ROWS, BS), (CAST_RO...  1.02 us
  transfers between devices with their start and end apart: 6, of which 3 were waited for; matrix products, arithmetic and copies ran while one was open for 0% of the time, Pallas kernels for 7%

profile of v7, /device:TPU:1, one launch (start us, length us, event | category | flops | bytes accessed | tf_op | source)
XLA Modules:
  0.0 40.5 jit_solution(12422622543981988078)
XLA Ops:
  0.6 1.0 %shard_map.50 = (f32[2,16,16,128]{3,2,1,0:T(8,128)S(1)}, f32[400,128]{1,0:T(8,128)S(1)}, f32[400,128]{1,0:T(8,128)S(1)}) custom-call(f32[3]{0:T(128)} %table_in.1, s32[16,16,128]{2,1,0:T(8,128)} %phase_in.1, f32[16,16,128]{2,1,0:T(8,128)} %source_in.1), custom_call_target="tpu_custom_call" | custom-call | tf_op jit(solution)/shard_map/pallas_call | solution.py:564
  1.7 3.3 %collective-permute-start = (f32[400,128]{1,0:T(8,128)S(1)}, f32[400,128]{1,0:T(8,128)S(1)}, u32[]{:S(2)}, u32[]{:S(2)}) collective-permute-start(f32[400,128]{1,0:T(8,128)S(1)} %get-tuple-element.43), channel_id=1, source_target_pairs={{0,32},{32,0},{64,96},{96,64},{128,160},{160,128},{192,224},{224,1... | collective-permute-start | bytes 614408 | tf_op jit(solution)/shard_map/ppermute | solution.py:552
  5.0 0.0 collective-permute-start.1
  5.0 0.2 shard_map.51
  5.2 0.8 %collective-permute-done.near_cast = f32[400,128]{1,0:T(8,128)S(1)} collective-permute-done((f32[400,128]{1,0:T(8,128)S(1)}, f32[400,128]{1,0:T(8,128)S(1)}, u32[]{:S(2)}, u32[]{:S(2)}) %collective-permute-start) | collective-permute-done | bytes 204832 | tf_op jit(solution)/shard_map/ppermute | solution.py:552
  6.1 4.4 %collective-permute-done.1.far_cast = f32[400,128]{1,0:T(8,128)S(1)} collective-permute-done((f32[400,128]{1,0:T(8,128)S(1)}, f32[400,128]{1,0:T(8,128)S(1)}, u32[]{:S(2)}, u32[]{:S(2)}) %collective-permute-start.1) | collective-permute-done | bytes 204832 | tf_op jit(solution)/shard_map/ppermute | solution.py:552
  10.5 0.3 shard_map.52
  10.8 0.1 collective-permute-start.2
  10.9 6.7 %collective-permute-start.3 = (f32[2,2,32,128]{3,2,1,0:T(8,128)S(1)}, f32[2,2,32,128]{3,2,1,0:T(8,128)S(1)}, u32[]{:S(2)}, u32[]{:S(2)}) collective-permute-start(f32[2,2,32,128]{3,2,1,0:T(8,128)S(1)} %get-tuple-element.46), channel_id=1, source_target_pairs={{0,31},{1,2},{2,1},{3,4},{4,3},{5,6},{6,5},{7,8},{8,7},{9,10},{10,... | collective-permute-start | bytes 196616 | tf_op jit(solution)/shard_map/ppermute | solution.py:552
  17.6 1.7 %shard_map.53 = (f32[16,24,128]{2,1,0:T(8,128)S(1)}, f32[16,24,128]{2,1,0:T(8,128)S(1)}, f32[16,24,128]{2,1,0:T(8,128)S(1)}, f32[16,24,128]{2,1,0:T(8,128)S(1)},...) custom-call(f32[2,16,16,128]{3,2,1,0:T(8,128)S(1)} %get-tuple-elemen, ...), custom_call_target="tpu_custom_call" | custom-call | tf_op jit(solution)/shard_map/pallas_call | solution.py:578
  19.3 0.0 collective-permute-done.2.near_span
  19.3 0.0 collective-permute-done.3.far_span
  19.4 1.3 %shard_map.54 = f32[8,8,128]{2,1,0:T(8,128)S(1)} custom-call(f32[2,2,32,128]{3,2,1,0:T(8,128)S(1)} %collective-permute-done.2.near_span, f32[2,2,32,128]{3,2,1,0:T(8,128)S(1)} %collective-permute-done.3.far_span, f32[2,8,48,128]{3,2,1,0:T(8,128)S(1)} %get-tuple-element.48.inner, f32[16,16,128]{2,1,0:T(8,128)S(1)} %get-tuple-element.49.merged, ...), custom_call_target="tpu_custom_call" | custom-call | tf_op jit(solution)/shard_map/pallas_call | solution.py:584
  20.6 9.9 %all_to_all.5.own = f32[8,8,128]{2,1,0:T(8,128)S(1)} all-to-all(f32[8,8,128]{2,1,0:T(8,128)S(1)} %shard_map.54), channel_id=1, replica_groups=mesh['cast'=8,'span'=32] {'cast'}, dimensions={0} | all-to-all | bytes 65536 | tf_op jit(solution)/shard_map/all_to_all | solution.py:591
  30.5 0.0 collective-permute-start.5
  30.5 5.1 %collective-permute-start.4 = (f32[8,8,128]{2,1,0:T(8,128)S(1)}, f32[8,8,128]{2,1,0:T(8,128)S(1)}, u32[]{:S(2)}, u32[]{:S(2)}) collective-permute-start(f32[8,8,128]{2,1,0:T(8,128)S(1)} %all_to_all.5.own), channel_id=1, source_target_pairs={{0,31},{1,2},{2,1},{3,4},{4,3},{5,6},{6,5},{7,8},{8,7},{9,10},{10,... | collective-permute-start | bytes 98312 | tf_op jit(solution)/shard_map/ppermute | solution.py:552
  35.6 1.1 %shard_map.55 = (f32[8,24,128]{2,1,0:T(8,128)S(1)}, f32[8,24,128]{2,1,0:T(8,128)S(1)}, f32[8,24,128]{2,1,0:T(8,128)S(1)}, f32[8,24,128]{2,1,0:T(8,128)S(1)}, f32...) custom-call(f32[2,2,32,128]{3,2,1,0:T(8,128)S(1)} %collective-permut, ...), custom_call_target="tpu_custom_call" | custom-call | tf_op jit(solution)/shard_map/pallas_call | solution.py:587
  36.7 0.0 collective-permute-done.5.near_column
  36.7 0.2 collective-permute-done.4.far_column
  36.9 3.7 %shard_map.56 = (f32[16,16,128]{2,1,0:T(8,128)}, f32[16,16,128]{2,1,0:T(8,128)}) custom-call(f32[8,8,128]{2,1,0:T(8,128)S(1)} %all_to_all.5.own, f32[8,8,128]{2,1,0:T(8,128)S(1)} %collective-permute-done.4.far_column, f32[8,8,128]{2,1,0:T(8,128)S(1)} %collective-permute-done.5.near_column, bf16[128,128]{1,0:T(8,128)(2,1)S(1)} %get-tuple-element.52.narrow, ...), custom_call_target="tpu_custom_call" | custom-call | tf_op jit(solution)/shard_map/pallas_call | solution.py:608
Async XLA Ops:
  1.7 4.4 %collective-permute-start = (f32[400,128]{1,0:T(8,128)S(1)}, f32[400,128]{1,0:T(8,128)S(1)}, u32[]{:S(2)}, u32[]{:S(2)}) collective-permute-start(f32[400,128]{1,0:T(8,128)S(1)} %get-tuple-element.43), channel_id=1, source_target_pairs={{0,32},{32,0},{64,96},{96,64},{128,160},{160,128},{192,224},{224,1... | collective-permute-start | bytes 614408 | tf_op jit(solution)/shard_map/ppermute | solution.py:552
  5.0 5.5 %collective-permute-start.1 = (f32[400,128]{1,0:T(8,128)S(1)}, f32[400,128]{1,0:T(8,128)S(1)}, u32[]{:S(2)}, u32[]{:S(2)}) collective-permute-start(f32[400,128]{1,0:T(8,128)S(1)} %get-tuple-element.44), channel_id=1, source_target_pairs={{0,224},{32,64},{64,32},{96,128},{128,96},{160,192},{192,160},{224... | collective-permute-start | bytes 614408 | tf_op jit(solution)/shard_map/ppermute | solution.py:552
  10.8 8.5 %collective-permute-start.2 = (f32[2,2,32,128]{3,2,1,0:T(8,128)S(1)}, f32[2,2,32,128]{3,2,1,0:T(8,128)S(1)}, u32[]{:S(2)}, u32[]{:S(2)}) collective-permute-start(f32[2,2,32,128]{3,2,1,0:T(8,128)S(1)} %get-tuple-element.45), channel_id=1, source_target_pairs={{0,1},{1,0},{2,3},{3,2},{4,5},{5,4},{6,7},{7,6},{8,9},{9,8},{10,11... | collective-permute-start | bytes 196616 | tf_op jit(solution)/shard_map/ppermute | solution.py:552
  10.9 8.4 %collective-permute-start.3 = (f32[2,2,32,128]{3,2,1,0:T(8,128)S(1)}, f32[2,2,32,128]{3,2,1,0:T(8,128)S(1)}, u32[]{:S(2)}, u32[]{:S(2)}) collective-permute-start(f32[2,2,32,128]{3,2,1,0:T(8,128)S(1)} %get-tuple-element.46), channel_id=1, source_target_pairs={{0,31},{1,2},{2,1},{3,4},{4,3},{5,6},{6,5},{7,8},{8,7},{9,10},{10,... | collective-permute-start | bytes 196616 | tf_op jit(solution)/shard_map/ppermute | solution.py:552
  30.5 6.2 %collective-permute-start.5 = (f32[8,8,128]{2,1,0:T(8,128)S(1)}, f32[8,8,128]{2,1,0:T(8,128)S(1)}, u32[]{:S(2)}, u32[]{:S(2)}) collective-permute-start(f32[8,8,128]{2,1,0:T(8,128)S(1)} %all_to_all.5.own), channel_id=1, source_target_pairs={{0,1},{1,0},{2,3},{3,2},{4,5},{5,4},{6,7},{7,6},{8,9},{9,8},{10,11... | collective-permute-start | bytes 98312 | tf_op jit(solution)/shard_map/ppermute | solution.py:552
  30.5 6.4 %collective-permute-start.4 = (f32[8,8,128]{2,1,0:T(8,128)S(1)}, f32[8,8,128]{2,1,0:T(8,128)S(1)}, u32[]{:S(2)}, u32[]{:S(2)}) collective-permute-start(f32[8,8,128]{2,1,0:T(8,128)S(1)} %all_to_all.5.own), channel_id=1, source_target_pairs={{0,31},{1,2},{2,1},{3,4},{4,3},{5,6},{6,5},{7,8},{8,7},{9,10},{10,... | collective-permute-start | bytes 98312 | tf_op jit(solution)/shard_map/ppermute | solution.py:552

commit v8 on v7

--- a/solution.py
+++ b/solution.py
@@ -287,7 +287,7 @@
     return [(16 * sub + 64 * half, group * 4 + sub + 8 * half) for sub in range(4) for half in range(2)]
 
 
-def margin_kernel(near_own, far_own, near_cast, far_cast, near_span, far_span):
+def margin_kernel(near_own, far_own, far_cast, near_cast, near_span, far_span):
     lane = iota((16, BS), 1)
     seg = lane % HALO
     for a in range(2):
@@ -314,7 +314,7 @@
     return jnp.concatenate([shift(sent[:8], step + more, 1), moved, shift(sent[-8:], step + more, 1)], axis=0)
 
 
-def own_kernel(own, near_cast, far_cast, own_merge, x, b, cast, span, height, diag, relax, merged, merged_mid, inner, scratch):
+def own_kernel(own, far_cast, near_cast, own_merge, x, b, cast, span, height, diag, relax, merged, merged_mid, inner, scratch):
     first, last, outside = beyond(ROWS, HALO)
     visc, source = [], []
     for z in range(HZ):
@@ -424,7 +424,7 @@
 ):
     count = own.shape[0]
     rows = 4 * count
-    lane = iota((rows, 128), 1)
+    part_lane = iota((rows, 128), 1) // 32
     index = lax.axis_index("cast")
 
     fields = []
@@ -434,13 +434,11 @@
             left, right = by_side("span", near_column[d, rows_d], far_column[d, rows_d])
             for s, block in enumerate((own[d, rows_d], right, left)):
                 tiles[s, 4 * d : 4 * d + 4] = block
+        own_tile, right, left = tiles[0], shift(tiles[1], 32, 1), shift(tiles[2], -32, 1)
         slabs = []
         for z in range(4):
-            o = shift(tiles[0], -32 * z, 1)
-            r = shift(tiles[1], 32 - 32 * z, 1)
-            l = shift(tiles[2], 96 - 32 * z, 1)
-            fill = 1.0 if part == 0 else 0.0
-            slabs.append(jnp.where(lane < 32, o, jnp.where(lane < 64, r, jnp.where(lane >= 96, l, fill))))
+            both = jnp.where(part_lane == (z + 1) % 4, right, left)
+            slabs.append(shift(jnp.where(part_lane == z, own_tile, both), -32 * z, 1))
         fields.append(slabs)
     coeff2, source2 = fields
     level2 = whole_level(coeff2, source2)
@@ -507,23 +505,28 @@
 
     copies = []
 
+    beside = lane % 64 < 16
+
+    def joined(side):
+        return jnp.where(beside, shift(side[rows], -32, 1), side[rows])
+
     def give(number, out, z, mid, side):
-        half, k = divmod(z, PACK)
-        low = shift(side[rows], -16 - 64 * half, 1)
-        high = shift(side[rows], 80 - 64 * half, 1)
-        results[number, z] = jnp.where(lane < 8, low, jnp.where(lane >= 120, high, mid[rows]))
+        value = shift(side, -16 - 64 * (z // PACK), 1)
+        results[number, z] = jnp.where((lane < 8) | (lane >= 120), value, mid[rows])
         if z % 4 == 3:
             quarter = pl.ds(z - 3, 4)
             copy = pltpu.make_async_copy(results.at[number, quarter], out.at[quarter], sems.at[number, z // 4])
             copy.start()
             copies.append(copy)
 
+    sides = [joined(value) for value in edge_x]
     for z in range(HZ):
-        give(0, solution_out, z, own_x[z], edge_x[z % PACK])
+        give(0, solution_out, z, own_x[z], sides[z % PACK])
     edge_r = level_edge.residual(edge_x)
     own_r = level_own.residual(own_x)
+    sides = [joined(value) for value in edge_r]
     for z in range(HZ):
-        give(1, residual_out, z, own_r[z], edge_r[z % PACK])
+        give(1, residual_out, z, own_r[z], sides[z % PACK])
     for copy in copies:
         copy.wait()
 
@@ -572,7 +575,7 @@
     near_own, far_own, own_merge, edge_merge, move, *spreads = call(
         prepare_kernel, [VMEM], [(2, 2, BC, BS)] * 2 + tables
     )(own)
-    near_span, far_span = call(margin_kernel, [VMEM] * 4, [packed, packed])(near_own, far_own, near_cast, far_cast)
+    near_span, far_span = call(margin_kernel, [VMEM] * 4, [packed, packed])(near_own, far_own, far_cast, near_cast)
     near_span = swap(near_span, "span", False)
     far_span = swap(far_span, "span", True)
     *kept_own, merged, merged_mid, inner = call(
@@ -580,7 +583,7 @@
         [VMEM] * 4,
         own_state + [(HZ, HALF, BS), (HZ, HALF - 8, BS), (2, PACK, ROWS, BS)],
         [(HZ, ROWS, BS)],
-    )(own, near_cast, far_cast, own_merge)
+    )(own, far_cast, near_cast, own_merge)
     (slots,) = call(
         edge_kernel, [VMEM] * 6, [(count, 8, BS)], [(8, SENT, BS), (4, 16, BS)]
     )(near_span, far_span, inner, merged_mid, edge_merge, move)

time: 40.7 us -> 40.7 us (level)
  waiting for transfers between devices: 5.43 us -> 2.3 us
  starting transfers between devices: 15.2 us -> 17.6 us
  blocking collectives: 9.88 us -> 10.6 us
    ppermute x6, waiting for transfers between devices: 5.43 us -> 2.3 us  [swap(): return lax.ppermute(value, axis, list(enumerate(partner)))]
    ppermute x6, starting transfers between devices: 15.2 us -> 17.6 us  [swap(): return lax.ppermute(value, axis, list(enumerate(partner)))]
    all_to_all x1, blocking collectives: 9.88 us -> 10.6 us  [shards(): column = lax.all_to_all(slots, 'cast', 0, 0)]
  transfers between devices with their start and end apart: 6 -> 6, of which waited for: 3 -> 2; matrix products, arithmetic and copies ran while one was open for 0% -> 0% of each run, Pallas kernels for 7% -> 7%
where the time goes in v8:
time: 40.7 us; the launch traced here: 40.6 us
  starting transfers between devices  17.6 us (43%)
  blocking collectives  10.6 us (26%)
  Pallas kernels  9.38 us (23%)
  waiting for transfers between devices  2.3 us (6%)
  between operations  0.68 us (2%)
    ppermute x6, starting transfers between devices, swap(): return lax.ppermute(value, axis, list(enumerate(partner)))  17.6 us
    all_to_all x1, blocking collectives, shards(): column = lax.all_to_all(slots, 'cast', 0, 0)  10.6 us
    pallas_call x1, Pallas kernels, shards(): call(ascent_kernel, [VMEM] * (3 + len(state)), [(HZ, BC, BS)] * 2, scratc...  3.72 us
    ppermute x6, waiting for transfers between devices, swap(): return lax.ppermute(value, axis, list(enumerate(partner)))  2.3 us
    pallas_call x1, Pallas kernels, shards(): call(own_kernel, [VMEM] * 4, own_state + [(HZ, HALF, BS), (HZ, HALF - 8,...  1.68 us
    pallas_call x1, Pallas kernels, shards(): call(edge_kernel, [VMEM] * 6, [(count, 8, BS)], [(8, SENT, BS), (4, 16, B...  1.28 us
    pallas_call x1, Pallas kernels, shards(): call(state_kernel, [VMEM] * 5, edge_state + level1_state, [(8, ROWS, BS)])  1.11 us
    pallas_call x1, Pallas kernels, shards(): call(stage_kernel, [HBM] * 3, [(2, HZ, BC, BS), (CAST_ROWS, BS), (CAST_RO...  1.02 us
  transfers between devices with their start and end apart: 6, of which 2 were waited for; matrix products, arithmetic and copies ran while one was open for 0% of the time, Pallas kernels for 7%

profile of v8, /device:TPU:1, one launch (start us, length us, event | category | flops | bytes accessed | tf_op | source)
XLA Modules:
  0.0 40.6 jit_solution(3257763235633901060)
XLA Ops:
  0.6 1.0 %shard_map.50 = (f32[2,16,16,128]{3,2,1,0:T(8,128)S(1)}, f32[400,128]{1,0:T(8,128)S(1)}, f32[400,128]{1,0:T(8,128)S(1)}) custom-call(f32[3]{0:T(128)} %table_in.1, s32[16,16,128]{2,1,0:T(8,128)} %phase_in.1, f32[16,16,128]{2,1,0:T(8,128)} %source_in.1), custom_call_target="tpu_custom_call" | custom-call | tf_op jit(solution)/shard_map/pallas_call | solution.py:567
  1.7 2.7 %collective-permute-start = (f32[400,128]{1,0:T(8,128)S(1)}, f32[400,128]{1,0:T(8,128)S(1)}, u32[]{:S(2)}, u32[]{:S(2)}) collective-permute-start(f32[400,128]{1,0:T(8,128)S(1)} %get-tuple-element.43), channel_id=1, source_target_pairs={{0,224},{32,64},{64,32},{96,128},{128,96},{160,192},{192,160},{224... | collective-permute-start | bytes 614408 | tf_op jit(solution)/shard_map/ppermute | solution.py:555
  4.3 1.1 %collective-permute-start.1 = (f32[400,128]{1,0:T(8,128)S(1)}, f32[400,128]{1,0:T(8,128)S(1)}, u32[]{:S(2)}, u32[]{:S(2)}) collective-permute-start(f32[400,128]{1,0:T(8,128)S(1)} %get-tuple-element.44), channel_id=1, source_target_pairs={{0,32},{32,0},{64,96},{96,64},{128,160},{160,128},{192,224},{224,1... | collective-permute-start | bytes 614408 | tf_op jit(solution)/shard_map/ppermute | solution.py:555
  5.4 0.2 shard_map.51
  5.7 2.1 %collective-permute-done.far_cast = f32[400,128]{1,0:T(8,128)S(1)} collective-permute-done((f32[400,128]{1,0:T(8,128)S(1)}, f32[400,128]{1,0:T(8,128)S(1)}, u32[]{:S(2)}, u32[]{:S(2)}) %collective-permute-start) | collective-permute-done | bytes 204832 | tf_op jit(solution)/shard_map/ppermute | solution.py:555
  7.8 0.0 collective-permute-done.1.near_cast
  7.8 0.3 shard_map.52
  8.1 1.7 %collective-permute-start.2 = (f32[2,2,32,128]{3,2,1,0:T(8,128)S(1)}, f32[2,2,32,128]{3,2,1,0:T(8,128)S(1)}, u32[]{:S(2)}, u32[]{:S(2)}) collective-permute-start(f32[2,2,32,128]{3,2,1,0:T(8,128)S(1)} %get-tuple-element.45), channel_id=1, source_target_pairs={{0,1},{1,0},{2,3},{3,2},{4,5},{5,4},{6,7},{7,6},{8,9},{9,8},{10,11... | collective-permute-start | bytes 196616 | tf_op jit(solution)/shard_map/ppermute | solution.py:555
  9.8 7.2 %collective-permute-start.3 = (f32[2,2,32,128]{3,2,1,0:T(8,128)S(1)}, f32[2,2,32,128]{3,2,1,0:T(8,128)S(1)}, u32[]{:S(2)}, u32[]{:S(2)}) collective-permute-start(f32[2,2,32,128]{3,2,1,0:T(8,128)S(1)} %get-tuple-element.46), channel_id=1, source_target_pairs={{0,31},{1,2},{2,1},{3,4},{4,3},{5,6},{6,5},{7,8},{8,7},{9,10},{10,... | collective-permute-start | bytes 196616 | tf_op jit(solution)/shard_map/ppermute | solution.py:555
  17.0 1.7 %shard_map.53 = (f32[16,24,128]{2,1,0:T(8,128)S(1)}, f32[16,24,128]{2,1,0:T(8,128)S(1)}, f32[16,24,128]{2,1,0:T(8,128)S(1)}, f32[16,24,128]{2,1,0:T(8,128)S(1)},...) custom-call(f32[2,16,16,128]{3,2,1,0:T(8,128)S(1)} %get-tuple-elemen, ...), custom_call_target="tpu_custom_call" | custom-call | tf_op jit(solution)/shard_map/pallas_call | solution.py:581
  18.7 0.0 collective-permute-done.2.near_span
  18.7 0.0 collective-permute-done.3.far_span
  18.7 1.3 %shard_map.54 = f32[8,8,128]{2,1,0:T(8,128)S(1)} custom-call(f32[2,2,32,128]{3,2,1,0:T(8,128)S(1)} %collective-permute-done.2.near_span, f32[2,2,32,128]{3,2,1,0:T(8,128)S(1)} %collective-permute-done.3.far_span, f32[2,8,48,128]{3,2,1,0:T(8,128)S(1)} %get-tuple-element.48.inner, f32[16,16,128]{2,1,0:T(8,128)S(1)} %get-tuple-element.49.merged, ...), custom_call_target="tpu_custom_call" | custom-call | tf_op jit(solution)/shard_map/pallas_call | solution.py:587
  20.0 10.6 %all_to_all.5.own = f32[8,8,128]{2,1,0:T(8,128)S(1)} all-to-all(f32[8,8,128]{2,1,0:T(8,128)S(1)} %shard_map.54), channel_id=1, replica_groups=mesh['cast'=8,'span'=32] {'cast'}, dimensions={0} | all-to-all | bytes 65536 | tf_op jit(solution)/shard_map/all_to_all | solution.py:594
  30.6 0.0 collective-permute-start.5
  30.6 4.9 %collective-permute-start.4 = (f32[8,8,128]{2,1,0:T(8,128)S(1)}, f32[8,8,128]{2,1,0:T(8,128)S(1)}, u32[]{:S(2)}, u32[]{:S(2)}) collective-permute-start(f32[8,8,128]{2,1,0:T(8,128)S(1)} %all_to_all.5.own), channel_id=1, source_target_pairs={{0,31},{1,2},{2,1},{3,4},{4,3},{5,6},{6,5},{7,8},{8,7},{9,10},{10,... | collective-permute-start | bytes 98312 | tf_op jit(solution)/shard_map/ppermute | solution.py:555
  35.6 1.1 %shard_map.55 = (f32[8,24,128]{2,1,0:T(8,128)S(1)}, f32[8,24,128]{2,1,0:T(8,128)S(1)}, f32[8,24,128]{2,1,0:T(8,128)S(1)}, f32[8,24,128]{2,1,0:T(8,128)S(1)}, f32...) custom-call(f32[2,2,32,128]{3,2,1,0:T(8,128)S(1)} %collective-permut, ...), custom_call_target="tpu_custom_call" | custom-call | tf_op jit(solution)/shard_map/pallas_call | solution.py:590
  36.7 0.0 collective-permute-done.5.near_column
  36.7 0.2 collective-permute-done.4.far_column
  36.9 3.7 %shard_map.56 = (f32[16,16,128]{2,1,0:T(8,128)}, f32[16,16,128]{2,1,0:T(8,128)}) custom-call(f32[8,8,128]{2,1,0:T(8,128)S(1)} %all_to_all.5.own, f32[8,8,128]{2,1,0:T(8,128)S(1)} %collective-permute-done.4.far_column, f32[8,8,128]{2,1,0:T(8,128)S(1)} %collective-permute-done.5.near_column, bf16[128,128]{1,0:T(8,128)(2,1)S(1)} %get-tuple-element.52.narrow, ...), custom_call_target="tpu_custom_call" | custom-call | tf_op jit(solution)/shard_map/pallas_call | solution.py:611
Async XLA Ops:
  1.7 6.1 %collective-permute-start = (f32[400,128]{1,0:T(8,128)S(1)}, f32[400,128]{1,0:T(8,128)S(1)}, u32[]{:S(2)}, u32[]{:S(2)}) collective-permute-start(f32[400,128]{1,0:T(8,128)S(1)} %get-tuple-element.43), channel_id=1, source_target_pairs={{0,224},{32,64},{64,32},{96,128},{128,96},{160,192},{192,160},{224... | collective-permute-start | bytes 614408 | tf_op jit(solution)/shard_map/ppermute | solution.py:555
  4.3 3.4 %collective-permute-start.1 = (f32[400,128]{1,0:T(8,128)S(1)}, f32[400,128]{1,0:T(8,128)S(1)}, u32[]{:S(2)}, u32[]{:S(2)}) collective-permute-start(f32[400,128]{1,0:T(8,128)S(1)} %get-tuple-element.44), channel_id=1, source_target_pairs={{0,32},{32,0},{64,96},{96,64},{128,160},{160,128},{192,224},{224,1... | collective-permute-start | bytes 614408 | tf_op jit(solution)/shard_map/ppermute | solution.py:555
  8.1 10.6 %collective-permute-start.2 = (f32[2,2,32,128]{3,2,1,0:T(8,128)S(1)}, f32[2,2,32,128]{3,2,1,0:T(8,128)S(1)}, u32[]{:S(2)}, u32[]{:S(2)}) collective-permute-start(f32[2,2,32,128]{3,2,1,0:T(8,128)S(1)} %get-tuple-element.45), channel_id=1, source_target_pairs={{0,1},{1,0},{2,3},{3,2},{4,5},{5,4},{6,7},{7,6},{8,9},{9,8},{10,11... | collective-permute-start | bytes 196616 | tf_op jit(solution)/shard_map/ppermute | solution.py:555
  9.8 8.9 %collective-permute-start.3 = (f32[2,2,32,128]{3,2,1,0:T(8,128)S(1)}, f32[2,2,32,128]{3,2,1,0:T(8,128)S(1)}, u32[]{:S(2)}, u32[]{:S(2)}) collective-permute-start(f32[2,2,32,128]{3,2,1,0:T(8,128)S(1)} %get-tuple-element.46), channel_id=1, source_target_pairs={{0,31},{1,2},{2,1},{3,4},{4,3},{5,6},{6,5},{7,8},{8,7},{9,10},{10,... | collective-permute-start | bytes 196616 | tf_op jit(solution)/shard_map/ppermute | solution.py:555
  30.6 6.1 %collective-permute-start.5 = (f32[8,8,128]{2,1,0:T(8,128)S(1)}, f32[8,8,128]{2,1,0:T(8,128)S(1)}, u32[]{:S(2)}, u32[]{:S(2)}) collective-permute-start(f32[8,8,128]{2,1,0:T(8,128)S(1)} %all_to_all.5.own), channel_id=1, source_target_pairs={{0,1},{1,0},{2,3},{3,2},{4,5},{5,4},{6,7},{7,6},{8,9},{9,8},{10,11... | collective-permute-start | bytes 98312 | tf_op jit(solution)/shard_map/ppermute | solution.py:555
  30.6 6.2 %collective-permute-start.4 = (f32[8,8,128]{2,1,0:T(8,128)S(1)}, f32[8,8,128]{2,1,0:T(8,128)S(1)}, u32[]{:S(2)}, u32[]{:S(2)}) collective-permute-start(f32[8,8,128]{2,1,0:T(8,128)S(1)} %all_to_all.5.own), channel_id=1, source_target_pairs={{0,31},{1,2},{2,1},{3,4},{4,3},{5,6},{6,5},{7,8},{8,7},{9,10},{10,... | collective-permute-start | bytes 98312 | tf_op jit(solution)/shard_map/ppermute | solution.py:555

commit v9 on v8

--- a/solution.py
+++ b/solution.py
@@ -58,7 +58,7 @@
 
 
 class Level:
-    def __init__(self, cast, span, height, diag, relax, source, depth, packed=False):
+    def __init__(self, cast, span, height, diag, relax, source, depth, packed=1):
         self.cast, self.span, self.height = cast, span, height
         self.diag, self.relax, self.source = diag, relax, source
         self.depth, self.packed = depth, packed
@@ -66,10 +66,10 @@
     def near(self, x, z):
         last = self.depth - 1
         below, above = x[max(z - 1, 0)], x[min(z + 1, last)]
-        if self.packed and z == 0:
-            below = shift(x[last], 64, 1)
-        if self.packed and z == last:
-            above = shift(x[0], 64, 1)
+        if self.packed > 1 and z == 0:
+            below = shift(x[last], BS // self.packed, 1)
+        if self.packed > 1 and z == last:
+            above = shift(x[0], -(BS // self.packed), 1)
         return near(x[z], below, above, self.cast[z], self.span[z], self.height[z], self.height[z + 1])
 
     def start(self):
@@ -113,9 +113,10 @@
     cast = [2.0 / (v + shift(v, 1, 0)) for v in visc]
     span = [2.0 / (v + shift(v, 1, 1)) for v in visc]
     inner = [2.0 / (a + b) for a, b in zip(visc[:-1], visc[1:])]
-    if packed:
-        bottom = jnp.where(iota(shape, 1) < 64, 0.0, 2.0 / (visc[0] + shift(visc[-1], 64, 1)))
-        top = shift(bottom, 64, 1)
+    if packed > 1:
+        width = BS // packed
+        bottom = jnp.where(iota(shape, 1) < width, 0.0, 2.0 / (visc[0] + shift(visc[-1], width, 1)))
+        top = shift(bottom, -width, 1)
     else:
         bottom = top = jnp.zeros(shape, F32)
     height = [bottom] + inner + [top]
@@ -254,7 +255,7 @@
     return jnp.where(where, 1.0, 0.0).astype(BF16)
 
 
-def prepare_kernel(own, near_own, far_own, own_merge, edge_merge, move, narrow, widen, grow, double, expand):
+def prepare_kernel(own, near_own, far_own, own_merge, mid_merge, edge_merge, slot_merge, move, narrow, widen, grow, double, expand):
     lane = iota((BC, BS), 1)
     for a in range(2):
         for group in range(2):
@@ -267,6 +268,7 @@
             far_own[a, group], near_own[a, group] = by_side("span", tail, head)
     i, j = iota((BS, BS), 0), iota((BS, BS), 1)
     own_merge[...] = ones((i // 2 == j) & (i >= 8) & (i < 120))
+    mid_merge[...] = ones((i // 2 == j) & (i >= 4) & (i < 124))
     narrow[...] = ones(((i < 64) & (i // 2 == j)) | ((i >= 96) & (i // 2 + 64 == j)))
     widen[...] = ones(((j < 64) & (j // 2 == i)) | ((j >= 96) & (j // 2 + 64 == i)))
     grow[...] = ones(((j < 96) & (j // 2 == i)) | ((j >= 96) & (j // 2 + 64 == i)))
@@ -275,6 +277,10 @@
     m = i % 64
     target = jnp.where(m < 24, (m // 2 + 120) % BS, m // 2 + 40)
     edge_merge[...] = ones(((m < 24) | (m >= 40)) & (target == j % BS) & (i // 64 == j // BS))
+    i, j = iota((BS, 4 * BS), 0), iota((BS, 4 * BS), 1)
+    m = i % 32
+    target = jnp.where(m < 12, (m // 2 + 124) % BS, m // 2 + 52)
+    slot_merge[...] = ones(((m < 12) | (m >= 20)) & (target == j % BS) & (i // 32 == j // BS))
     i, j = iota((4 * BS, BS), 0), iota((4 * BS, BS), 1)
     move[...] = ones((i % BS < 64) & (i % BS // 2 + 32 * (i // BS) == j))
     i, j = iota((2 * BS, BS), 0), iota((2 * BS, BS), 1)
@@ -284,7 +290,7 @@
 
 
 def places(group):
-    return [(16 * sub + 64 * half, group * 4 + sub + 8 * half) for sub in range(4) for half in range(2)]
+    return [(16 * sub + 32 * g, group * 2 + sub + 4 * g) for sub in range(2) for g in range(4)]
 
 
 def margin_kernel(near_own, far_own, far_cast, near_cast, near_span, far_span):
@@ -314,7 +320,7 @@
     return jnp.concatenate([shift(sent[:8], step + more, 1), moved, shift(sent[-8:], step + more, 1)], axis=0)
 
 
-def own_kernel(own, far_cast, near_cast, own_merge, x, b, cast, span, height, diag, relax, merged, merged_mid, inner, scratch):
+def own_kernel(own, far_cast, near_cast, own_merge, mid_merge, x, b, cast, span, height, diag, relax, merged, merged_mid, inner, inner4, scratch):
     first, last, outside = beyond(ROWS, HALO)
     visc, source = [], []
     for z in range(HZ):
@@ -330,36 +336,48 @@
                 shift(low, 16, 1),
                 jnp.where(lane < 64, shift(low, 48, 1), jnp.where(lane < 96, shift(high, 80, 1), shift(high, 112, 1))),
             )
-    level = fine_level(visc, source, outside, False)
+        quarter = lane[8 : ROWS - 8]
+        for k in range(4):
+            value = None
+            for g in range(4):
+                slab = field[k + 4 * g][8 : ROWS - 8]
+                edges = jnp.where(quarter % 32 < 16, shift(slab, 32 * g + 8, 1), shift(slab, 32 * g - 104, 1))
+                value = edges if value is None else jnp.where(quarter // 32 == g, edges, value)
+            inner4[a, k] = value
+    level = fine_level(visc, source, outside, 1)
     values = level.sweep(level.start())
     keep(level, values, (x, b, cast, span, height, diag, relax))
     parts = coarse_parts(visc, level.residual(values), scratch)
     total = product(parts, own_merge[...])
     for k in range(HZ):
         merged[k] = total[HALF * k : HALF * (k + 1)]
+    total = product(parts, mid_merge[...])
+    for k in range(HZ):
         merged_mid[k] = total[HALF * k + 4 : HALF * (k + 1) - 4]
 
 
 def edge_levels(near_span, far_span, inner, merged, edge_merge, scratch, halo):
     rows = BC + 2 * halo
     first, last, outside = beyond(rows, halo)
-    lane = iota((rows, BS), 1) % 64
+    wide = halo == HALO
+    packed = 2 if wide else 4
+    lane = iota((rows, BS), 1) % (BS // packed)
     fields = []
     for a in range(2):
         slabs = []
-        for k in range(PACK):
-            group, sub = divmod(k, 4)
+        for k in range(HZ // packed):
+            group, offset = k % 4 // 2, 16 * (k % 2) + 32 * (k // 4)
             left, right = by_side("span", near_span[a, group], far_span[a, group])
-            if halo == HALO:
-                l, r = spread_rows(left, -16 * sub, 12), spread_rows(right, 48 - 16 * sub, -12)
+            if wide:
+                l, r = spread_rows(left, -offset, 12), spread_rows(right, 48 - offset, -12)
+                value = jnp.where(lane < 16, l, jnp.where(lane >= 48, r, inner[a, k]))
             else:
-                l, r = shift(left, -16 * sub, 1), shift(right, 48 - 16 * sub, 1)
-            own = inner[a, k, HALO - halo : HALO + BC + halo]
-            value = jnp.where(lane < 16, l, jnp.where(lane >= 48, r, own))
+                l, r = shift(left, -offset - 8, 1), shift(right, 24 - offset, 1)
+                value = jnp.where(lane < 8, l, jnp.where(lane >= 24, r, inner[a, k]))
             slabs.append(ends(value, first, last, halo) if a == 0 else value)
         fields.append(slabs)
     visc, source = fields
-    level = fine_level(visc, source, outside, True)
+    level = fine_level(visc, source, outside, packed)
     values = level.sweep(level.start())
     fine = level, values
     parts = coarse_parts(visc, level.residual(values), scratch)
@@ -371,11 +389,11 @@
     coarse = []
     for k in range(HZ):
         a, z = divmod(k, 8)
-        side, pos = divmod(z, 4)
-        row = half * (4 * a + pos)
+        side, pos = divmod(z, 4 if wide else 2)
+        row = half * (HZ // packed // 2 * a + pos)
         coarse.append(merged[k] + total[row : row + half, BS * side : BS * (side + 1)])
     lane = iota((half, BS), 1)
-    known = (lane < 72) | (lane >= 120)
+    known = (lane < BS // 2 + edge) | (lane >= BS - edge)
     coeff = [jnp.where(known, 0.125 * ends(c, first, last, edge), 1.0) for c in coarse[:8]]
     source = [0.5 * c for c in coarse[8:]]
     height = height_faces(coeff)
@@ -488,7 +506,7 @@
         for s in range(2):
             wide_edge[k, pl.ds(s, KEPT1, stride=2), :] = spread[KEPT1 * k : KEPT1 * (k + 1)]
     level_own = Level(casto, spano, heighto, diago, relaxo, bo, HZ)
-    level_edge = Level(caste, spane, heighte, diage, relaxe, be, PACK, True)
+    level_edge = Level(caste, spane, heighte, diage, relaxe, be, PACK, 2)
 
     def refined(wide, k):
         edge = jnp.where(iota((8, BS), 0) < 4, wide[k, BC : BC + 8], wide[k, BC + 8 :])
@@ -570,23 +588,23 @@
     far_cast = swap(far_cast, "cast", True)
     near_cast = swap(near_cast, "cast", False)
     square = (BS, BS)
-    tables = [square, (BS, 2 * BS), (4 * BS, BS), square, square, square, square, (2 * BS, BS)]
+    tables = [square, square, (BS, 2 * BS), (BS, 4 * BS), (4 * BS, BS), square, square, square, square, (2 * BS, BS)]
     tables = [jax.ShapeDtypeStruct(t, BF16) for t in tables]
-    near_own, far_own, own_merge, edge_merge, move, *spreads = call(
+    near_own, far_own, own_merge, mid_merge, edge_merge, slot_merge, move, *spreads = call(
         prepare_kernel, [VMEM], [(2, 2, BC, BS)] * 2 + tables
     )(own)
     near_span, far_span = call(margin_kernel, [VMEM] * 4, [packed, packed])(near_own, far_own, far_cast, near_cast)
     near_span = swap(near_span, "span", False)
     far_span = swap(far_span, "span", True)
-    *kept_own, merged, merged_mid, inner = call(
+    *kept_own, merged, merged_mid, inner, inner4 = call(
         own_kernel,
-        [VMEM] * 4,
-        own_state + [(HZ, HALF, BS), (HZ, HALF - 8, BS), (2, PACK, ROWS, BS)],
+        [VMEM] * 5,
+        own_state + [(HZ, HALF, BS), (HZ, HALF - 8, BS), (2, PACK, ROWS, BS), (2, 4, SENT, BS)],
         [(HZ, ROWS, BS)],
-    )(own, far_cast, near_cast, own_merge)
+    )(own, far_cast, near_cast, own_merge, mid_merge)
     (slots,) = call(
-        edge_kernel, [VMEM] * 6, [(count, 8, BS)], [(8, SENT, BS), (4, 16, BS)]
-    )(near_span, far_span, inner, merged_mid, edge_merge, move)
+        edge_kernel, [VMEM] * 6, [(count, 8, BS)], [(4, SENT, BS), (4, 16, BS)]
+    )(near_span, far_span, inner4, merged_mid, slot_merge, move)
     kept_edge = call(state_kernel, [VMEM] * 5, edge_state + level1_state, [(8, ROWS, BS)])(
         near_span, far_span, inner, merged, edge_merge
     )

time: 40.7 us -> 40.6 us (level)
  transfers between devices with their start and end apart: 6 -> 6, of which waited for: 2 -> 2; matrix products, arithmetic and copies ran while one was open for 0% -> 0% of each run, Pallas kernels for 7% -> 8%
where the time goes in v9:
time: 40.6 us; the launch traced here: 40.4 us
  starting transfers between devices  17.6 us (43%)
  blocking collectives  10.3 us (25%)
  Pallas kernels  9.64 us (24%)
  waiting for transfers between devices  2.26 us (6%)
  between operations  0.69 us (2%)
    ppermute x6, starting transfers between devices, swap(): return lax.ppermute(value, axis, list(enumerate(partner)))  17.6 us
    all_to_all x1, blocking collectives, shards(): column = lax.all_to_all(slots, 'cast', 0, 0)  10.3 us
    pallas_call x1, Pallas kernels, shards(): call(ascent_kernel, [VMEM] * (3 + len(state)), [(HZ, BC, BS)] * 2, scratc...  3.73 us
    ppermute x6, waiting for transfers between devices, swap(): return lax.ppermute(value, axis, list(enumerate(partner)))  2.26 us
    pallas_call x1, Pallas kernels, shards(): call(own_kernel, [VMEM] * 5, own_state + [(HZ, HALF, BS), (HZ, HALF - 8,...  2.04 us
    pallas_call x1, Pallas kernels, shards(): call(edge_kernel, [VMEM] * 6, [(count, 8, BS)], [(4, SENT, BS), (4, 16, B...  1.13 us
    pallas_call x1, Pallas kernels, shards(): call(state_kernel, [VMEM] * 5, edge_state + level1_state, [(8, ROWS, BS)])  1.11 us
    pallas_call x1, Pallas kernels, shards(): call(stage_kernel, [HBM] * 3, [(2, HZ, BC, BS), (CAST_ROWS, BS), (CAST_RO...  1.02 us
  transfers between devices with their start and end apart: 6, of which 2 were waited for; matrix products, arithmetic and copies ran while one was open for 0% of the time, Pallas kernels for 8%

profile of v9, /device:TPU:1, one launch (start us, length us, event | category | flops | bytes accessed | tf_op | source)
XLA Modules:
  0.0 40.4 jit_solution(2243633569062978205)
XLA Ops:
  0.6 1.0 %shard_map.50 = (f32[2,16,16,128]{3,2,1,0:T(8,128)S(1)}, f32[400,128]{1,0:T(8,128)S(1)}, f32[400,128]{1,0:T(8,128)S(1)}) custom-call(f32[3]{0:T(128)} %table_in.1, s32[16,16,128]{2,1,0:T(8,128)} %phase_in.1, f32[16,16,128]{2,1,0:T(8,128)} %source_in.1), custom_call_target="tpu_custom_call" | custom-call | tf_op jit(solution)/shard_map/pallas_call | solution.py:585
  1.7 2.7 %collective-permute-start = (f32[400,128]{1,0:T(8,128)S(1)}, f32[400,128]{1,0:T(8,128)S(1)}, u32[]{:S(2)}, u32[]{:S(2)}) collective-permute-start(f32[400,128]{1,0:T(8,128)S(1)} %get-tuple-element.46), channel_id=1, source_target_pairs={{0,224},{32,64},{64,32},{96,128},{128,96},{160,192},{192,160},{224... | collective-permute-start | bytes 614408 | tf_op jit(solution)/shard_map/ppermute | solution.py:573
  4.3 1.1 %collective-permute-start.1 = (f32[400,128]{1,0:T(8,128)S(1)}, f32[400,128]{1,0:T(8,128)S(1)}, u32[]{:S(2)}, u32[]{:S(2)}) collective-permute-start(f32[400,128]{1,0:T(8,128)S(1)} %get-tuple-element.47), channel_id=1, source_target_pairs={{0,32},{32,0},{64,96},{96,64},{128,160},{160,128},{192,224},{224,1... | collective-permute-start | bytes 614408 | tf_op jit(solution)/shard_map/ppermute | solution.py:573
  5.4 0.3 shard_map.51
  5.7 2.1 %collective-permute-done.far_cast = f32[400,128]{1,0:T(8,128)S(1)} collective-permute-done((f32[400,128]{1,0:T(8,128)S(1)}, f32[400,128]{1,0:T(8,128)S(1)}, u32[]{:S(2)}, u32[]{:S(2)}) %collective-permute-start) | collective-permute-done | bytes 204832 | tf_op jit(solution)/shard_map/ppermute | solution.py:573
  7.8 0.0 collective-permute-done.1.near_cast
  7.8 0.3 shard_map.52
  8.1 1.7 %collective-permute-start.2 = (f32[2,2,32,128]{3,2,1,0:T(8,128)S(1)}, f32[2,2,32,128]{3,2,1,0:T(8,128)S(1)}, u32[]{:S(2)}, u32[]{:S(2)}) collective-permute-start(f32[2,2,32,128]{3,2,1,0:T(8,128)S(1)} %get-tuple-element.48), channel_id=1, source_target_pairs={{0,1},{1,0},{2,3},{3,2},{4,5},{5,4},{6,7},{7,6},{8,9},{9,8},{10,11... | collective-permute-start | bytes 196616 | tf_op jit(solution)/shard_map/ppermute | solution.py:573
  9.8 7.2 %collective-permute-start.3 = (f32[2,2,32,128]{3,2,1,0:T(8,128)S(1)}, f32[2,2,32,128]{3,2,1,0:T(8,128)S(1)}, u32[]{:S(2)}, u32[]{:S(2)}) collective-permute-start(f32[2,2,32,128]{3,2,1,0:T(8,128)S(1)} %get-tuple-element.49), channel_id=1, source_target_pairs={{0,31},{1,2},{2,1},{3,4},{4,3},{5,6},{6,5},{7,8},{8,7},{9,10},{10,... | collective-permute-start | bytes 196616 | tf_op jit(solution)/shard_map/ppermute | solution.py:573
  17.0 2.0 %shard_map.53 = (f32[16,24,128]{2,1,0:T(8,128)S(1)}, f32[16,24,128]{2,1,0:T(8,128)S(1)}, f32[16,24,128]{2,1,0:T(8,128)S(1)}, f32[16,24,128]{2,1,0:T(8,128)S(1)},...) custom-call(f32[2,16,16,128]{3,2,1,0:T(8,128)S(1)} %get-tuple-elemen, ...), custom_call_target="tpu_custom_call" | custom-call | tf_op jit(solution)/shard_map/pallas_call | solution.py:599
  19.1 0.0 collective-permute-done.2.near_span
  19.1 0.0 collective-permute-done.3.far_span
  19.1 1.1 %shard_map.54 = f32[8,8,128]{2,1,0:T(8,128)S(1)} custom-call(f32[2,2,32,128]{3,2,1,0:T(8,128)S(1)} %collective-permute-done.2.near_span, f32[2,2,32,128]{3,2,1,0:T(8,128)S(1)} %collective-permute-done.3.far_span, f32[2,4,32,128]{3,2,1,0:T(8,128)S(1)} %get-tuple-element.52.inner, f32[16,16,128]{2,1,0:T(8,128)S(1)} %get-tuple-element.53.merged, ...), custom_call_target="tpu_custom_call" | custom-call | tf_op jit(solution)/shard_map/pallas_call | solution.py:605
  20.2 10.3 %all_to_all.5.own = f32[8,8,128]{2,1,0:T(8,128)S(1)} all-to-all(f32[8,8,128]{2,1,0:T(8,128)S(1)} %shard_map.54), channel_id=1, replica_groups=mesh['cast'=8,'span'=32] {'cast'}, dimensions={0} | all-to-all | bytes 65536 | tf_op jit(solution)/shard_map/all_to_all | solution.py:612
  30.5 0.0 collective-permute-start.5
  30.5 4.9 %collective-permute-start.4 = (f32[8,8,128]{2,1,0:T(8,128)S(1)}, f32[8,8,128]{2,1,0:T(8,128)S(1)}, u32[]{:S(2)}, u32[]{:S(2)}) collective-permute-start(f32[8,8,128]{2,1,0:T(8,128)S(1)} %all_to_all.5.own), channel_id=1, source_target_pairs={{0,31},{1,2},{2,1},{3,4},{4,3},{5,6},{6,5},{7,8},{8,7},{9,10},{10,... | collective-permute-start | bytes 98312 | tf_op jit(solution)/shard_map/ppermute | solution.py:573
  35.4 1.1 %shard_map.55 = (f32[8,24,128]{2,1,0:T(8,128)S(1)}, f32[8,24,128]{2,1,0:T(8,128)S(1)}, f32[8,24,128]{2,1,0:T(8,128)S(1)}, f32[8,24,128]{2,1,0:T(8,128)S(1)}, f32...) custom-call(f32[2,2,32,128]{3,2,1,0:T(8,128)S(1)} %collective-permut, ...), custom_call_target="tpu_custom_call" | custom-call | tf_op jit(solution)/shard_map/pallas_call | solution.py:608
  36.5 0.0 collective-permute-done.5.near_column
  36.5 0.2 collective-permute-done.4.far_column
  36.7 3.7 %shard_map.56 = (f32[16,16,128]{2,1,0:T(8,128)}, f32[16,16,128]{2,1,0:T(8,128)}) custom-call(f32[8,8,128]{2,1,0:T(8,128)S(1)} %all_to_all.5.own, f32[8,8,128]{2,1,0:T(8,128)S(1)} %collective-permute-done.4.far_column, f32[8,8,128]{2,1,0:T(8,128)S(1)} %collective-permute-done.5.near_column, bf16[128,128]{1,0:T(8,128)(2,1)S(1)} %get-tuple-element.56.narrow, ...), custom_call_target="tpu_custom_call" | custom-call | tf_op jit(solution)/shard_map/pallas_call | solution.py:629
Async XLA Ops:
  1.7 6.1 %collective-permute-start = (f32[400,128]{1,0:T(8,128)S(1)}, f32[400,128]{1,0:T(8,128)S(1)}, u32[]{:S(2)}, u32[]{:S(2)}) collective-permute-start(f32[400,128]{1,0:T(8,128)S(1)} %get-tuple-element.46), channel_id=1, source_target_pairs={{0,224},{32,64},{64,32},{96,128},{128,96},{160,192},{192,160},{224... | collective-permute-start | bytes 614408 | tf_op jit(solution)/shard_map/ppermute | solution.py:573
  4.3 3.4 %collective-permute-start.1 = (f32[400,128]{1,0:T(8,128)S(1)}, f32[400,128]{1,0:T(8,128)S(1)}, u32[]{:S(2)}, u32[]{:S(2)}) collective-permute-start(f32[400,128]{1,0:T(8,128)S(1)} %get-tuple-element.47), channel_id=1, source_target_pairs={{0,32},{32,0},{64,96},{96,64},{128,160},{160,128},{192,224},{224,1... | collective-permute-start | bytes 614408 | tf_op jit(solution)/shard_map/ppermute | solution.py:573
  8.1 10.9 %collective-permute-start.2 = (f32[2,2,32,128]{3,2,1,0:T(8,128)S(1)}, f32[2,2,32,128]{3,2,1,0:T(8,128)S(1)}, u32[]{:S(2)}, u32[]{:S(2)}) collective-permute-start(f32[2,2,32,128]{3,2,1,0:T(8,128)S(1)} %get-tuple-element.48), channel_id=1, source_target_pairs={{0,1},{1,0},{2,3},{3,2},{4,5},{5,4},{6,7},{7,6},{8,9},{9,8},{10,11... | collective-permute-start | bytes 196616 | tf_op jit(solution)/shard_map/ppermute | solution.py:573
  9.8 9.2 %collective-permute-start.3 = (f32[2,2,32,128]{3,2,1,0:T(8,128)S(1)}, f32[2,2,32,128]{3,2,1,0:T(8,128)S(1)}, u32[]{:S(2)}, u32[]{:S(2)}) collective-permute-start(f32[2,2,32,128]{3,2,1,0:T(8,128)S(1)} %get-tuple-element.49), channel_id=1, source_target_pairs={{0,31},{1,2},{2,1},{3,4},{4,3},{5,6},{6,5},{7,8},{8,7},{9,10},{10,... | collective-permute-start | bytes 196616 | tf_op jit(solution)/shard_map/ppermute | solution.py:573
  30.5 6.1 %collective-permute-start.5 = (f32[8,8,128]{2,1,0:T(8,128)S(1)}, f32[8,8,128]{2,1,0:T(8,128)S(1)}, u32[]{:S(2)}, u32[]{:S(2)}) collective-permute-start(f32[8,8,128]{2,1,0:T(8,128)S(1)} %all_to_all.5.own), channel_id=1, source_target_pairs={{0,1},{1,0},{2,3},{3,2},{4,5},{5,4},{6,7},{7,6},{8,9},{9,8},{10,11... | collective-permute-start | bytes 98312 | tf_op jit(solution)/shard_map/ppermute | solution.py:573
  30.5 6.2 %collective-permute-start.4 = (f32[8,8,128]{2,1,0:T(8,128)S(1)}, f32[8,8,128]{2,1,0:T(8,128)S(1)}, u32[]{:S(2)}, u32[]{:S(2)}) collective-permute-start(f32[8,8,128]{2,1,0:T(8,128)S(1)} %all_to_all.5.own), channel_id=1, source_target_pairs={{0,31},{1,2},{2,1},{3,4},{4,3},{5,6},{6,5},{7,8},{8,7},{9,10},{10,... | collective-permute-start | bytes 98312 | tf_op jit(solution)/shard_map/ppermute | solution.py:573

commit v10 on v9

--- a/solution.py
+++ b/solution.py
@@ -102,8 +102,11 @@
             ]
         return x
 
+    def residual_at(self, x, z):
+        return self.source[z] - self.diag[z] * x[z] + self.near(x, z)
+
     def residual(self, x):
-        return [self.source[z] - self.diag[z] * x[z] + self.near(x, z) for z in range(self.depth)]
+        return [self.residual_at(x, z) for z in range(self.depth)]
 
 
 def fine_level(visc, source, outside, packed):
@@ -234,19 +237,22 @@
 
     copies = [
         pltpu.make_async_copy(table_in, table, sems.at[0]),
-        pltpu.make_async_copy(phase_in, phase, sems.at[1]),
-        pltpu.make_async_copy(source_in, out.at[1], sems.at[2]),
+        pltpu.make_async_copy(phase_in.at[pl.ds(0, 8)], phase.at[pl.ds(0, 8)], sems.at[1]),
+        pltpu.make_async_copy(phase_in.at[pl.ds(8, 8)], phase.at[pl.ds(8, 8)], sems.at[2]),
+        pltpu.make_async_copy(source_in, out.at[1], sems.at[3]),
     ]
     for copy in copies:
         copy.start()
     copies[0].wait()
     copies[1].wait()
     for z in range(HZ):
+        if z == 8:
+            copies[2].wait()
         p = phase[z]
         value = jnp.where(p == 0, table[0], jnp.where(p == 1, table[1], table[2]))
         out[0, z] = value
         put(0, z, value)
-    copies[2].wait()
+    copies[3].wait()
     for z in range(HZ):
         put(1, z, out[1, z])
 
@@ -540,11 +546,9 @@
     sides = [joined(value) for value in edge_x]
     for z in range(HZ):
         give(0, solution_out, z, own_x[z], sides[z % PACK])
-    edge_r = level_edge.residual(edge_x)
-    own_r = level_own.residual(own_x)
-    sides = [joined(value) for value in edge_r]
+    sides = [joined(value) for value in level_edge.residual(edge_x)]
     for z in range(HZ):
-        give(1, residual_out, z, own_r[z], sides[z % PACK])
+        give(1, residual_out, z, level_own.residual_at(own_x, z), sides[z % PACK])
     for copy in copies:
         copy.wait()
 
@@ -581,7 +585,7 @@
     level1_state = [(8, KEPT1, BS)] * 4 + [(9, KEPT1, BS), (8, KEPT1, BS)]
 
     arguments = (pltpu.with_memory_space_constraint(a, pltpu.HBM) for a in (viscosity_table, phase, pressure_source))
-    stage_scratch = [pltpu.SMEM((3,), F32), pltpu.VMEM((HZ, BC, BS), jnp.int32), pltpu.SemaphoreType.DMA((3,))]
+    stage_scratch = [pltpu.SMEM((3,), F32), pltpu.VMEM((HZ, BC, BS), jnp.int32), pltpu.SemaphoreType.DMA((4,))]
     own, far_cast, near_cast = call(
         stage_kernel, [HBM] * 3, [(2, HZ, BC, BS), (CAST_ROWS, BS), (CAST_ROWS, BS)], stage_scratch
     )(*arguments)

time: 40.6 us -> 40.6 us (level)
  no operation moved by 1% of the time
where the time goes in v10:
time: 40.6 us; the launch traced here: 40.5 us
  starting transfers between devices  17.6 us (43%)
  blocking collectives  10.3 us (25%)
  Pallas kernels  9.65 us (24%)
  waiting for transfers between devices  2.26 us (6%)
  between operations  0.69 us (2%)
    ppermute x6, starting transfers between devices, swap(): return lax.ppermute(value, axis, list(enumerate(partner)))  17.6 us
    all_to_all x1, blocking collectives, shards(): column = lax.all_to_all(slots, 'cast', 0, 0)  10.3 us
    pallas_call x1, Pallas kernels, shards(): call(ascent_kernel, [VMEM] * (3 + len(state)), [(HZ, BC, BS)] * 2, scratc...  3.73 us
    ppermute x6, waiting for transfers between devices, swap(): return lax.ppermute(value, axis, list(enumerate(partner)))  2.26 us
    pallas_call x1, Pallas kernels, shards(): call(own_kernel, [VMEM] * 5, own_state + [(HZ, HALF, BS), (HZ, HALF - 8,...  2.04 us
    pallas_call x1, Pallas kernels, shards(): call(edge_kernel, [VMEM] * 6, [(count, 8, BS)], [(4, SENT, BS), (4, 16, B...  1.13 us
    pallas_call x1, Pallas kernels, shards(): call(state_kernel, [VMEM] * 5, edge_state + level1_state, [(8, ROWS, BS)])  1.11 us
    pallas_call x1, Pallas kernels, shards(): call(stage_kernel, [HBM] * 3, [(2, HZ, BC, BS), (CAST_ROWS, BS), (CAST_RO...  1.03 us
  transfers between devices with their start and end apart: 6, of which 2 were waited for; matrix products, arithmetic and copies ran while one was open for 0% of the time, Pallas kernels for 8%

profile of v10, /device:TPU:1, one launch (start us, length us, event | category | flops | bytes accessed | tf_op | source)
XLA Modules:
  0.0 40.5 jit_solution(10704560248128597734)
XLA Ops:
  0.6 1.0 %shard_map.50 = (f32[2,16,16,128]{3,2,1,0:T(8,128)S(1)}, f32[400,128]{1,0:T(8,128)S(1)}, f32[400,128]{1,0:T(8,128)S(1)}) custom-call(f32[3]{0:T(128)} %table_in.1, s32[16,16,128]{2,1,0:T(8,128)} %phase_in.1, f32[16,16,128]{2,1,0:T(8,128)} %source_in.1), custom_call_target="tpu_custom_call" | custom-call | tf_op jit(solution)/shard_map/pallas_call | solution.py:589
  1.7 2.7 %collective-permute-start = (f32[400,128]{1,0:T(8,128)S(1)}, f32[400,128]{1,0:T(8,128)S(1)}, u32[]{:S(2)}, u32[]{:S(2)}) collective-permute-start(f32[400,128]{1,0:T(8,128)S(1)} %get-tuple-element.46), channel_id=1, source_target_pairs={{0,224},{32,64},{64,32},{96,128},{128,96},{160,192},{192,160},{224... | collective-permute-start | bytes 614408 | tf_op jit(solution)/shard_map/ppermute | solution.py:577
  4.4 1.1 %collective-permute-start.1 = (f32[400,128]{1,0:T(8,128)S(1)}, f32[400,128]{1,0:T(8,128)S(1)}, u32[]{:S(2)}, u32[]{:S(2)}) collective-permute-start(f32[400,128]{1,0:T(8,128)S(1)} %get-tuple-element.47), channel_id=1, source_target_pairs={{0,32},{32,0},{64,96},{96,64},{128,160},{160,128},{192,224},{224,1... | collective-permute-start | bytes 614408 | tf_op jit(solution)/shard_map/ppermute | solution.py:577
  5.5 0.3 shard_map.51
  5.7 2.1 %collective-permute-done.far_cast = f32[400,128]{1,0:T(8,128)S(1)} collective-permute-done((f32[400,128]{1,0:T(8,128)S(1)}, f32[400,128]{1,0:T(8,128)S(1)}, u32[]{:S(2)}, u32[]{:S(2)}) %collective-permute-start) | collective-permute-done | bytes 204832 | tf_op jit(solution)/shard_map/ppermute | solution.py:577
  7.8 0.0 collective-permute-done.1.near_cast
  7.8 0.3 shard_map.52
  8.2 1.7 %collective-permute-start.2 = (f32[2,2,32,128]{3,2,1,0:T(8,128)S(1)}, f32[2,2,32,128]{3,2,1,0:T(8,128)S(1)}, u32[]{:S(2)}, u32[]{:S(2)}) collective-permute-start(f32[2,2,32,128]{3,2,1,0:T(8,128)S(1)} %get-tuple-element.48), channel_id=1, source_target_pairs={{0,1},{1,0},{2,3},{3,2},{4,5},{5,4},{6,7},{7,6},{8,9},{9,8},{10,11... | collective-permute-start | bytes 196616 | tf_op jit(solution)/shard_map/ppermute | solution.py:577
  9.8 7.2 %collective-permute-start.3 = (f32[2,2,32,128]{3,2,1,0:T(8,128)S(1)}, f32[2,2,32,128]{3,2,1,0:T(8,128)S(1)}, u32[]{:S(2)}, u32[]{:S(2)}) collective-permute-start(f32[2,2,32,128]{3,2,1,0:T(8,128)S(1)} %get-tuple-element.49), channel_id=1, source_target_pairs={{0,31},{1,2},{2,1},{3,4},{4,3},{5,6},{6,5},{7,8},{8,7},{9,10},{10,... | collective-permute-start | bytes 196616 | tf_op jit(solution)/shard_map/ppermute | solution.py:577
  17.0 2.0 %shard_map.53 = (f32[16,24,128]{2,1,0:T(8,128)S(1)}, f32[16,24,128]{2,1,0:T(8,128)S(1)}, f32[16,24,128]{2,1,0:T(8,128)S(1)}, f32[16,24,128]{2,1,0:T(8,128)S(1)},...) custom-call(f32[2,16,16,128]{3,2,1,0:T(8,128)S(1)} %get-tuple-elemen, ...), custom_call_target="tpu_custom_call" | custom-call | tf_op jit(solution)/shard_map/pallas_call | solution.py:603
  19.1 0.0 collective-permute-done.2.near_span
  19.1 0.0 collective-permute-done.3.far_span
  19.1 1.1 %shard_map.54 = f32[8,8,128]{2,1,0:T(8,128)S(1)} custom-call(f32[2,2,32,128]{3,2,1,0:T(8,128)S(1)} %collective-permute-done.2.near_span, f32[2,2,32,128]{3,2,1,0:T(8,128)S(1)} %collective-permute-done.3.far_span, f32[2,4,32,128]{3,2,1,0:T(8,128)S(1)} %get-tuple-element.52.inner, f32[16,16,128]{2,1,0:T(8,128)S(1)} %get-tuple-element.53.merged, ...), custom_call_target="tpu_custom_call" | custom-call | tf_op jit(solution)/shard_map/pallas_call | solution.py:609
  20.2 10.3 %all_to_all.5.own = f32[8,8,128]{2,1,0:T(8,128)S(1)} all-to-all(f32[8,8,128]{2,1,0:T(8,128)S(1)} %shard_map.54), channel_id=1, replica_groups=mesh['cast'=8,'span'=32] {'cast'}, dimensions={0} | all-to-all | bytes 65536 | tf_op jit(solution)/shard_map/all_to_all | solution.py:616
  30.5 0.0 collective-permute-start.5
  30.5 4.9 %collective-permute-start.4 = (f32[8,8,128]{2,1,0:T(8,128)S(1)}, f32[8,8,128]{2,1,0:T(8,128)S(1)}, u32[]{:S(2)}, u32[]{:S(2)}) collective-permute-start(f32[8,8,128]{2,1,0:T(8,128)S(1)} %all_to_all.5.own), channel_id=1, source_target_pairs={{0,31},{1,2},{2,1},{3,4},{4,3},{5,6},{6,5},{7,8},{8,7},{9,10},{10,... | collective-permute-start | bytes 98312 | tf_op jit(solution)/shard_map/ppermute | solution.py:577
  35.4 1.1 %shard_map.55 = (f32[8,24,128]{2,1,0:T(8,128)S(1)}, f32[8,24,128]{2,1,0:T(8,128)S(1)}, f32[8,24,128]{2,1,0:T(8,128)S(1)}, f32[8,24,128]{2,1,0:T(8,128)S(1)}, f32...) custom-call(f32[2,2,32,128]{3,2,1,0:T(8,128)S(1)} %collective-permut, ...), custom_call_target="tpu_custom_call" | custom-call | tf_op jit(solution)/shard_map/pallas_call | solution.py:612
  36.5 0.0 collective-permute-done.5.near_column
  36.6 0.2 collective-permute-done.4.far_column
  36.7 3.7 %shard_map.56 = (f32[16,16,128]{2,1,0:T(8,128)}, f32[16,16,128]{2,1,0:T(8,128)}) custom-call(f32[8,8,128]{2,1,0:T(8,128)S(1)} %all_to_all.5.own, f32[8,8,128]{2,1,0:T(8,128)S(1)} %collective-permute-done.4.far_column, f32[8,8,128]{2,1,0:T(8,128)S(1)} %collective-permute-done.5.near_column, bf16[128,128]{1,0:T(8,128)(2,1)S(1)} %get-tuple-element.56.narrow, ...), custom_call_target="tpu_custom_call" | custom-call | tf_op jit(solution)/shard_map/pallas_call | solution.py:633
Async XLA Ops:
  1.7 6.1 %collective-permute-start = (f32[400,128]{1,0:T(8,128)S(1)}, f32[400,128]{1,0:T(8,128)S(1)}, u32[]{:S(2)}, u32[]{:S(2)}) collective-permute-start(f32[400,128]{1,0:T(8,128)S(1)} %get-tuple-element.46), channel_id=1, source_target_pairs={{0,224},{32,64},{64,32},{96,128},{128,96},{160,192},{192,160},{224... | collective-permute-start | bytes 614408 | tf_op jit(solution)/shard_map/ppermute | solution.py:577
  4.4 3.4 %collective-permute-start.1 = (f32[400,128]{1,0:T(8,128)S(1)}, f32[400,128]{1,0:T(8,128)S(1)}, u32[]{:S(2)}, u32[]{:S(2)}) collective-permute-start(f32[400,128]{1,0:T(8,128)S(1)} %get-tuple-element.47), channel_id=1, source_target_pairs={{0,32},{32,0},{64,96},{96,64},{128,160},{160,128},{192,224},{224,1... | collective-permute-start | bytes 614408 | tf_op jit(solution)/shard_map/ppermute | solution.py:577
  8.2 10.9 %collective-permute-start.2 = (f32[2,2,32,128]{3,2,1,0:T(8,128)S(1)}, f32[2,2,32,128]{3,2,1,0:T(8,128)S(1)}, u32[]{:S(2)}, u32[]{:S(2)}) collective-permute-start(f32[2,2,32,128]{3,2,1,0:T(8,128)S(1)} %get-tuple-element.48), channel_id=1, source_target_pairs={{0,1},{1,0},{2,3},{3,2},{4,5},{5,4},{6,7},{7,6},{8,9},{9,8},{10,11... | collective-permute-start | bytes 196616 | tf_op jit(solution)/shard_map/ppermute | solution.py:577
  9.8 9.2 %collective-permute-start.3 = (f32[2,2,32,128]{3,2,1,0:T(8,128)S(1)}, f32[2,2,32,128]{3,2,1,0:T(8,128)S(1)}, u32[]{:S(2)}, u32[]{:S(2)}) collective-permute-start(f32[2,2,32,128]{3,2,1,0:T(8,128)S(1)} %get-tuple-element.49), channel_id=1, source_target_pairs={{0,31},{1,2},{2,1},{3,4},{4,3},{5,6},{6,5},{7,8},{8,7},{9,10},{10,... | collective-permute-start | bytes 196616 | tf_op jit(solution)/shard_map/ppermute | solution.py:577
  30.5 6.1 %collective-permute-start.5 = (f32[8,8,128]{2,1,0:T(8,128)S(1)}, f32[8,8,128]{2,1,0:T(8,128)S(1)}, u32[]{:S(2)}, u32[]{:S(2)}) collective-permute-start(f32[8,8,128]{2,1,0:T(8,128)S(1)} %all_to_all.5.own), channel_id=1, source_target_pairs={{0,1},{1,0},{2,3},{3,2},{4,5},{5,4},{6,7},{7,6},{8,9},{9,8},{10,11... | collective-permute-start | bytes 98312 | tf_op jit(solution)/shard_map/ppermute | solution.py:577
  30.5 6.2 %collective-permute-start.4 = (f32[8,8,128]{2,1,0:T(8,128)S(1)}, f32[8,8,128]{2,1,0:T(8,128)S(1)}, u32[]{:S(2)}, u32[]{:S(2)}) collective-permute-start(f32[8,8,128]{2,1,0:T(8,128)S(1)} %all_to_all.5.own), channel_id=1, source_target_pairs={{0,31},{1,2},{2,1},{3,4},{4,3},{5,6},{6,5},{7,8},{8,7},{9,10},{10,... | collective-permute-start | bytes 98312 | tf_op jit(solution)/shard_map/ppermute | solution.py:577

commit v11 on v10

--- a/solution.py
+++ b/solution.py
@@ -35,7 +35,8 @@
 def product(a, b):
     high = a.astype(BF16)
     low = (a - high.astype(F32)).astype(BF16)
-    return jnp.dot(high, b, preferred_element_type=F32) + jnp.dot(low, b, preferred_element_type=F32)
+    parts, twice = jnp.concatenate([high, low], axis=1), jnp.concatenate([b, b], axis=0)
+    return jnp.dot(parts, twice, preferred_element_type=F32)
 
 
 def harmonic(a, b):

time: 40.6 us -> 40.1 us (0.988)
  Pallas kernels: 9.65 us -> 9.14 us
where the time goes in v11:
time: 40.1 us; the launch traced here: 40 us
  starting transfers between devices  17.6 us (44%)
  blocking collectives  10.3 us (26%)
  Pallas kernels  9.14 us (23%)
  waiting for transfers between devices  2.26 us (6%)
  between operations  0.67 us (2%)
    ppermute x6, starting transfers between devices, swap(): return lax.ppermute(value, axis, list(enumerate(partner)))  17.6 us
    all_to_all x1, blocking collectives, shards(): column = lax.all_to_all(slots, 'cast', 0, 0)  10.3 us
    pallas_call x1, Pallas kernels, shards(): call(ascent_kernel, [VMEM] * (3 + len(state)), [(HZ, BC, BS)] * 2, scratc...  3.44 us
    ppermute x6, waiting for transfers between devices, swap(): return lax.ppermute(value, axis, list(enumerate(partner)))  2.26 us
    pallas_call x1, Pallas kernels, shards(): call(own_kernel, [VMEM] * 5, own_state + [(HZ, HALF, BS), (HZ, HALF - 8,...  1.98 us
    pallas_call x1, Pallas kernels, shards(): call(state_kernel, [VMEM] * 5, edge_state + level1_state, [(8, ROWS, BS)])  1.1 us
    pallas_call x1, Pallas kernels, shards(): call(stage_kernel, [HBM] * 3, [(2, HZ, BC, BS), (CAST_ROWS, BS), (CAST_RO...  1.03 us
    pallas_call x1, Pallas kernels, shards(): call(edge_kernel, [VMEM] * 6, [(count, 8, BS)], [(4, SENT, BS), (4, 16, B...  0.97 us
  transfers between devices with their start and end apart: 6, of which 2 were waited for; matrix products, arithmetic and copies ran while one was open for 0% of the time, Pallas kernels for 8%

profile of v11, /device:TPU:1, one launch (start us, length us, event | category | flops | bytes accessed | tf_op | source)
XLA Modules:
  0.0 40.0 jit_solution(16651136559260079176)
XLA Ops:
  0.6 1.0 %shard_map.50 = (f32[2,16,16,128]{3,2,1,0:T(8,128)S(1)}, f32[400,128]{1,0:T(8,128)S(1)}, f32[400,128]{1,0:T(8,128)S(1)}) custom-call(f32[3]{0:T(128)} %table_in.1, s32[16,16,128]{2,1,0:T(8,128)} %phase_in.1, f32[16,16,128]{2,1,0:T(8,128)} %source_in.1), custom_call_target="tpu_custom_call" | custom-call | tf_op jit(solution)/shard_map/pallas_call | solution.py:590
  1.7 2.7 %collective-permute-start = (f32[400,128]{1,0:T(8,128)S(1)}, f32[400,128]{1,0:T(8,128)S(1)}, u32[]{:S(2)}, u32[]{:S(2)}) collective-permute-start(f32[400,128]{1,0:T(8,128)S(1)} %get-tuple-element.46), channel_id=1, source_target_pairs={{0,224},{32,64},{64,32},{96,128},{128,96},{160,192},{192,160},{224... | collective-permute-start | bytes 614408 | tf_op jit(solution)/shard_map/ppermute | solution.py:578
  4.4 1.1 %collective-permute-start.1 = (f32[400,128]{1,0:T(8,128)S(1)}, f32[400,128]{1,0:T(8,128)S(1)}, u32[]{:S(2)}, u32[]{:S(2)}) collective-permute-start(f32[400,128]{1,0:T(8,128)S(1)} %get-tuple-element.47), channel_id=1, source_target_pairs={{0,32},{32,0},{64,96},{96,64},{128,160},{160,128},{192,224},{224,1... | collective-permute-start | bytes 614408 | tf_op jit(solution)/shard_map/ppermute | solution.py:578
  5.5 0.3 shard_map.51
  5.7 2.1 %collective-permute-done.far_cast = f32[400,128]{1,0:T(8,128)S(1)} collective-permute-done((f32[400,128]{1,0:T(8,128)S(1)}, f32[400,128]{1,0:T(8,128)S(1)}, u32[]{:S(2)}, u32[]{:S(2)}) %collective-permute-start) | collective-permute-done | bytes 204832 | tf_op jit(solution)/shard_map/ppermute | solution.py:578
  7.8 0.0 collective-permute-done.1.near_cast
  7.8 0.3 shard_map.52
  8.2 1.7 %collective-permute-start.2 = (f32[2,2,32,128]{3,2,1,0:T(8,128)S(1)}, f32[2,2,32,128]{3,2,1,0:T(8,128)S(1)}, u32[]{:S(2)}, u32[]{:S(2)}) collective-permute-start(f32[2,2,32,128]{3,2,1,0:T(8,128)S(1)} %get-tuple-element.48), channel_id=1, source_target_pairs={{0,1},{1,0},{2,3},{3,2},{4,5},{5,4},{6,7},{7,6},{8,9},{9,8},{10,11... | collective-permute-start | bytes 196616 | tf_op jit(solution)/shard_map/ppermute | solution.py:578
  9.8 7.2 %collective-permute-start.3 = (f32[2,2,32,128]{3,2,1,0:T(8,128)S(1)}, f32[2,2,32,128]{3,2,1,0:T(8,128)S(1)}, u32[]{:S(2)}, u32[]{:S(2)}) collective-permute-start(f32[2,2,32,128]{3,2,1,0:T(8,128)S(1)} %get-tuple-element.49), channel_id=1, source_target_pairs={{0,31},{1,2},{2,1},{3,4},{4,3},{5,6},{6,5},{7,8},{8,7},{9,10},{10,... | collective-permute-start | bytes 196616 | tf_op jit(solution)/shard_map/ppermute | solution.py:578
  17.0 2.0 %shard_map.53 = (f32[16,24,128]{2,1,0:T(8,128)S(1)}, f32[16,24,128]{2,1,0:T(8,128)S(1)}, f32[16,24,128]{2,1,0:T(8,128)S(1)}, f32[16,24,128]{2,1,0:T(8,128)S(1)},...) custom-call(f32[2,16,16,128]{3,2,1,0:T(8,128)S(1)} %get-tuple-elemen, ...), custom_call_target="tpu_custom_call" | custom-call | tf_op jit(solution)/shard_map/pallas_call | solution.py:604
  19.0 0.0 collective-permute-done.2.near_span
  19.0 0.0 collective-permute-done.3.far_span
  19.0 1.0 %shard_map.54 = f32[8,8,128]{2,1,0:T(8,128)S(1)} custom-call(f32[2,2,32,128]{3,2,1,0:T(8,128)S(1)} %collective-permute-done.2.near_span, f32[2,2,32,128]{3,2,1,0:T(8,128)S(1)} %collective-permute-done.3.far_span, f32[2,4,32,128]{3,2,1,0:T(8,128)S(1)} %get-tuple-element.52.inner, f32[16,16,128]{2,1,0:T(8,128)S(1)} %get-tuple-element.53.merged, ...), custom_call_target="tpu_custom_call" | custom-call | tf_op jit(solution)/shard_map/pallas_call | solution.py:610
  20.0 10.3 %all_to_all.5.own = f32[8,8,128]{2,1,0:T(8,128)S(1)} all-to-all(f32[8,8,128]{2,1,0:T(8,128)S(1)} %shard_map.54), channel_id=1, replica_groups=mesh['cast'=8,'span'=32] {'cast'}, dimensions={0} | all-to-all | bytes 65536 | tf_op jit(solution)/shard_map/all_to_all | solution.py:617
  30.3 0.0 collective-permute-start.5
  30.3 4.9 %collective-permute-start.4 = (f32[8,8,128]{2,1,0:T(8,128)S(1)}, f32[8,8,128]{2,1,0:T(8,128)S(1)}, u32[]{:S(2)}, u32[]{:S(2)}) collective-permute-start(f32[8,8,128]{2,1,0:T(8,128)S(1)} %all_to_all.5.own), channel_id=1, source_target_pairs={{0,31},{1,2},{2,1},{3,4},{4,3},{5,6},{6,5},{7,8},{8,7},{9,10},{10,... | collective-permute-start | bytes 98312 | tf_op jit(solution)/shard_map/ppermute | solution.py:578
  35.3 1.1 %shard_map.55 = (f32[8,24,128]{2,1,0:T(8,128)S(1)}, f32[8,24,128]{2,1,0:T(8,128)S(1)}, f32[8,24,128]{2,1,0:T(8,128)S(1)}, f32[8,24,128]{2,1,0:T(8,128)S(1)}, f32...) custom-call(f32[2,2,32,128]{3,2,1,0:T(8,128)S(1)} %collective-permut, ...), custom_call_target="tpu_custom_call" | custom-call | tf_op jit(solution)/shard_map/pallas_call | solution.py:613
  36.4 0.0 collective-permute-done.5.near_column
  36.4 0.2 collective-permute-done.4.far_column
  36.6 3.4 %shard_map.56 = (f32[16,16,128]{2,1,0:T(8,128)}, f32[16,16,128]{2,1,0:T(8,128)}) custom-call(f32[8,8,128]{2,1,0:T(8,128)S(1)} %all_to_all.5.own, f32[8,8,128]{2,1,0:T(8,128)S(1)} %collective-permute-done.4.far_column, f32[8,8,128]{2,1,0:T(8,128)S(1)} %collective-permute-done.5.near_column, bf16[128,128]{1,0:T(8,128)(2,1)S(1)} %get-tuple-element.56.narrow, ...), custom_call_target="tpu_custom_call" | custom-call | tf_op jit(solution)/shard_map/pallas_call | solution.py:634
Async XLA Ops:
  1.7 6.1 %collective-permute-start = (f32[400,128]{1,0:T(8,128)S(1)}, f32[400,128]{1,0:T(8,128)S(1)}, u32[]{:S(2)}, u32[]{:S(2)}) collective-permute-start(f32[400,128]{1,0:T(8,128)S(1)} %get-tuple-element.46), channel_id=1, source_target_pairs={{0,224},{32,64},{64,32},{96,128},{128,96},{160,192},{192,160},{224... | collective-permute-start | bytes 614408 | tf_op jit(solution)/shard_map/ppermute | solution.py:578
  4.4 3.4 %collective-permute-start.1 = (f32[400,128]{1,0:T(8,128)S(1)}, f32[400,128]{1,0:T(8,128)S(1)}, u32[]{:S(2)}, u32[]{:S(2)}) collective-permute-start(f32[400,128]{1,0:T(8,128)S(1)} %get-tuple-element.47), channel_id=1, source_target_pairs={{0,32},{32,0},{64,96},{96,64},{128,160},{160,128},{192,224},{224,1... | collective-permute-start | bytes 614408 | tf_op jit(solution)/shard_map/ppermute | solution.py:578
  8.2 10.9 %collective-permute-start.2 = (f32[2,2,32,128]{3,2,1,0:T(8,128)S(1)}, f32[2,2,32,128]{3,2,1,0:T(8,128)S(1)}, u32[]{:S(2)}, u32[]{:S(2)}) collective-permute-start(f32[2,2,32,128]{3,2,1,0:T(8,128)S(1)} %get-tuple-element.48), channel_id=1, source_target_pairs={{0,1},{1,0},{2,3},{3,2},{4,5},{5,4},{6,7},{7,6},{8,9},{9,8},{10,11... | collective-permute-start | bytes 196616 | tf_op jit(solution)/shard_map/ppermute | solution.py:578
  9.8 9.2 %collective-permute-start.3 = (f32[2,2,32,128]{3,2,1,0:T(8,128)S(1)}, f32[2,2,32,128]{3,2,1,0:T(8,128)S(1)}, u32[]{:S(2)}, u32[]{:S(2)}) collective-permute-start(f32[2,2,32,128]{3,2,1,0:T(8,128)S(1)} %get-tuple-element.49), channel_id=1, source_target_pairs={{0,31},{1,2},{2,1},{3,4},{4,3},{5,6},{6,5},{7,8},{8,7},{9,10},{10,... | collective-permute-start | bytes 196616 | tf_op jit(solution)/shard_map/ppermute | solution.py:578
  30.3 6.1 %collective-permute-start.5 = (f32[8,8,128]{2,1,0:T(8,128)S(1)}, f32[8,8,128]{2,1,0:T(8,128)S(1)}, u32[]{:S(2)}, u32[]{:S(2)}) collective-permute-start(f32[8,8,128]{2,1,0:T(8,128)S(1)} %all_to_all.5.own), channel_id=1, source_target_pairs={{0,1},{1,0},{2,3},{3,2},{4,5},{5,4},{6,7},{7,6},{8,9},{9,8},{10,11... | collective-permute-start | bytes 98312 | tf_op jit(solution)/shard_map/ppermute | solution.py:578
  30.3 6.2 %collective-permute-start.4 = (f32[8,8,128]{2,1,0:T(8,128)S(1)}, f32[8,8,128]{2,1,0:T(8,128)S(1)}, u32[]{:S(2)}, u32[]{:S(2)}) collective-permute-start(f32[8,8,128]{2,1,0:T(8,128)S(1)} %all_to_all.5.own), channel_id=1, source_target_pairs={{0,31},{1,2},{2,1},{3,4},{4,3},{5,6},{6,5},{7,8},{8,7},{9,10},{10,... | collective-permute-start | bytes 98312 | tf_op jit(solution)/shard_map/ppermute | solution.py:578

commit v12 on v11

--- a/solution.py
+++ b/solution.py
@@ -45,12 +45,9 @@
 
 def near(x, below, above, cast, span, low, high):
     return (
-        cast * shift(x, 1, 0)
-        + shift(cast * x, -1, 0)
-        + span * shift(x, 1, 1)
-        + shift(span * x, -1, 1)
-        + low * below
-        + high * above
+        (cast * shift(x, 1, 0) + shift(cast * x, -1, 0))
+        + (low * below + high * above)
+        + (span * shift(x, 1, 1) + shift(span * x, -1, 1))
     )
 
 

time: 40.1 us -> 40.1 us (level)
  no operation moved by 1% of the time
where the time goes in v12:
time: 40.1 us; the launch traced here: 40 us
  starting transfers between devices  17.6 us (44%)
  blocking collectives  10.3 us (26%)
  Pallas kernels  9.13 us (23%)
  waiting for transfers between devices  2.27 us (6%)
  between operations  0.67 us (2%)
    ppermute x6, starting transfers between devices, swap(): return lax.ppermute(value, axis, list(enumerate(partner)))  17.6 us
    all_to_all x1, blocking collectives, shards(): column = lax.all_to_all(slots, 'cast', 0, 0)  10.3 us
    pallas_call x1, Pallas kernels, shards(): call(ascent_kernel, [VMEM] * (3 + len(state)), [(HZ, BC, BS)] * 2, scratc...  3.43 us
    ppermute x6, waiting for transfers between devices, swap(): return lax.ppermute(value, axis, list(enumerate(partner)))  2.27 us
    pallas_call x1, Pallas kernels, shards(): call(own_kernel, [VMEM] * 5, own_state + [(HZ, HALF, BS), (HZ, HALF - 8,...  1.98 us
    pallas_call x1, Pallas kernels, shards(): call(state_kernel, [VMEM] * 5, edge_state + level1_state, [(8, ROWS, BS)])  1.1 us
    pallas_call x1, Pallas kernels, shards(): call(stage_kernel, [HBM] * 3, [(2, HZ, BC, BS), (CAST_ROWS, BS), (CAST_RO...  1.03 us
    pallas_call x1, Pallas kernels, shards(): call(edge_kernel, [VMEM] * 6, [(count, 8, BS)], [(4, SENT, BS), (4, 16, B...  0.97 us
  transfers between devices with their start and end apart: 6, of which 2 were waited for; matrix products, arithmetic and copies ran while one was open for 0% of the time, Pallas kernels for 8%

profile of v12, /device:TPU:1, one launch (start us, length us, event | category | flops | bytes accessed | tf_op | source)
XLA Modules:
  0.0 40.0 jit_solution(11150657182843050462)
XLA Ops:
  0.6 1.0 %shard_map.50 = (f32[2,16,16,128]{3,2,1,0:T(8,128)S(1)}, f32[400,128]{1,0:T(8,128)S(1)}, f32[400,128]{1,0:T(8,128)S(1)}) custom-call(f32[3]{0:T(128)} %table_in.1, s32[16,16,128]{2,1,0:T(8,128)} %phase_in.1, f32[16,16,128]{2,1,0:T(8,128)} %source_in.1), custom_call_target="tpu_custom_call" | custom-call | tf_op jit(solution)/shard_map/pallas_call | solution.py:587
  1.7 2.7 %collective-permute-start = (f32[400,128]{1,0:T(8,128)S(1)}, f32[400,128]{1,0:T(8,128)S(1)}, u32[]{:S(2)}, u32[]{:S(2)}) collective-permute-start(f32[400,128]{1,0:T(8,128)S(1)} %get-tuple-element.46), channel_id=1, source_target_pairs={{0,224},{32,64},{64,32},{96,128},{128,96},{160,192},{192,160},{224... | collective-permute-start | bytes 614408 | tf_op jit(solution)/shard_map/ppermute | solution.py:575
  4.4 1.1 %collective-permute-start.1 = (f32[400,128]{1,0:T(8,128)S(1)}, f32[400,128]{1,0:T(8,128)S(1)}, u32[]{:S(2)}, u32[]{:S(2)}) collective-permute-start(f32[400,128]{1,0:T(8,128)S(1)} %get-tuple-element.47), channel_id=1, source_target_pairs={{0,32},{32,0},{64,96},{96,64},{128,160},{160,128},{192,224},{224,1... | collective-permute-start | bytes 614408 | tf_op jit(solution)/shard_map/ppermute | solution.py:575
  5.5 0.3 shard_map.51
  5.7 2.1 %collective-permute-done.far_cast = f32[400,128]{1,0:T(8,128)S(1)} collective-permute-done((f32[400,128]{1,0:T(8,128)S(1)}, f32[400,128]{1,0:T(8,128)S(1)}, u32[]{:S(2)}, u32[]{:S(2)}) %collective-permute-start) | collective-permute-done | bytes 204832 | tf_op jit(solution)/shard_map/ppermute | solution.py:575
  7.8 0.0 collective-permute-done.1.near_cast
  7.8 0.3 shard_map.52
  8.2 1.7 %collective-permute-start.2 = (f32[2,2,32,128]{3,2,1,0:T(8,128)S(1)}, f32[2,2,32,128]{3,2,1,0:T(8,128)S(1)}, u32[]{:S(2)}, u32[]{:S(2)}) collective-permute-start(f32[2,2,32,128]{3,2,1,0:T(8,128)S(1)} %get-tuple-element.48), channel_id=1, source_target_pairs={{0,1},{1,0},{2,3},{3,2},{4,5},{5,4},{6,7},{7,6},{8,9},{9,8},{10,11... | collective-permute-start | bytes 196616 | tf_op jit(solution)/shard_map/ppermute | solution.py:575
  9.8 7.2 %collective-permute-start.3 = (f32[2,2,32,128]{3,2,1,0:T(8,128)S(1)}, f32[2,2,32,128]{3,2,1,0:T(8,128)S(1)}, u32[]{:S(2)}, u32[]{:S(2)}) collective-permute-start(f32[2,2,32,128]{3,2,1,0:T(8,128)S(1)} %get-tuple-element.49), channel_id=1, source_target_pairs={{0,31},{1,2},{2,1},{3,4},{4,3},{5,6},{6,5},{7,8},{8,7},{9,10},{10,... | collective-permute-start | bytes 196616 | tf_op jit(solution)/shard_map/ppermute | solution.py:575
  17.0 2.0 %shard_map.53 = (f32[16,24,128]{2,1,0:T(8,128)S(1)}, f32[16,24,128]{2,1,0:T(8,128)S(1)}, f32[16,24,128]{2,1,0:T(8,128)S(1)}, f32[16,24,128]{2,1,0:T(8,128)S(1)},...) custom-call(f32[2,16,16,128]{3,2,1,0:T(8,128)S(1)} %get-tuple-elemen, ...), custom_call_target="tpu_custom_call" | custom-call | tf_op jit(solution)/shard_map/pallas_call | solution.py:601
  19.0 0.0 collective-permute-done.2.near_span
  19.0 0.0 collective-permute-done.3.far_span
  19.0 1.0 %shard_map.54 = f32[8,8,128]{2,1,0:T(8,128)S(1)} custom-call(f32[2,2,32,128]{3,2,1,0:T(8,128)S(1)} %collective-permute-done.2.near_span, f32[2,2,32,128]{3,2,1,0:T(8,128)S(1)} %collective-permute-done.3.far_span, f32[2,4,32,128]{3,2,1,0:T(8,128)S(1)} %get-tuple-element.52.inner, f32[16,16,128]{2,1,0:T(8,128)S(1)} %get-tuple-element.53.merged, ...), custom_call_target="tpu_custom_call" | custom-call | tf_op jit(solution)/shard_map/pallas_call | solution.py:607
  20.0 10.3 %all_to_all.5.own = f32[8,8,128]{2,1,0:T(8,128)S(1)} all-to-all(f32[8,8,128]{2,1,0:T(8,128)S(1)} %shard_map.54), channel_id=1, replica_groups=mesh['cast'=8,'span'=32] {'cast'}, dimensions={0} | all-to-all | bytes 65536 | tf_op jit(solution)/shard_map/all_to_all | solution.py:614
  30.3 0.0 collective-permute-start.5
  30.3 4.9 %collective-permute-start.4 = (f32[8,8,128]{2,1,0:T(8,128)S(1)}, f32[8,8,128]{2,1,0:T(8,128)S(1)}, u32[]{:S(2)}, u32[]{:S(2)}) collective-permute-start(f32[8,8,128]{2,1,0:T(8,128)S(1)} %all_to_all.5.own), channel_id=1, source_target_pairs={{0,31},{1,2},{2,1},{3,4},{4,3},{5,6},{6,5},{7,8},{8,7},{9,10},{10,... | collective-permute-start | bytes 98312 | tf_op jit(solution)/shard_map/ppermute | solution.py:575
  35.3 1.1 %shard_map.55 = (f32[8,24,128]{2,1,0:T(8,128)S(1)}, f32[8,24,128]{2,1,0:T(8,128)S(1)}, f32[8,24,128]{2,1,0:T(8,128)S(1)}, f32[8,24,128]{2,1,0:T(8,128)S(1)}, f32...) custom-call(f32[2,2,32,128]{3,2,1,0:T(8,128)S(1)} %collective-permut, ...), custom_call_target="tpu_custom_call" | custom-call | tf_op jit(solution)/shard_map/pallas_call | solution.py:610
  36.4 0.0 collective-permute-done.5.near_column
  36.4 0.2 collective-permute-done.4.far_column
  36.6 3.4 %shard_map.56 = (f32[16,16,128]{2,1,0:T(8,128)}, f32[16,16,128]{2,1,0:T(8,128)}) custom-call(f32[8,8,128]{2,1,0:T(8,128)S(1)} %all_to_all.5.own, f32[8,8,128]{2,1,0:T(8,128)S(1)} %collective-permute-done.4.far_column, f32[8,8,128]{2,1,0:T(8,128)S(1)} %collective-permute-done.5.near_column, bf16[128,128]{1,0:T(8,128)(2,1)S(1)} %get-tuple-element.56.narrow, ...), custom_call_target="tpu_custom_call" | custom-call | tf_op jit(solution)/shard_map/pallas_call | solution.py:631
Async XLA Ops:
  1.7 6.1 %collective-permute-start = (f32[400,128]{1,0:T(8,128)S(1)}, f32[400,128]{1,0:T(8,128)S(1)}, u32[]{:S(2)}, u32[]{:S(2)}) collective-permute-start(f32[400,128]{1,0:T(8,128)S(1)} %get-tuple-element.46), channel_id=1, source_target_pairs={{0,224},{32,64},{64,32},{96,128},{128,96},{160,192},{192,160},{224... | collective-permute-start | bytes 614408 | tf_op jit(solution)/shard_map/ppermute | solution.py:575
  4.4 3.4 %collective-permute-start.1 = (f32[400,128]{1,0:T(8,128)S(1)}, f32[400,128]{1,0:T(8,128)S(1)}, u32[]{:S(2)}, u32[]{:S(2)}) collective-permute-start(f32[400,128]{1,0:T(8,128)S(1)} %get-tuple-element.47), channel_id=1, source_target_pairs={{0,32},{32,0},{64,96},{96,64},{128,160},{160,128},{192,224},{224,1... | collective-permute-start | bytes 614408 | tf_op jit(solution)/shard_map/ppermute | solution.py:575
  8.2 10.9 %collective-permute-start.2 = (f32[2,2,32,128]{3,2,1,0:T(8,128)S(1)}, f32[2,2,32,128]{3,2,1,0:T(8,128)S(1)}, u32[]{:S(2)}, u32[]{:S(2)}) collective-permute-start(f32[2,2,32,128]{3,2,1,0:T(8,128)S(1)} %get-tuple-element.48), channel_id=1, source_target_pairs={{0,1},{1,0},{2,3},{3,2},{4,5},{5,4},{6,7},{7,6},{8,9},{9,8},{10,11... | collective-permute-start | bytes 196616 | tf_op jit(solution)/shard_map/ppermute | solution.py:575
  9.8 9.2 %collective-permute-start.3 = (f32[2,2,32,128]{3,2,1,0:T(8,128)S(1)}, f32[2,2,32,128]{3,2,1,0:T(8,128)S(1)}, u32[]{:S(2)}, u32[]{:S(2)}) collective-permute-start(f32[2,2,32,128]{3,2,1,0:T(8,128)S(1)} %get-tuple-element.49), channel_id=1, source_target_pairs={{0,31},{1,2},{2,1},{3,4},{4,3},{5,6},{6,5},{7,8},{8,7},{9,10},{10,... | collective-permute-start | bytes 196616 | tf_op jit(solution)/shard_map/ppermute | solution.py:575
  30.3 6.0 %collective-permute-start.5 = (f32[8,8,128]{2,1,0:T(8,128)S(1)}, f32[8,8,128]{2,1,0:T(8,128)S(1)}, u32[]{:S(2)}, u32[]{:S(2)}) collective-permute-start(f32[8,8,128]{2,1,0:T(8,128)S(1)} %all_to_all.5.own), channel_id=1, source_target_pairs={{0,1},{1,0},{2,3},{3,2},{4,5},{5,4},{6,7},{7,6},{8,9},{9,8},{10,11... | collective-permute-start | bytes 98312 | tf_op jit(solution)/shard_map/ppermute | solution.py:575
  30.3 6.2 %collective-permute-start.4 = (f32[8,8,128]{2,1,0:T(8,128)S(1)}, f32[8,8,128]{2,1,0:T(8,128)S(1)}, u32[]{:S(2)}, u32[]{:S(2)}) collective-permute-start(f32[8,8,128]{2,1,0:T(8,128)S(1)} %all_to_all.5.own), channel_id=1, source_target_pairs={{0,31},{1,2},{2,1},{3,4},{4,3},{5,6},{6,5},{7,8},{8,7},{9,10},{10,... | collective-permute-start | bytes 98312 | tf_op jit(solution)/shard_map/ppermute | solution.py:575
